TPU v7x, 32 devices: a whole 2x2x4 slice. The times are simulated.
32 devices in a mesh: gx: 2 (over core), gy: 4 (over z), gz: 4 (over y, x).
Axes of the slice: x: 2, y: 2, z: 4, core: 2. Of those that a mesh axis runs over, the one named last changes fastest.
Arguments:
- density_volume: float32 [64, 512, 512], P('gz', 'gy', 'gx'), may hold values from -4 to 4
Outputs:
- colour: float32 [3, 512, 512], P(None, ('gy', 'gz'), 'gx')
- depth_map: float32 [512, 512], P(('gy', 'gz'), 'gx')
- transparency: float32 [512, 512], P(('gy', 'gz'), 'gx')
All inputs are finite; a program needn't handle non-finite values.
Results may differ from a plain program's by a relative error of at most 0.0003.
Values sent between devices are 32-bit elements; how exact they have to be, the bound alone decides.
No kernel may reach another device: no remote copies, remote signals or barrier semaphores. Data moves between devices by JAX's collectives and lax.ppermute only.
A program may use at most 128 MiB of HBM per device.

v0:
```python
import jax
import jax.numpy as jnp
from jax import lax
from jax.sharding import PartitionSpec as P


def with_halo(shard, sides, width):
    for axis, dim in sides:
        peers, length = (lax.axis_size(axis), shard.shape[dim])
        up = [(i, (i + 1) % peers) for i in range(peers - 1)]
        down = [(j, i) for i, j in up]
        last = lax.slice_in_dim(shard, length - width, length, axis=dim)
        initial = lax.slice_in_dim(shard, 0, width, axis=dim)
        before = lax.ppermute(last, axis, up)
        after = lax.ppermute(initial, axis, down)
        shard = jnp.concatenate([before, shard, after], axis=dim)
    return shard


def fourth(far_low, near_low, near_high, far_high):
    return (far_low - 8.0 * near_low + 8.0 * near_high - far_high) / 12.0


def shade(sample, grad_z, grad_y, grad_x):
    square = grad_z * grad_z + grad_y * grad_y + grad_x * grad_x
    facing = (0.64 * grad_z + 0.6 * grad_y + 0.48 * grad_x) * lax.rsqrt(square + 1.0)
    diffuse = 0.3 + 0.7 * jnp.maximum(facing, 0.0)
    edge_gain = 1.0 + square / (square + 1.0)
    density = jax.nn.softplus(sample) * edge_gain
    colour_red = jax.nn.sigmoid(2.0 * sample) * diffuse
    colour_green = jnp.exp(-0.5 * sample * sample) * diffuse
    colour_blue = jax.nn.sigmoid(-2.0 * sample) * diffuse
    return (density, colour_red, colour_green, colour_blue)


def blend_depth(received):
    through = received[4]
    running = jnp.cumprod(through, axis=0)
    front_pass = jnp.concatenate([jnp.ones_like(running[:1]), running[:-1]], axis=0)
    shaded = jnp.sum(front_pass[None] * received[:4], axis=1)
    return jnp.concatenate([shaded, running[-1:]], axis=0)


def on_device(density_volume):
    cells_z, cells_y, cells_x = density_volume.shape
    depth_count = lax.axis_size("gz")
    depth_index = lax.axis_index("gz")
    total_z = cells_z * depth_count
    depth_step = 2.0 / total_z
    padded = with_halo(density_volume, (("gx", 2), ("gy", 1), ("gz", 0)), 2)
    centre = padded[2:-2, 2:-2, 2:-2]
    grad_z = fourth(
        padded[0:-4, 2:-2, 2:-2],
        padded[1:-3, 2:-2, 2:-2],
        padded[3:-1, 2:-2, 2:-2],
        padded[4:, 2:-2, 2:-2],
    )
    grad_y = fourth(
        padded[2:-2, 0:-4, 2:-2],
        padded[2:-2, 1:-3, 2:-2],
        padded[2:-2, 3:-1, 2:-2],
        padded[2:-2, 4:, 2:-2],
    )
    grad_x = fourth(
        padded[2:-2, 2:-2, 0:-4],
        padded[2:-2, 2:-2, 1:-3],
        padded[2:-2, 2:-2, 3:-1],
        padded[2:-2, 2:-2, 4:],
    )
    density, colour_red, colour_green, colour_blue = shade(centre, grad_z, grad_y, grad_x)
    pixels = cells_y * cells_x
    optical = (density * depth_step).reshape(cells_z, pixels)
    row_iota = lax.broadcasted_iota(jnp.int32, (cells_z, cells_z), 0)
    col_iota = lax.broadcasted_iota(jnp.int32, (cells_z, cells_z), 1)
    lower_tri = (row_iota >= col_iota).astype(jnp.float32)
    inclusive = jnp.dot(
        lower_tri, optical, precision=lax.Precision.HIGHEST, preferred_element_type=jnp.float32
    )
    weight = jnp.exp(-(inclusive - optical)) * (1.0 - jnp.exp(-optical))
    depth_pos = (
        (depth_index * cells_z + jnp.arange(cells_z, dtype=jnp.int32)).astype(jnp.float32) + 0.5
    ) / total_z
    partial_value = jnp.stack(
        [
            jnp.sum(weight * colour_red.reshape(cells_z, pixels), axis=0),
            jnp.sum(weight * colour_green.reshape(cells_z, pixels), axis=0),
            jnp.sum(weight * colour_blue.reshape(cells_z, pixels), axis=0),
            jnp.sum(weight * depth_pos[:, None], axis=0),
            jnp.exp(-inclusive[-1]),
        ]
    ).reshape(5, cells_y, cells_x)
    piece_rows = cells_y // depth_count
    stacked = partial_value.reshape(5, depth_count, piece_rows, cells_x)
    final_image = blend_depth(
        lax.all_to_all(stacked, "gz", split_axis=1, concat_axis=1, tiled=True)
    )
    return (final_image[:3], final_image[3], final_image[4])


def solution(mesh):
    return jax.shard_map(
        on_device,
        mesh=mesh,
        in_specs=(P("gz", "gy", "gx"),),
        out_specs=(P(None, ("gy", "gz"), "gx"), P(("gy", "gz"), "gx"), P(("gy", "gz"), "gx")),
        check_vma=False,
    )
```

profile of v0, /device:TPU:0, one launch (start us, length us, event | category | flops | bytes accessed | tf_op | source)
XLA Modules:
  0.0 101.9 jit_solution(17254441752755021613)
XLA Ops:
  0.6 2.9 %fusion.27 = (f32[16,128,2]{2,1,0:T(8,128)}, f32[16,128,2]{2,1,0:T(8,128)S(1)}) fusion(f32[16,128,256]{2,1,0:T(8,128)} %param.1), kind=kLoop, calls=%fused_computation.73 | loop fusion | bytes 65536 | tf_op jit(solution)/shard_map/slice | solution.py:12
  3.5 1.7 %copy.11 = f32[16,128,2]{1,0,2:T(8,128)S(1)} copy(f32[16,128,2]{2,1,0:T(8,128)} %get-tuple-element.23) | data formatting | bytes 32768
  5.2 2.4 %collective-permute-start = (f32[16,128,2]{1,0,2:T(8,128)S(1)}, f32[16,128,2]{1,0,2:T(8,128)S(1)}, u32[]{:S(2)}, u32[]{:S(2)}) collective-permute-start(f32[16,128,2]{1,0,2:T(8,128)S(1)} %copy.11), channel_id=1, source_target_pairs={{0,16},{1,17},{2,18},{3,19},{4,20},{5,21},{6,22},{7,23},{8,24},{9,... | collective-permute-start | bytes 49160 | tf_op jit(solution)/shard_map/ppermute | solution.py:14
  7.9 1.3 %collective-permute-start.1 = (f32[16,128,2]{1,0,2:T(8,128)S(1)}, f32[16,128,2]{1,0,2:T(8,128)S(1)}, u32[]{:S(2)}, u32[]{:S(2)}) collective-permute-start(f32[16,128,2]{1,0,2:T(8,128)S(1)} %copy.12), channel_id=1, source_target_pairs={{16,0},{17,1},{18,2},{19,3},{20,4},{21,5},{22,6},{23,7},{24,8},{25... | collective-permute-start | bytes 49160 | tf_op jit(solution)/shard_map/ppermute | solution.py:15
  9.6 1.4 %collective-permute-done.1 = f32[16,128,2]{1,0,2:T(8,128)S(1)} collective-permute-done((f32[16,128,2]{1,0,2:T(8,128)S(1)}, f32[16,128,2]{1,0,2:T(8,128)S(1)}, u32[]{:S(2)}, u32[]{:S(2)}) %collective-permute-start.1) | collective-permute-done | bytes 16416 | tf_op jit(solution)/shard_map/ppermute | solution.py:15
  11.0 1.4 %copy.7 = f32[16,128,2]{2,1,0:T(8,128)} copy(f32[16,128,2]{1,0,2:T(8,128)S(1)} %collective-permute-done.1) | data formatting | bytes 32768 | tf_op jit(solution)/shard_map/ppermute | solution.py:15
  13.6 4.3 %collective-permute-start.2 = (f32[16,2,260]{2,1,0:T(2,128)S(1)}, f32[16,2,260]{2,1,0:T(2,128)S(1)}, u32[]{:S(2)}, u32[]{:S(2)}) collective-permute-start(f32[16,2,260]{2,1,0:T(2,128)S(1)} %get-tuple-element.20), channel_id=1, source_target_pairs={{0,4},{4,8},{8,12},{1,5},{5,9},{9,13},{2,6},{6,10},{10,14},{3,7},{... | collective-permute-start | bytes 99848 | tf_op jit(solution)/shard_map/ppermute | solution.py:14
  17.9 1.3 %collective-permute-start.3 = (f32[16,2,260]{2,1,0:T(2,128)S(1)}, f32[16,2,260]{2,1,0:T(2,128)S(1)}, u32[]{:S(2)}, u32[]{:S(2)}) collective-permute-start(f32[16,2,260]{2,1,0:T(2,128)S(1)} %get-tuple-element.21), channel_id=1, source_target_pairs={{4,0},{8,4},{12,8},{5,1},{9,5},{13,9},{6,2},{10,6},{14,10},{7,3},{... | collective-permute-start | bytes 99848 | tf_op jit(solution)/shard_map/ppermute | solution.py:15
  19.7 4.3 %collective-permute-done.3 = f32[16,2,260]{2,1,0:T(2,128)S(1)} collective-permute-done((f32[16,2,260]{2,1,0:T(2,128)S(1)}, f32[16,2,260]{2,1,0:T(2,128)S(1)}, u32[]{:S(2)}, u32[]{:S(2)}) %collective-permute-start.3) | collective-permute-done | bytes 33312 | tf_op jit(solution)/shard_map/ppermute | solution.py:15
  24.3 3.4 %collective-permute-start.4 = (f32[2,132,260]{2,1,0:T(8,128)S(1)}, f32[2,132,260]{2,1,0:T(8,128)S(1)}, u32[]{:S(2)}, u32[]{:S(2)}) collective-permute-start(f32[2,132,260]{2,1,0:T(8,128)S(1)} %get-tuple-element.14), channel_id=1, source_target_pairs={{0,1},{1,2},{2,3},{4,5},{5,6},{6,7},{8,9},{9,10},{10,11},{12,13},{... | collective-permute-start | bytes 823688 | tf_op jit(solution)/shard_map/ppermute | solution.py:14
  27.7 1.3 %collective-permute-start.5 = (f32[2,132,260]{2,1,0:T(8,128)S(1)}, f32[2,132,260]{2,1,0:T(8,128)S(1)}, u32[]{:S(2)}, u32[]{:S(2)}) collective-permute-start(f32[2,132,260]{2,1,0:T(8,128)S(1)} %get-tuple-element.15), channel_id=1, source_target_pairs={{1,0},{2,1},{3,2},{5,4},{6,5},{7,6},{9,8},{10,9},{11,10},{13,12},{... | collective-permute-start | bytes 823688 | tf_op jit(solution)/shard_map/ppermute | solution.py:15
  29.0 4.8 %maximum_maximum_fusion.1 = (f32[16,130,260]{2,1,0:T(8,128)}, f32[16,130,260]{2,1,0:T(8,128)}) fusion(f32[16,128,2]{2,1,0:T(8,128)S(1)} %copy-done.1, f32[16,128,256]{2,1,0:T(8,128)S(1)} %copy-done, f32[16,128,2]{2,1,0:T(8,128)S(1)} %copy.6, f32[16,2,260]{2,1,0:T(2,128)S(1)} %collective-permute-done.2, f32[16,2,260]{2,1,0:T(2,128)S(1)} %collective-permute-done.3), kind=kLoop, calls=%fused_computation.3 | loop fusion | flops 3244800 | bytes 6522880 | tf_op jit(solution)/shard_map/concatenate | solution.py:16
  33.8 1.7 %collective-permute-done.4 = f32[2,132,260]{2,1,0:T(8,128)S(1)} collective-permute-done((f32[2,132,260]{2,1,0:T(8,128)S(1)}, f32[2,132,260]{2,1,0:T(8,128)S(1)}, u32[]{:S(2)}, u32[]{:S(2)}) %collective-permute-start.4) | collective-permute-done | bytes 274592 | tf_op jit(solution)/shard_map/ppermute | solution.py:14
  35.5 10.9 %collective-permute-done.5 = f32[2,132,260]{2,1,0:T(8,128)S(1)} collective-permute-done((f32[2,132,260]{2,1,0:T(8,128)S(1)}, f32[2,132,260]{2,1,0:T(8,128)S(1)}, u32[]{:S(2)}, u32[]{:S(2)}) %collective-permute-start.5) | collective-permute-done | bytes 274592 | tf_op jit(solution)/shard_map/ppermute | solution.py:15
  46.4 6.6 %maximum_maximum_fusion = (f32[18,132,260]{2,1,0:T(8,128)}, f32[18,132,260]{2,1,0:T(8,128)}) fusion(f32[16,2,260]{2,1,0:T(2,128)S(1)} %collective-permute-done.3, f32[16,128,2]{2,1,0:T(8,128)S(1)} %copy-done.1, f32[16,128,256]{2,1,0:T(8,128)S(1)} %copy-done, f32[16,128,2]{2,1,0:T(8,128)S(1)} %copy.6, f32[16,2,260]{2,1,0:T(2,128)S(1)} %collective-permute-done.2, ...), kind=kLoop, calls=%fused_computation.1 | loop fusion | flops 6177600 | bytes 7687680 | tf_op jit(solution)/shard_map/concatenate | solution.py:16
  53.0 20.0 %divide_multiply_fusion.1 = (f32[16,128,256]{2,1,0:T(8,128)}, f32[16,128,256]{2,1,0:T(8,128)}, f32[16,128,256]{2,1,0:T(8,128)}, f32[16,128,256]{2,1,0:T(8,128)}, f32[16,128,256]{2,1,0:T(8,128)}) fusion(f32[16,128,256]{2,1,0:T(8,128)S(1)} %copy-done, f32[18,132,260]{2,1,0:T(8,128)} %get-tuple-element.13, f32[18,132,260]{2,1,0:T(8,128)} %get-tuple-element.12, ...), kind=kLoop, calls=%fused_computation.45 | loop fusion | flops 22020096 | bytes 29392896 | tf_op jit(solution)/shard_map/mul | solution.py:30
  73.0 5.2 %fusion.8 = (f32[16,128,256]{2,1,0:T(8,128)S(1)}, f32[16,128,256]{2,1,0:T(8,128)S(1)}, f32[16,128,256]{2,1,0:T(8,128)S(1)}) fusion(f32[16,128,256]{2,1,0:T(8,128)} %get-tuple-element.8, f32[16,128,256]{2,1,0:T(8,128)S(1)} %copy-done, f32[16,128,256]{2,1,0:T(8,128)} %get-tuple-element.11, f32[16,128,256]{2,1,0:T(8,128)} %get-tuple-element.10, ...), kind=kLoop, calls=%fused_computation.20 | loop fusion | flops 14155776 | bytes 16777216 | tf_op jit(solution)/shard_map/mul | solution.py:31
  78.2 1.2 %copy.16 = f32[2,8,128,256]{3,1,2,0:T(8,128)S(1)} copy(f32[2,8,128,256]{3,2,1,0:T(8,128)S(1)} %bitcast.24) | data formatting | bytes 4194304
  79.4 1.2 %copy.13 = f32[2,8,128,256]{3,1,2,0:T(8,128)S(1)} copy(f32[2,8,128,256]{3,2,1,0:T(8,128)S(1)} %bitcast.23) | data formatting | bytes 4194304
  80.6 1.2 %copy.15 = f32[2,8,128,256]{3,1,2,0:T(8,128)S(1)} copy(f32[2,8,128,256]{3,2,1,0:T(8,128)S(1)} %bitcast.22) | data formatting | bytes 4194304
  82.2 1.2 %copy.14 = f32[2,8,128,256]{3,1,2,0:T(8,128)S(1)} copy(f32[2,8,128,256]{3,2,1,0:T(8,128)S(1)} %bitcast.25) | data formatting | bytes 4194304
  83.4 4.5 %multiply_reduce_fusion = (f32[32768]{0:T(1024)S(1)}, f32[32768]{0:T(1024)S(1)}, f32[32768]{0:T(1024)S(1)}, f32[32768]{0:T(1024)S(1)}, f32[16,32768]{1,0:T(8,128)}) fusion(f32[16]{0:T(128)S(1)} %add_multiply_fusion, f32[16,32768]{1,0:T(8,128)S(1)} %bitcast.18, f32[16,32768]{1,0:T(8,128)S(1)} %bitcast.20, f32[16,32768]{1,0:T(8,128)S(1)} %bitcast.21, ...), kind=kOutput, calls=%fused_computation.40 | convolution fusion | flops 107348224 | bytes 11010112 | tf_op jit(solution)/shard_map/dot_general | solution.py:76
  88.1 1.7 %fusion.23 = f32[32768]{0:T(1024)S(1)} fusion(f32[16,32768]{1,0:T(8,128)} %get-tuple-element.27), kind=kLoop, calls=%fused_computation.59 | loop fusion | flops 32768 | bytes 262144 | tf_op jit(solution)/shard_map/exp | solution.py:89
  89.9 10.6 %all_to_all.5 = f32[5,4,32,256]{3,2,0,1:T(8,128)S(1)} all-to-all(f32[5,4,32,256]{3,2,0,1:T(8,128)S(1)} %bitcast_dynamic-update-slice_fusion), channel_id=1, replica_groups=mesh['gx'=2,'gy'=4,'gz'=4] {'gz'}, dimensions={1} | all-to-all | bytes 1310720 | tf_op jit(solution)/shard_map/all_to_all | solution.py:95
  (29 shorter events, 4.6 us)
Async XLA Ops:
  3.5 8.9 %copy-start = (f32[16,128,256]{2,1,0:T(8,128)S(1)}, f32[16,128,256]{2,1,0:T(8,128)}, u32[]{:S(2)}) copy-start(f32[16,128,256]{2,1,0:T(8,128)} %param.1) | copy-start | bytes 6291460
  5.2 4.0 %collective-permute-start = (f32[16,128,2]{1,0,2:T(8,128)S(1)}, f32[16,128,2]{1,0,2:T(8,128)S(1)}, u32[]{:S(2)}, u32[]{:S(2)}) collective-permute-start(f32[16,128,2]{1,0,2:T(8,128)S(1)} %copy.11), channel_id=1, source_target_pairs={{0,16},{1,17},{2,18},{3,19},{4,20},{5,21},{6,22},{7,23},{8,24},{9,... | collective-permute-start | bytes 49160 | tf_op jit(solution)/shard_map/ppermute | solution.py:14
  7.9 3.1 %collective-permute-start.1 = (f32[16,128,2]{1,0,2:T(8,128)S(1)}, f32[16,128,2]{1,0,2:T(8,128)S(1)}, u32[]{:S(2)}, u32[]{:S(2)}) collective-permute-start(f32[16,128,2]{1,0,2:T(8,128)S(1)} %copy.12), channel_id=1, source_target_pairs={{16,0},{17,1},{18,2},{19,3},{20,4},{21,5},{22,6},{23,7},{24,8},{25... | collective-permute-start | bytes 49160 | tf_op jit(solution)/shard_map/ppermute | solution.py:15
  12.5 11.5 %copy-start.1 = (f32[16,128,2]{2,1,0:T(8,128)S(1)}, f32[16,128,2]{2,1,0:T(8,128)}, u32[]{:S(2)}) copy-start(f32[16,128,2]{2,1,0:T(8,128)} %copy.7) | copy-start | bytes 49156
  13.6 6.1 %collective-permute-start.2 = (f32[16,2,260]{2,1,0:T(2,128)S(1)}, f32[16,2,260]{2,1,0:T(2,128)S(1)}, u32[]{:S(2)}, u32[]{:S(2)}) collective-permute-start(f32[16,2,260]{2,1,0:T(2,128)S(1)} %get-tuple-element.20), channel_id=1, source_target_pairs={{0,4},{4,8},{8,12},{1,5},{5,9},{9,13},{2,6},{6,10},{10,14},{3,7},{... | collective-permute-start | bytes 99848 | tf_op jit(solution)/shard_map/ppermute | solution.py:14
  17.9 6.0 %collective-permute-start.3 = (f32[16,2,260]{2,1,0:T(2,128)S(1)}, f32[16,2,260]{2,1,0:T(2,128)S(1)}, u32[]{:S(2)}, u32[]{:S(2)}) collective-permute-start(f32[16,2,260]{2,1,0:T(2,128)S(1)} %get-tuple-element.21), channel_id=1, source_target_pairs={{4,0},{8,4},{12,8},{5,1},{9,5},{13,9},{6,2},{10,6},{14,10},{7,3},{... | collective-permute-start | bytes 99848 | tf_op jit(solution)/shard_map/ppermute | solution.py:15
  24.3 11.2 %collective-permute-start.4 = (f32[2,132,260]{2,1,0:T(8,128)S(1)}, f32[2,132,260]{2,1,0:T(8,128)S(1)}, u32[]{:S(2)}, u32[]{:S(2)}) collective-permute-start(f32[2,132,260]{2,1,0:T(8,128)S(1)} %get-tuple-element.14), channel_id=1, source_target_pairs={{0,1},{1,2},{2,3},{4,5},{5,6},{6,7},{8,9},{9,10},{10,11},{12,13},{... | collective-permute-start | bytes 823688 | tf_op jit(solution)/shard_map/ppermute | solution.py:14
  27.7 18.7 %collective-permute-start.5 = (f32[2,132,260]{2,1,0:T(8,128)S(1)}, f32[2,132,260]{2,1,0:T(8,128)S(1)}, u32[]{:S(2)}, u32[]{:S(2)}) collective-permute-start(f32[2,132,260]{2,1,0:T(8,128)S(1)} %get-tuple-element.15), channel_id=1, source_target_pairs={{1,0},{2,1},{3,2},{5,4},{6,5},{7,6},{9,8},{10,9},{11,10},{13,12},{... | collective-permute-start | bytes 823688 | tf_op jit(solution)/shard_map/ppermute | solution.py:15
  80.6 1.6 %copy-start.2 = (f32[16,128,256]{2,1,0:T(8,128)S(1)}, f32[16,128,256]{2,1,0:T(8,128)}, u32[]{:S(2)}) copy-start(f32[16,128,256]{2,1,0:T(8,128)} %get-tuple-element.7) | copy-start | bytes 6291460
where the time goes:
time: 102 us
  other arithmetic  39.8 us (39%)
  waiting for transfers between devices  18.6 us (18%)
  starting transfers between devices  14 us (14%)
  local copies, waits for them, and re-layouts  13.5 us (13%)
  blocking collectives  10.6 us (10%)
  matrix products  4.45 us (4%)
    mul x1, other arithmetic, shade(): colour_red = jax.nn.sigmoid(2.0 * sample) * diffuse  20 us
    ppermute x3, waiting for transfers between devices, with_halo(): after = lax.ppermute(initial, axis, down)  16.5 us
    concatenate x2, other arithmetic, with_halo(): shard = jnp.concatenate([before, shard, after], axis=dim)  11.4 us
    all_to_all x1, blocking collectives, on_device(): lax.all_to_all(stacked, 'gz', split_axis=1, concat_axis=1, tiled=True)  10.6 us
    ppermute x3, starting transfers between devices, with_halo(): before = lax.ppermute(last, axis, up)  10.1 us
    unnamed x16, local copies, waits for them, and re-layouts  7.32 us
    mul x1, other arithmetic, shade(): colour_green = jnp.exp(-0.5 * sample * sample) * diffuse  5.18 us
    dot_general x1, matrix products, on_device(): jnp.dot(lower_tri, optical, precision=lax.Precision.HIGHEST, preferred_el...  4.45 us
  transfers between devices with their start and end apart: 6, of which 5 were waited for; matrix products, arithmetic and copies ran while one was open for 5% of the time, Pallas kernels for 0%

commit v1 on v0

v1 whole, which is shorter than its diff:
```python
import functools

import jax
import jax.numpy as jnp
from jax import lax
from jax.experimental import pallas as pl
from jax.experimental.pallas import tpu as pltpu
from jax.sharding import PartitionSpec as P

EDGE = 8


def band(offset):
    one = jnp.where(offset == 1, 8.0, jnp.where(offset == -1, -8.0, 0.0))
    two = jnp.where(offset == 2, -1.0, jnp.where(offset == -2, 1.0, 0.0))
    return (one + two).astype(jnp.bfloat16)


def split(value):
    high = value.astype(jnp.bfloat16)
    return high, (value - high.astype(jnp.float32)).astype(jnp.bfloat16)


def dot(a, b):
    return jnp.dot(a, b, preferred_element_type=jnp.float32)


def emit(sample, base, lin, grad_z, depth_step, through, position):
    root = lax.rsqrt(base + grad_z * grad_z * (1.0 / 144.0))
    diffuse = 0.3 + jnp.maximum((lin + grad_z * (0.64 * 0.7 / 12.0)) * root, 0.0)
    grown = jnp.exp(sample)
    optical = jnp.log(1.0 + grown) * ((2.0 - root * root) * depth_step)
    behind = through * jnp.exp(-optical)
    weight = through - behind
    lit = weight * diffuse
    square = grown * grown
    blue = lit / (1.0 + square)
    return behind, (blue * square, lit * jnp.exp(-0.5 * sample * sample), blue, weight * position)


def inner_kernel(ids, x_ref, ya_ref, yb_ref, e_ref, image_ref, part_ref, gx_ref, gy_ref, *, total_z, last_y):
    cells_z, rows, cols = x_ref.shape
    strip = e_ref.shape[2]
    depth_step = 2.0 / total_z
    at_x, at_y, at_z = ids[0], ids[1], ids[2]
    even = at_y % 2 == 0
    iota = functools.partial(lax.broadcasted_iota, jnp.int32)
    along_x = band(iota((cols, cols), 0) - iota((cols, cols), 1))
    lane = iota((strip, cols), 0) - iota((strip, cols), 1)
    beyond_x = jnp.where(at_x == 0, band(lane + cols), band(lane - strip))
    along_y = band(iota((rows, rows), 1) - iota((rows, rows), 0))
    out_row, slot = iota((rows, 2 * EDGE), 0), iota((rows, 2 * EDGE), 1)
    below = (slot < EDGE) == even
    cell = slot % EDGE
    beyond_y = band(jnp.where(below, rows + cell, cell - EDGE) - out_row)
    there = jnp.where(below, (at_y < last_y).astype(jnp.int32), (at_y > 0).astype(jnp.int32))
    beyond_y = jnp.where(there > 0, beyond_y, jnp.zeros_like(beyond_y))

    def gradients(k):
        high, low = split(x_ref[k])
        edge_high, edge_low = split(e_ref[k])
        gx_ref[...] = (
            dot(high, along_x) + dot(low, along_x)
            + dot(edge_high, beyond_x) + dot(edge_low, beyond_x)
        )
        rim_high, rim_low = split(jnp.concatenate([ya_ref[k], yb_ref[k]], axis=0))
        gy_ref[...] = (
            dot(along_y, high) + dot(along_y, low)
            + dot(beyond_y, rim_high) + dot(beyond_y, rim_low)
        )

    def pair(at):
        grad_x, grad_y = gx_ref[at], gy_ref[at]
        base = 1.0 + (grad_x * grad_x + grad_y * grad_y) * (1.0 / 144.0)
        lin = grad_x * (0.48 * 0.7 / 12.0) + grad_y * (0.6 * 0.7 / 12.0)
        return base, lin

    chunk = 16
    spans = [pl.ds(r, chunk) for r in range(0, rows, chunk)]
    for index, k in enumerate((0, 1, cells_z - 2, cells_z - 1)):
        gradients(k)
        for at in spans:
            base, lin = pair(at)
            part_ref[index, 0, at] = base
            part_ref[index, 1, at] = lin

    for channel in range(4):
        image_ref[channel] = jnp.zeros((rows, cols), jnp.float32)
    image_ref[4] = jnp.ones((rows, cols), jnp.float32)

    @pl.loop(2, cells_z - 2)
    def _(k):
        gradients(k)
        position = ((at_z * cells_z + k).astype(jnp.float32) + 0.5) / total_z
        for at in spans:
            base, lin = pair(at)
            grad_z = (x_ref[k - 2, at] - x_ref[k + 2, at]) + 8.0 * (x_ref[k + 1, at] - x_ref[k - 1, at])
            through, adds = emit(x_ref[k, at], base, lin, grad_z, depth_step, image_ref[4, at], position)
            image_ref[4, at] = through
            for channel, value in enumerate(adds):
                image_ref[channel, at] += value


def outer_kernel(ids, blocks, front_ref, back_ref, za_ref, zb_ref, image_ref, part_ref, *out_refs, total_z, cells_z):
    depth_step = 2.0 / total_z
    at_z = ids[2]
    last_z = total_z // cells_z - 1
    even = at_z % 2 == 0
    none = jnp.zeros(za_ref.shape[1:], jnp.float32)

    def before(layer):
        value = jnp.where(even, zb_ref[layer], za_ref[layer])
        return jnp.where(at_z > 0, value, none)

    def after(layer):
        value = jnp.where(even, za_ref[layer], zb_ref[layer])
        return jnp.where(at_z < last_z, value, none)

    f = front_ref
    b = back_ref
    ahead, next_ahead = before(0), before(1)
    behind, next_behind = after(0), after(1)
    cells = (
        (0, 0, f[0], (ahead - f[2]) + 8.0 * (f[1] - next_ahead)),
        (1, 1, f[1], (next_ahead - f[3]) + 8.0 * (f[2] - f[0])),
        (2, cells_z - 2, b[2], (b[0] - behind) + 8.0 * (b[3] - b[1])),
        (3, cells_z - 1, b[3], (b[1] - next_behind) + 8.0 * (behind - b[2])),
    )
    through = jnp.ones_like(none)
    sums = [jnp.zeros_like(none)] * 4
    for index, k, sample, grad_z in cells:
        if index == 2:
            sums = [s + through * image_ref[c] for c, s in enumerate(sums)]
            through = through * image_ref[4]
        position = ((at_z * cells_z + k).astype(jnp.float32) + 0.5) / total_z
        through, adds = emit(
            sample, part_ref[index, 0], part_ref[index, 1], grad_z, depth_step, through, position
        )
        sums = [s + a for s, a in zip(sums, adds)]
    image = sums + [through]
    for step, out_ref in enumerate(out_refs):

        @pl.when(pl.program_id(0) == step)
        def _():
            for channel, value in enumerate(image):
                out_ref[channel] = value


def join(front, back):
    through = front[4]
    return [front[c] + through * back[c] for c in range(4)] + [through * back[4]]


def put(image, colour_ref, depth_ref, clear_ref):
    for channel in range(3):
        colour_ref[channel] = image[channel]
    depth_ref[...] = image[3]
    clear_ref[...] = image[4]


def blend_four(ids, own_ref, one_ref, two_ref, three_ref, colour_ref, depth_ref, clear_ref):
    at_z = ids[2]
    odd, high = at_z % 2 == 1, at_z >= 2
    own, one, two, three = (
        [ref[c] for c in range(5)] for ref in (own_ref, one_ref, two_ref, three_ref)
    )

    def ordered(swap, a, b):
        front = [jnp.where(swap, q, p) for p, q in zip(a, b)]
        back = [jnp.where(swap, p, q) for p, q in zip(a, b)]
        return join(front, back)

    mine = ordered(odd, own, one)
    other = ordered(odd, two, three)
    put(ordered(high, mine, other), colour_ref, depth_ref, clear_ref)


def blend_all(parts_ref, colour_ref, depth_ref, clear_ref):
    image = [parts_ref[0, c] for c in range(5)]
    for k in range(1, parts_ref.shape[0]):
        image = join(image, [parts_ref[k, c] for c in range(5)])
    put(image, colour_ref, depth_ref, clear_ref)


def pairs(count):
    first = [(i, i ^ 1) for i in range(count)]
    second = [(i, (i - 1 if i % 2 == 0 else i + 1)) for i in range(1, count - 1)]
    return first, second + [(0, 0), (count - 1, count - 1)]


def exchange(block, axis, dim, width):
    length = block.shape[dim]
    even = lax.axis_index(axis) % 2 == 0
    first, second = pairs(lax.axis_size(axis))
    low, high = 0, length - width
    one = lax.dynamic_slice_in_dim(block, jnp.where(even, high, low), width, dim)
    two = lax.dynamic_slice_in_dim(block, jnp.where(even, low, high), width, dim)
    return lax.ppermute(one, axis, first), lax.ppermute(two, axis, second)


def on_device(block):
    cells_z, rows, cols = block.shape
    count_z = lax.axis_size("gz")
    total_z = cells_z * count_z
    at_x, at_y, at_z = (lax.axis_index(a) for a in ("gx", "gy", "gz"))
    ids = jnp.stack([at_x, at_y, at_z]).astype(jnp.int32)
    piece = rows // count_z
    strip = 128

    za, zb = exchange(block, "gz", 0, 2)
    ya, yb = exchange(block, "gy", 1, EDGE)
    edge = lax.dynamic_slice_in_dim(block, jnp.where(at_x == 0, cols - strip, 0), strip, 2)
    edge = lax.ppermute(edge, "gx", [(0, 1), (1, 0)])

    smem = pl.BlockSpec(memory_space=pltpu.SMEM)
    vmem = pl.BlockSpec(memory_space=pltpu.VMEM)
    params = pltpu.CompilerParams(vmem_limit_bytes=40 * 1024 * 1024)
    f32 = jnp.float32
    image, part = pl.pallas_call(
        functools.partial(inner_kernel, total_z=total_z, last_y=lax.axis_size("gy") - 1),
        out_shape=(
            jax.ShapeDtypeStruct((5, rows, cols), f32),
            jax.ShapeDtypeStruct((4, 2, rows, cols), f32),
        ),
        in_specs=[smem, vmem, vmem, vmem, vmem],
        out_specs=(vmem, vmem),
        scratch_shapes=[pltpu.VMEM((rows, cols), f32), pltpu.VMEM((rows, cols), f32)],
        compiler_params=params,
        cost_estimate=pl.CostEstimate(
            flops=100 * block.size, bytes_accessed=8 * block.size, transcendentals=6 * block.size
        ),
        name="inner",
    )(ids, block, ya, yb, edge)

    four = count_z == 4
    if four:
        order = jnp.stack([at_z ^ 1, at_z ^ 2, at_z ^ 3, at_z]).astype(jnp.int32)
    else:
        order = jnp.arange(count_z, dtype=jnp.int32)
    layers = cells_z // 4
    out_specs = [pl.BlockSpec((5, piece, cols), lambda i, ids, order: (0, 0, 0))] * count_z
    parts = pl.pallas_call(
        functools.partial(outer_kernel, total_z=total_z, cells_z=cells_z),
        out_shape=[jax.ShapeDtypeStruct((5, piece, cols), f32)] * count_z,
        grid_spec=pltpu.PrefetchScalarGridSpec(
            num_scalar_prefetch=2,
            grid=(count_z,),
            in_specs=[
                pl.BlockSpec((4, piece, cols), lambda i, ids, order: (0, order[i], 0)),
                pl.BlockSpec((4, piece, cols), lambda i, ids, order: (layers - 1, order[i], 0)),
                pl.BlockSpec((2, piece, cols), lambda i, ids, order: (0, order[i], 0)),
                pl.BlockSpec((2, piece, cols), lambda i, ids, order: (0, order[i], 0)),
                pl.BlockSpec((5, piece, cols), lambda i, ids, order: (0, order[i], 0)),
                pl.BlockSpec((4, 2, piece, cols), lambda i, ids, order: (0, 0, order[i], 0)),
            ],
            out_specs=out_specs,
        ),
        compiler_params=params,
        name="outer",
    )(ids, order, block, block, za, zb, image, part)

    out_shape = (
        jax.ShapeDtypeStruct((3, piece, cols), f32),
        jax.ShapeDtypeStruct((piece, cols), f32),
        jax.ShapeDtypeStruct((piece, cols), f32),
    )
    if four:
        peers = [
            lax.ppermute(parts[s - 1], "gz", [(i, i ^ s) for i in range(count_z)]) for s in (1, 2, 3)
        ]
        return pl.pallas_call(
            blend_four,
            out_shape=out_shape,
            in_specs=[smem] + [vmem] * 4,
            out_specs=(vmem, vmem, vmem),
            name="blend",
        )(ids, parts[3], *peers)
    gathered = lax.all_to_all(jnp.stack(parts), "gz", split_axis=0, concat_axis=0, tiled=True)
    return pl.pallas_call(
        blend_all, out_shape=out_shape, in_specs=[vmem], out_specs=(vmem, vmem, vmem), name="blend"
    )(gathered)


def solution(mesh):
    return jax.shard_map(
        on_device,
        mesh=mesh,
        in_specs=(P("gz", "gy", "gx"),),
        out_specs=(P(None, ("gy", "gz"), "gx"), P(("gy", "gz"), "gx"), P(("gy", "gz"), "gx")),
        check_vma=False,
    )
```

time: 102 us -> 40.4 us (0.40)
  the two profiles are of different devices: /device:TPU:0 before, /device:TPU:8 now
where the time goes in v1:
time: 40.4 us; the launch traced here: 40.2 us
  starting transfers between devices  12.7 us (31%)
  Pallas kernels  11.7 us (29%)
  waiting for transfers between devices  10.4 us (26%)
  local copies, waits for them, and re-layouts  4.56 us (11%)
  between operations  0.75 us (2%)
    pallas_call x1, Pallas kernels, on_device(): pl.pallas_call(functools.partial(inner_kernel, total_z=total_z, last_y=la...  7.77 us
    ppermute x4, starting transfers between devices, exchange(): return (lax.ppermute(one, axis, first), lax.ppermute(two, axis, second))  7.27 us
    ppermute x3, waiting for transfers between devices, on_device(): lax.ppermute(parts[s - 1], 'gz', [(i, i ^ s) for i in range(count_z)])  6.97 us
    ppermute x3, starting transfers between devices, on_device(): lax.ppermute(parts[s - 1], 'gz', [(i, i ^ s) for i in range(count_z)])  5.4 us
    ppermute x4, waiting for transfers between devices, exchange(): return (lax.ppermute(one, axis, first), lax.ppermute(two, axis, second))  3.44 us
    dynamic_slice x1, local copies, waits for them, and re-layouts, on_device(): lax.dynamic_slice_in_dim(block, jnp.where(at_x == 0, cols - strip, 0), st...  2.46 us
    pallas_call x1, Pallas kernels, on_device(): pl.pallas_call(functools.partial(outer_kernel, total_z=total_z, cells_z=c...  2.05 us
    pallas_call x1, Pallas kernels, on_device(): pl.pallas_call(blend_four, out_shape=out_shape, in_specs=[smem] + [vmem]...  1.88 us
  transfers between devices with their start and end apart: 8, of which 4 were waited for; matrix products, arithmetic and copies ran while one was open for 2% of the time, Pallas kernels for 19%

profile of v1, /device:TPU:8, one launch (start us, length us, event | category | flops | bytes accessed | tf_op | source)
XLA Modules:
  0.0 40.2 jit_solution(5521146045357585983)
XLA Ops:
  0.6 2.5 %constant_dynamic-slice_fusion = f32[16,128,128]{2,1,0:T(8,128)} fusion(f32[16,128,256]{2,1,0:T(8,128)} %back_ref.1, s32[]{:T(128)S(6)} %select_n.38), kind=kLoop, calls=%fused_computation | loop fusion | bytes 2097156 | tf_op jit(solution)/shard_map/dynamic_slice | solution.py:212
  3.1 0.0 collective-permute-start.4
  3.2 1.6 %collective-permute-start = (f32[2,128,256]{2,1,0:T(8,128)S(1)}, f32[2,128,256]{2,1,0:T(8,128)S(1)}, u32[]{:S(2)}, u32[]{:S(2)}) collective-permute-start(f32[2,128,256]{2,1,0:T(8,128)S(1)} %get-tuple-element.18), channel_id=1, source_target_pairs={{0,1},{1,0},{2,3},{3,2},{4,5},{5,4},{6,7},{7,6},{8,9},{9,8},{10,11... | collective-permute-start | bytes 786440 | tf_op jit(solution)/shard_map/ppermute | solution.py:198
  4.7 0.7 %collective-permute-start.1 = (f32[2,128,256]{2,1,0:T(8,128)S(1)}, f32[2,128,256]{2,1,0:T(8,128)S(1)}, u32[]{:S(2)}, u32[]{:S(2)}) collective-permute-start(f32[2,128,256]{2,1,0:T(8,128)S(1)} %get-tuple-element.17), channel_id=1, source_target_pairs={{1,2},{2,1},{0,0},{3,3},{5,6},{6,5},{4,4},{7,7},{9,10},{10,9},{8,8... | collective-permute-start | bytes 786440 | tf_op jit(solution)/shard_map/ppermute | solution.py:198
  5.4 0.7 %constant_dynamic-slice_fusion.1 = (f32[16,8,256]{2,1,0:T(8,128)S(1)}, f32[16,8,256]{2,1,0:T(8,128)}) fusion(f32[16,128,256]{2,1,0:T(8,128)S(1)} %copy-done, s32[]{:T(128)S(6)} %select_n.37, s32[]{:T(128)S(6)} %select_n.36), kind=kLoop, calls=%fused_computation.1 | loop fusion | bytes 524296 | tf_op jit(solution)/shard_map/dynamic_slice | solution.py:197
  6.1 0.4 %collective-permute-start.2 = (f32[16,8,256]{2,1,0:T(8,128)}, f32[16,8,256]{2,1,0:T(8,128)S(1)}, u32[]{:S(2)}, u32[]{:S(2)}) collective-permute-start(f32[16,8,256]{2,1,0:T(8,128)} %get-tuple-element.16), channel_id=1, source_target_pairs={{0,4},{4,0},{8,12},{12,8},{1,5},{5,1},{9,13},{13,9},{2,6},{6,2},{1... | collective-permute-start | bytes 393224 | tf_op jit(solution)/shard_map/ppermute | solution.py:198
  6.5 4.6 %collective-permute-start.3 = (f32[16,8,256]{2,1,0:T(8,128)S(1)}, f32[16,8,256]{2,1,0:T(8,128)S(1)}, u32[]{:S(2)}, u32[]{:S(2)}) collective-permute-start(f32[16,8,256]{2,1,0:T(8,128)S(1)} %get-tuple-element.15), channel_id=1, source_target_pairs={{4,8},{8,4},{0,0},{12,12},{5,9},{9,5},{1,1},{13,13},{6,10},{10,6},... | collective-permute-start | bytes 393224 | tf_op jit(solution)/shard_map/ppermute | solution.py:198
  11.1 0.1 pad_add_fusion.ids
  11.2 0.1 pad_add_fusion.1.blocks
  11.3 0.6 %collective-permute-done.2.ya_ref = f32[16,8,256]{2,1,0:T(8,128)S(1)} collective-permute-done((f32[16,8,256]{2,1,0:T(8,128)}, f32[16,8,256]{2,1,0:T(8,128)S(1)}, u32[]{:S(2)}, u32[]{:S(2)}) %collective-permute-start.2) | collective-permute-done | bytes 131104 | tf_op jit(solution)/shard_map/ppermute | solution.py:198
  11.9 2.8 %collective-permute-done.3.yb_ref = f32[16,8,256]{2,1,0:T(8,128)S(1)} collective-permute-done((f32[16,8,256]{2,1,0:T(8,128)S(1)}, f32[16,8,256]{2,1,0:T(8,128)S(1)}, u32[]{:S(2)}, u32[]{:S(2)}) %collective-permute-start.3) | collective-permute-done | bytes 131104 | tf_op jit(solution)/shard_map/ppermute | solution.py:198
  14.7 0.0 collective-permute-done.4.e_ref
  14.7 7.8 %inner.1 = (f32[5,128,256]{2,1,0:T(8,128)S(1)}, f32[4,2,128,256]{3,2,1,0:T(8,128)S(1)}) custom-call(s32[3]{0:T(128)S(1)} %pad_add_fusion.ids, f32[16,128,256]{2,1,0:T(8,128)S(1)} %copy-done, f32[16,8,256]{2,1,0:T(8,128)S(1)} %collective-permute-done.2.ya_ref, f32[16,8,256]{2,1,0:T(8,128)S(1)} %collective-permute-done.3.yb_ref, ...), custom_call_target="tpu_custom_call" | custom-call | flops 52428800 | bytes 4194304 | tf_op jit(solution)/shard_map/inner/pallas_call | solution.py:219
  22.5 0.0 collective-permute-done.za_ref
  22.5 2.0 %outer.1 = (f32[5,32,256]{2,1,0:T(8,128)S(1)}, f32[5,32,256]{2,1,0:T(8,128)S(1)}, f32[5,32,256]{2,1,0:T(8,128)S(1)}, f32[5,32,256]{2,1,0:T(8,128)S(1)}) custom-call(s32[3]{0:T(128)S(1)} %pad_add_fusion.ids, s32[4]{0:T(128)S(1)} %pad_add_fusion.1.blocks, f32[16,128,256]{2,1,0:T(8,128)S(1)} %copy-done, f32[16,128,256]{2,1,0:T(8,128)S(1)} %copy-done, ...), custom_call_target="tpu_custom_call" | custom-call | tf_op jit(solution)/shard_map/outer/pallas_call | solution.py:242
  24.6 0.7 %copy-done.1 = f32[5,32,256]{2,1,0:T(8,128)} copy-done((f32[5,32,256]{2,1,0:T(8,128)}, f32[5,32,256]{2,1,0:T(8,128)S(1)}, u32[]{:S(2)}) %copy-start.1) | copy-done | bytes 163864
  25.3 3.9 %collective-permute-start.5 = (f32[5,32,256]{2,1,0:T(8,128)S(1)}, f32[5,32,256]{2,1,0:T(8,128)S(1)}, u32[]{:S(2)}, u32[]{:S(2)}) collective-permute-start(f32[5,32,256]{2,1,0:T(8,128)S(1)} %get-tuple-element.12), channel_id=1, source_target_pairs={{0,1},{1,0},{2,3},{3,2},{4,5},{5,4},{6,7},{7,6},{8,9},{9,8},{10,11... | collective-permute-start | bytes 491528 | tf_op jit(solution)/shard_map/ppermute | solution.py:269
  29.2 0.0 collective-permute-start.6
  29.2 1.5 %collective-permute-start.7 = (f32[5,32,256]{2,1,0:T(8,128)S(1)}, f32[5,32,256]{2,1,0:T(8,128)S(1)}, u32[]{:S(2)}, u32[]{:S(2)}) collective-permute-start(f32[5,32,256]{2,1,0:T(8,128)S(1)} %get-tuple-element.14), channel_id=1, source_target_pairs={{0,3},{1,2},{2,1},{3,0},{4,7},{5,6},{6,5},{7,4},{8,11},{9,10},{10,... | collective-permute-start | bytes 491528 | tf_op jit(solution)/shard_map/ppermute | solution.py:269
  30.7 3.0 %collective-permute-done.5.one_ref = f32[5,32,256]{2,1,0:T(8,128)S(1)} collective-permute-done((f32[5,32,256]{2,1,0:T(8,128)S(1)}, f32[5,32,256]{2,1,0:T(8,128)S(1)}, u32[]{:S(2)}, u32[]{:S(2)}) %collective-permute-start.5) | collective-permute-done | bytes 163872 | tf_op jit(solution)/shard_map/ppermute | solution.py:269
  33.7 4.0 %collective-permute-done.6.two_ref = f32[5,32,256]{2,1,0:T(8,128)S(1)} collective-permute-done((f32[5,32,256]{2,1,0:T(8,128)S(1)}, f32[5,32,256]{2,1,0:T(8,128)S(1)}, u32[]{:S(2)}, u32[]{:S(2)}) %collective-permute-start.6) | collective-permute-done | bytes 163872 | tf_op jit(solution)/shard_map/ppermute | solution.py:269
  37.6 0.6 %copy-done.4 = f32[5,32,256]{2,1,0:T(8,128)} copy-done((f32[5,32,256]{2,1,0:T(8,128)}, f32[5,32,256]{2,1,0:T(8,128)S(1)}, u32[]{:S(2)}) %copy-start.4) | copy-done | bytes 163864
  38.3 0.1 copy-done.5
  38.3 1.9 %blend.1 = (f32[3,32,256]{2,1,0:T(8,128)}, f32[32,256]{1,0:T(8,128)}, f32[32,256]{1,0:T(8,128)}) custom-call(s32[3]{0:T(128)} %copy-done.2, f32[5,32,256]{2,1,0:T(8,128)} %copy-done.1, f32[5,32,256]{2,1,0:T(8,128)} %copy-done.3, f32[5,32,256]{2,1,0:T(8,128)} %copy-done.4, f32[5,32,256]{2,1,0:T(8,128)} %copy-done.5), custom_call_target="tpu_custom_call" | custom-call | tf_op jit(solution)/shard_map/blend/pallas_call | solution.py:271
  (12 shorter events, 0.1 us)
Async XLA Ops:
  0.6 2.5 %copy-start = (f32[16,128,256]{2,1,0:T(8,128)S(1)}, f32[16,128,256]{2,1,0:T(8,128)}, u32[]{:S(2)}) copy-start(f32[16,128,256]{2,1,0:T(8,128)} %back_ref.1) | copy-start | bytes 6291460
  3.1 11.6 %collective-permute-start.4 = (f32[16,128,128]{2,1,0:T(8,128)}, f32[16,128,128]{2,1,0:T(8,128)}, u32[]{:S(2)}, u32[]{:S(2)}) collective-permute-start(f32[16,128,128]{2,1,0:T(8,128)} %constant_dynamic-slice_fusion), channel_id=1, source_target_pairs={{0,16},{16,0},{1,17},{17,1},{2,18},{18,2},{3,19},{19,3},{4,20},{20... | collective-permute-start | bytes 3145736 | tf_op jit(solution)/shard_map/ppermute | solution.py:213
  3.2 19.3 %collective-permute-start = (f32[2,128,256]{2,1,0:T(8,128)S(1)}, f32[2,128,256]{2,1,0:T(8,128)S(1)}, u32[]{:S(2)}, u32[]{:S(2)}) collective-permute-start(f32[2,128,256]{2,1,0:T(8,128)S(1)} %get-tuple-element.18), channel_id=1, source_target_pairs={{0,1},{1,0},{2,3},{3,2},{4,5},{5,4},{6,7},{7,6},{8,9},{9,8},{10,11... | collective-permute-start | bytes 786440 | tf_op jit(solution)/shard_map/ppermute | solution.py:198
  4.7 17.8 %collective-permute-start.1 = (f32[2,128,256]{2,1,0:T(8,128)S(1)}, f32[2,128,256]{2,1,0:T(8,128)S(1)}, u32[]{:S(2)}, u32[]{:S(2)}) collective-permute-start(f32[2,128,256]{2,1,0:T(8,128)S(1)} %get-tuple-element.17), channel_id=1, source_target_pairs={{1,2},{2,1},{0,0},{3,3},{5,6},{6,5},{4,4},{7,7},{9,10},{10,9},{8,8... | collective-permute-start | bytes 786440 | tf_op jit(solution)/shard_map/ppermute | solution.py:198
  6.1 5.8 %collective-permute-start.2 = (f32[16,8,256]{2,1,0:T(8,128)}, f32[16,8,256]{2,1,0:T(8,128)S(1)}, u32[]{:S(2)}, u32[]{:S(2)}) collective-permute-start(f32[16,8,256]{2,1,0:T(8,128)} %get-tuple-element.16), channel_id=1, source_target_pairs={{0,4},{4,0},{8,12},{12,8},{1,5},{5,1},{9,13},{13,9},{2,6},{6,2},{1... | collective-permute-start | bytes 393224 | tf_op jit(solution)/shard_map/ppermute | solution.py:198
  6.5 8.2 %collective-permute-start.3 = (f32[16,8,256]{2,1,0:T(8,128)S(1)}, f32[16,8,256]{2,1,0:T(8,128)S(1)}, u32[]{:S(2)}, u32[]{:S(2)}) collective-permute-start(f32[16,8,256]{2,1,0:T(8,128)S(1)} %get-tuple-element.15), channel_id=1, source_target_pairs={{4,8},{8,4},{0,0},{12,12},{5,9},{9,5},{1,1},{13,13},{6,10},{10,6},... | collective-permute-start | bytes 393224 | tf_op jit(solution)/shard_map/ppermute | solution.py:198
  11.2 11.3 %copy-start.2 = (s32[3]{0:T(128)}, s32[3]{0:T(128)S(1)}, u32[]{:S(2)}) copy-start(s32[3]{0:T(128)S(1)} %pad_add_fusion.ids) | copy-start | bytes 40
  24.6 0.7 %copy-start.1 = (f32[5,32,256]{2,1,0:T(8,128)}, f32[5,32,256]{2,1,0:T(8,128)S(1)}, u32[]{:S(2)}) copy-start(f32[5,32,256]{2,1,0:T(8,128)S(1)} %get-tuple-element.11.own_ref) | copy-start | bytes 491524
  25.3 8.4 %collective-permute-start.5 = (f32[5,32,256]{2,1,0:T(8,128)S(1)}, f32[5,32,256]{2,1,0:T(8,128)S(1)}, u32[]{:S(2)}, u32[]{:S(2)}) collective-permute-start(f32[5,32,256]{2,1,0:T(8,128)S(1)} %get-tuple-element.12), channel_id=1, source_target_pairs={{0,1},{1,0},{2,3},{3,2},{4,5},{5,4},{6,7},{7,6},{8,9},{9,8},{10,11... | collective-permute-start | bytes 491528 | tf_op jit(solution)/shard_map/ppermute | solution.py:269
  29.2 8.4 %collective-permute-start.6 = (f32[5,32,256]{2,1,0:T(8,128)S(1)}, f32[5,32,256]{2,1,0:T(8,128)S(1)}, u32[]{:S(2)}, u32[]{:S(2)}) collective-permute-start(f32[5,32,256]{2,1,0:T(8,128)S(1)} %get-tuple-element.13), channel_id=1, source_target_pairs={{0,2},{1,3},{2,0},{3,1},{4,6},{5,7},{6,4},{7,5},{8,10},{9,11},{10,... | collective-permute-start | bytes 491528 | tf_op jit(solution)/shard_map/ppermute | solution.py:269
  29.2 8.4 %collective-permute-start.7 = (f32[5,32,256]{2,1,0:T(8,128)S(1)}, f32[5,32,256]{2,1,0:T(8,128)S(1)}, u32[]{:S(2)}, u32[]{:S(2)}) collective-permute-start(f32[5,32,256]{2,1,0:T(8,128)S(1)} %get-tuple-element.14), channel_id=1, source_target_pairs={{0,3},{1,2},{2,1},{3,0},{4,7},{5,6},{6,5},{7,4},{8,11},{9,10},{10,... | collective-permute-start | bytes 491528 | tf_op jit(solution)/shard_map/ppermute | solution.py:269
  33.7 4.0 %copy-start.3 = (f32[5,32,256]{2,1,0:T(8,128)}, f32[5,32,256]{2,1,0:T(8,128)S(1)}, u32[]{:S(2)}) copy-start(f32[5,32,256]{2,1,0:T(8,128)S(1)} %collective-permute-done.5.one_ref) | copy-start | bytes 491524
  37.6 0.7 %copy-start.4 = (f32[5,32,256]{2,1,0:T(8,128)}, f32[5,32,256]{2,1,0:T(8,128)S(1)}, u32[]{:S(2)}) copy-start(f32[5,32,256]{2,1,0:T(8,128)S(1)} %collective-permute-done.6.two_ref) | copy-start | bytes 491524
  37.6 0.7 %copy-start.5 = (f32[5,32,256]{2,1,0:T(8,128)}, f32[5,32,256]{2,1,0:T(8,128)S(1)}, u32[]{:S(2)}) copy-start(f32[5,32,256]{2,1,0:T(8,128)S(1)} %collective-permute-done.7.three_ref) | copy-start | bytes 491524

commit v2 on v1

v2 whole, which is shorter than its diff:
```python
import functools

import jax
import jax.numpy as jnp
from jax import lax
from jax.experimental import pallas as pl
from jax.experimental.pallas import tpu as pltpu
from jax.sharding import PartitionSpec as P

EDGE = 8


def band(offset):
    one = jnp.where(offset == 1, 8.0, jnp.where(offset == -1, -8.0, 0.0))
    two = jnp.where(offset == 2, -1.0, jnp.where(offset == -2, 1.0, 0.0))
    return (one + two).astype(jnp.bfloat16)


def split(value):
    high = value.astype(jnp.bfloat16)
    return high, (value - high.astype(jnp.float32)).astype(jnp.bfloat16)


def dot(a, b):
    return jnp.dot(a, b, preferred_element_type=jnp.float32)


def emit(sample, base, lin, grad_z, depth_step, through, position):
    root = lax.rsqrt(base + grad_z * grad_z * (1.0 / 144.0))
    diffuse = 0.3 + jnp.maximum((lin + grad_z * (0.64 * 0.7 / 12.0)) * root, 0.0)
    grown = jnp.exp(sample)
    optical = jnp.log(1.0 + grown) * ((2.0 - root * root) * depth_step)
    behind = through * jnp.exp(-optical)
    weight = through - behind
    lit = weight * diffuse
    square = grown * grown
    blue = lit / (1.0 + square)
    return behind, (blue * square, lit * jnp.exp(-0.5 * sample * sample), blue, weight * position)


def place():
    return tuple(lax.axis_index(a) for a in ("gx", "gy", "gz"))


def edges_kernel(x_ref, za_ref, zb_ref, ya_ref, yb_ref, e_ref, sems):
    cells_z, rows, cols = x_ref.shape
    at_x, at_y, at_z = place()
    strip = e_ref.shape[2]

    def starts(position, low, high):
        even = position % 2 == 0
        return jnp.where(even, high, low), jnp.where(even, low, high)

    z_one, z_two = starts(at_z, 0, cells_z - 2)
    y_one, y_two = (pl.multiple_of(v, EDGE) for v in starts(at_y, 0, rows - EDGE))
    x_one = pl.multiple_of(jnp.where(at_x == 0, cols - strip, 0), strip)
    copies = [
        pltpu.make_async_copy(x_ref.at[pl.ds(z_one, 2)], za_ref, sems.at[0]),
        pltpu.make_async_copy(x_ref.at[pl.ds(z_two, 2)], zb_ref, sems.at[1]),
        pltpu.make_async_copy(x_ref.at[:, pl.ds(y_one, EDGE)], ya_ref, sems.at[2]),
        pltpu.make_async_copy(x_ref.at[:, pl.ds(y_two, EDGE)], yb_ref, sems.at[3]),
        pltpu.make_async_copy(x_ref.at[:, :, pl.ds(x_one, strip)], e_ref, sems.at[4]),
    ]
    for copy in copies:
        copy.start()
    for copy in copies:
        copy.wait()


def inner_kernel(
    x_ref, ya_ref, yb_ref, e_ref, image_ref, part_ref, gx0, gx1, gy0, gy1, wx_ref, wy_ref, *, total_z, last_y
):
    cells_z, rows, cols = x_ref.shape
    strip = e_ref.shape[2]
    depth_step = 2.0 / total_z
    at_x, at_y, at_z = place()
    even = at_y % 2 == 0
    iota = functools.partial(lax.broadcasted_iota, jnp.int32)
    along_x = band(iota((cols, cols), 0) - iota((cols, cols), 1))
    lane = iota((strip, cols), 0) - iota((strip, cols), 1)
    beyond_x = band(lane + jnp.where(at_x == 0, cols, -strip))
    along_y = band(iota((rows, rows), 1) - iota((rows, rows), 0))
    out_row, slot = iota((rows, 2 * EDGE), 0), iota((rows, 2 * EDGE), 1)
    first = slot < EDGE
    cell = slot % EDGE
    below = jnp.where(first, even.astype(jnp.int32), 1 - even.astype(jnp.int32)) > 0
    top = jnp.where(at_y > 0, -EDGE, -4 * EDGE)
    bottom = jnp.where(at_y < last_y, rows, rows + 4 * EDGE)
    beyond_y = band(cell + jnp.where(below, bottom, top) - out_row)
    wx_ref[...] = jnp.concatenate([along_x, along_x, beyond_x, beyond_x], axis=0)
    wy_ref[...] = jnp.concatenate([along_y, along_y, beyond_y, beyond_y], axis=1)

    def gradients(k, gx_ref, gy_ref):
        high, low = split(x_ref[k])
        edge_high, edge_low = split(e_ref[k])
        rim_high, rim_low = split(jnp.concatenate([ya_ref[k], yb_ref[k]], axis=0))
        gx_ref[...] = dot(jnp.concatenate([high, low, edge_high, edge_low], axis=1), wx_ref[...])
        gy_ref[...] = dot(wy_ref[...], jnp.concatenate([high, low, rim_high, rim_low], axis=0))

    def pair(at, gx_ref, gy_ref):
        grad_x, grad_y = gx_ref[at], gy_ref[at]
        base = 1.0 + (grad_x * grad_x + grad_y * grad_y) * (1.0 / 144.0)
        lin = grad_x * (0.48 * 0.7 / 12.0) + grad_y * (0.6 * 0.7 / 12.0)
        return base, lin

    chunk = 16
    spans = [pl.ds(r, chunk) for r in range(0, rows, chunk)]
    slots = ((gx0, gy0), (gx1, gy1))

    def keep(index, pairs):
        for at in spans:
            base, lin = pair(at, *pairs)
            part_ref[index, 0, at] = base
            part_ref[index, 1, at] = lin

    def shade(k, pairs):
        position = ((at_z * cells_z + k).astype(jnp.float32) + 0.5) / total_z
        for at in spans:
            base, lin = pair(at, *pairs)
            grad_z = (x_ref[k - 2, at] - x_ref[k + 2, at]) + 8.0 * (x_ref[k + 1, at] - x_ref[k - 1, at])
            through, adds = emit(x_ref[k, at], base, lin, grad_z, depth_step, image_ref[4, at], position)
            image_ref[4, at] = through
            for channel, value in enumerate(adds):
                image_ref[channel, at] += value

    for channel in range(4):
        image_ref[channel] = jnp.zeros((rows, cols), jnp.float32)
    image_ref[4] = jnp.ones((rows, cols), jnp.float32)

    gradients(0, *slots[0])
    gradients(1, *slots[1])
    keep(0, slots[0])
    gradients(2, *slots[0])
    keep(1, slots[1])

    @pl.loop(0, (cells_z - 4) // 2)
    def _(step):
        k = 2 + 2 * step
        gradients(k + 1, *slots[1])
        shade(k, slots[0])
        gradients(k + 2, *slots[0])
        shade(k + 1, slots[1])

    gradients(cells_z - 1, *slots[1])
    keep(2, slots[0])
    keep(3, slots[1])


def outer_kernel(x_ref, za_ref, zb_ref, image_ref, part_ref, *out_refs, total_z):
    cells_z, _, cols = x_ref.shape
    depth_step = 2.0 / total_z
    at_z = place()[2]
    last_z = total_z // cells_z - 1
    even = at_z % 2 == 0
    count, piece = len(out_refs), out_refs[0].shape[1]
    chunk = min(piece, 16)
    none = jnp.zeros((chunk, cols), jnp.float32)
    for out, start in [(o, s) for o in range(count) for s in range(0, piece, chunk)]:
        block = at_z ^ out if count == 4 else out
        at = pl.ds(pl.multiple_of(block * piece + start, 8), chunk)

        def before(layer):
            return jnp.where(at_z > 0, jnp.where(even, zb_ref[layer, at], za_ref[layer, at]), none)

        def after(layer):
            return jnp.where(at_z < last_z, jnp.where(even, za_ref[layer, at], zb_ref[layer, at]), none)

        f = [x_ref[k, at] for k in range(4)]
        b = [x_ref[cells_z - 4 + k, at] for k in range(4)]
        ahead, next_ahead, behind, next_behind = before(0), before(1), after(0), after(1)
        cells = (
            (0, 0, f[0], (ahead - f[2]) + 8.0 * (f[1] - next_ahead)),
            (1, 1, f[1], (next_ahead - f[3]) + 8.0 * (f[2] - f[0])),
            (2, cells_z - 2, b[2], (b[0] - behind) + 8.0 * (b[3] - b[1])),
            (3, cells_z - 1, b[3], (b[1] - next_behind) + 8.0 * (behind - b[2])),
        )
        through = jnp.ones_like(none)
        sums = [none] * 4
        for index, k, sample, grad_z in cells:
            if index == 2:
                sums = [s + through * image_ref[c, at] for c, s in enumerate(sums)]
                through = through * image_ref[4, at]
            position = ((at_z * cells_z + k).astype(jnp.float32) + 0.5) / total_z
            through, adds = emit(
                sample, part_ref[index, 0, at], part_ref[index, 1, at], grad_z, depth_step, through, position
            )
            sums = [s + a for s, a in zip(sums, adds)]
        for channel, value in enumerate(sums + [through]):
            out_refs[out][channel, pl.ds(start, chunk)] = value


def join(front, back):
    through = front[4]
    return [front[c] + through * back[c] for c in range(4)] + [through * back[4]]


def put(image, colour_ref, depth_ref, clear_ref):
    for channel in range(3):
        colour_ref[channel] = image[channel]
    depth_ref[...] = image[3]
    clear_ref[...] = image[4]


def blend_four(own_ref, one_ref, two_ref, three_ref, colour_ref, depth_ref, clear_ref):
    at_z = place()[2]
    odd, high = at_z % 2 == 1, at_z >= 2
    own, one, two, three = (
        [ref[c] for c in range(5)] for ref in (own_ref, one_ref, two_ref, three_ref)
    )

    def ordered(swap, a, b):
        front = [jnp.where(swap, q, p) for p, q in zip(a, b)]
        back = [jnp.where(swap, p, q) for p, q in zip(a, b)]
        return join(front, back)

    mine = ordered(odd, own, one)
    other = ordered(odd, two, three)
    put(ordered(high, mine, other), colour_ref, depth_ref, clear_ref)


def blend_all(parts_ref, colour_ref, depth_ref, clear_ref):
    image = [parts_ref[0, c] for c in range(5)]
    for k in range(1, parts_ref.shape[0]):
        image = join(image, [parts_ref[k, c] for c in range(5)])
    put(image, colour_ref, depth_ref, clear_ref)


def pairs(count, closed):
    ends = [(0, count - 1), (count - 1, 0)] if closed else [(0, 0), (count - 1, count - 1)]
    first = [(i, i ^ 1) for i in range(count)]
    second = [(i, (i - 1 if i % 2 == 0 else i + 1)) for i in range(1, count - 1)]
    return first, second + ends


def on_device(block):
    cells_z, rows, cols = block.shape
    count_z, count_y = lax.axis_size("gz"), lax.axis_size("gy")
    total_z = cells_z * count_z
    piece = rows // count_z
    strip = 128
    f32 = jnp.float32

    def shaped(*shape):
        return jax.ShapeDtypeStruct(shape, f32)

    vmem = pl.BlockSpec(memory_space=pltpu.VMEM)
    edges = pl.pallas_call(
        edges_kernel,
        out_shape=(
            shaped(2, rows, cols), shaped(2, rows, cols),
            shaped(cells_z, EDGE, cols), shaped(cells_z, EDGE, cols),
            shaped(cells_z, rows, strip),
        ),
        in_specs=[pl.BlockSpec(memory_space=pltpu.HBM)],
        out_specs=(vmem,) * 5,
        scratch_shapes=[pltpu.SemaphoreType.DMA((5,))],
        compiler_params=pltpu.CompilerParams(vmem_limit_bytes=4 * 1024 * 1024),
        name="edges",
    )(block)
    z_first, z_second = pairs(count_z, False)
    y_first, y_second = pairs(count_y, True)
    za = lax.ppermute(edges[0], "gz", z_first)
    zb = lax.ppermute(edges[1], "gz", z_second)
    ya = lax.ppermute(edges[2], "gy", y_first)
    yb = lax.ppermute(edges[3], "gy", y_second)
    edge = lax.ppermute(edges[4], "gx", [(0, 1), (1, 0)])

    image, part = pl.pallas_call(
        functools.partial(inner_kernel, total_z=total_z, last_y=count_y - 1),
        out_shape=(shaped(5, rows, cols), shaped(4, 2, rows, cols)),
        in_specs=[vmem] * 4,
        out_specs=(vmem, vmem),
        scratch_shapes=[pltpu.VMEM((rows, cols), f32)] * 4
        + [
            pltpu.VMEM((2 * (cols + strip), cols), jnp.bfloat16),
            pltpu.VMEM((rows, 2 * (rows + 2 * EDGE)), jnp.bfloat16),
        ],
        compiler_params=pltpu.CompilerParams(vmem_limit_bytes=16 * 1024 * 1024),
        cost_estimate=pl.CostEstimate(
            flops=100 * block.size, bytes_accessed=8 * block.size, transcendentals=6 * block.size
        ),
        name="inner",
    )(block, ya, yb, edge)

    parts = pl.pallas_call(
        functools.partial(outer_kernel, total_z=total_z),
        out_shape=[shaped(5, piece, cols)] * count_z,
        in_specs=[vmem] * 5,
        out_specs=[vmem] * count_z,
        compiler_params=pltpu.CompilerParams(vmem_limit_bytes=16 * 1024 * 1024),
        name="outer",
    )(block, za, zb, image, part)

    out_shape = (shaped(3, piece, cols), shaped(piece, cols), shaped(piece, cols))
    small = pltpu.CompilerParams(vmem_limit_bytes=8 * 1024 * 1024)
    if count_z == 4:
        peers = [
            lax.ppermute(parts[s], "gz", [(i, i ^ s) for i in range(count_z)]) for s in (1, 2, 3)
        ]
        return pl.pallas_call(
            blend_four,
            out_shape=out_shape,
            in_specs=[vmem] * 4,
            out_specs=(vmem, vmem, vmem),
            compiler_params=small,
            name="blend",
        )(parts[0], *peers)
    gathered = lax.all_to_all(jnp.stack(parts), "gz", split_axis=0, concat_axis=0, tiled=True)
    return pl.pallas_call(
        blend_all,
        out_shape=out_shape,
        in_specs=[vmem],
        out_specs=(vmem, vmem, vmem),
        compiler_params=small,
        name="blend",
    )(gathered)


def solution(mesh):
    return jax.shard_map(
        on_device,
        mesh=mesh,
        in_specs=(P("gz", "gy", "gx"),),
        out_specs=(P(None, ("gy", "gz"), "gx"), P(("gy", "gz"), "gx"), P(("gy", "gz"), "gx")),
        check_vma=False,
    )
```

time: 40.4 us -> 35.4 us (0.88)
  the two profiles are of different devices: /device:TPU:8 before, /device:TPU:0 now
where the time goes in v2:
time: 35.4 us; the launch traced here: 35.2 us
  starting transfers between devices  13.4 us (38%)
  waiting for transfers between devices  13.2 us (37%)
  Pallas kernels  6.36 us (18%)
  local copies, waits for them, and re-layouts  1.59 us (4%)
  between operations  0.69 us (2%)
    ppermute x3, waiting for transfers between devices, on_device(): lax.ppermute(parts[s], 'gz', [(i, i ^ s) for i in range(count_z)])  6.7 us
    ppermute x3, starting transfers between devices, on_device(): lax.ppermute(parts[s], 'gz', [(i, i ^ s) for i in range(count_z)])  5.54 us
    ppermute x1, waiting for transfers between devices, on_device(): yb = lax.ppermute(edges[3], 'gy', y_second)  4.94 us
    pallas_call x1, Pallas kernels, on_device(): pl.pallas_call(functools.partial(inner_kernel, total_z=total_z, last_y=co...  4.64 us
    ppermute x1, starting transfers between devices, on_device(): za = lax.ppermute(edges[0], 'gz', z_first)  2.56 us
    ppermute x1, starting transfers between devices, on_device(): yb = lax.ppermute(edges[3], 'gy', y_second)  2.47 us
    ppermute x1, starting transfers between devices, on_device(): ya = lax.ppermute(edges[2], 'gy', y_first)  1.64 us
    unnamed x4, local copies, waits for them, and re-layouts  1.59 us
  transfers between devices with their start and end apart: 8, of which 4 were waited for; matrix products, arithmetic and copies ran while one was open for 0% of the time, Pallas kernels for 13%

profile of v2, /device:TPU:0, one launch (start us, length us, event | category | flops | bytes accessed | tf_op | source)
XLA Modules:
  0.0 35.2 jit_solution(16603309302855434278)
XLA Ops:
  0.6 0.0 copy-start
  0.6 1.6 %copy-done = f32[16,128,256]{2,1,0:T(8,128)S(1)} copy-done((f32[16,128,256]{2,1,0:T(8,128)S(1)}, f32[16,128,256]{2,1,0:T(8,128)}, u32[]{:S(2)}) %copy-start) | copy-done | bytes 2097176
  2.2 0.0 copy-start.1
  2.2 0.2 edges.1
  2.4 0.5 %collective-permute-start.4 = (f32[16,128,128]{2,1,0:T(8,128)S(1)}, f32[16,128,128]{2,1,0:T(8,128)S(1)}, u32[]{:S(2)}, u32[]{:S(2)}) collective-permute-start(f32[16,128,128]{2,1,0:T(8,128)S(1)} %get-tuple-element.18), channel_id=1, source_target_pairs={{0,16},{16,0},{1,17},{17,1},{2,18},{18,2},{3,19},{19,3},{4,20},{20... | collective-permute-start | bytes 3145736 | tf_op jit(solution)/shard_map/ppermute | solution.py:266
  2.9 2.6 %collective-permute-start = (f32[2,128,256]{2,1,0:T(8,128)S(1)}, f32[2,128,256]{2,1,0:T(8,128)S(1)}, u32[]{:S(2)}, u32[]{:S(2)}) collective-permute-start(f32[2,128,256]{2,1,0:T(8,128)S(1)} %get-tuple-element.14), channel_id=1, source_target_pairs={{0,1},{1,0},{2,3},{3,2},{4,5},{5,4},{6,7},{7,6},{8,9},{9,8},{10,11... | collective-permute-start | bytes 786440 | tf_op jit(solution)/shard_map/ppermute | solution.py:262
  5.5 0.7 %collective-permute-start.1 = (f32[2,128,256]{2,1,0:T(8,128)S(1)}, f32[2,128,256]{2,1,0:T(8,128)S(1)}, u32[]{:S(2)}, u32[]{:S(2)}) collective-permute-start(f32[2,128,256]{2,1,0:T(8,128)S(1)} %get-tuple-element.15), channel_id=1, source_target_pairs={{1,2},{2,1},{0,0},{3,3},{5,6},{6,5},{4,4},{7,7},{9,10},{10,9},{8,8... | collective-permute-start | bytes 786440 | tf_op jit(solution)/shard_map/ppermute | solution.py:263
  6.2 1.6 %collective-permute-start.2 = (f32[16,8,256]{2,1,0:T(8,128)S(1)}, f32[16,8,256]{2,1,0:T(8,128)S(1)}, u32[]{:S(2)}, u32[]{:S(2)}) collective-permute-start(f32[16,8,256]{2,1,0:T(8,128)S(1)} %get-tuple-element.16), channel_id=1, source_target_pairs={{0,4},{4,0},{8,12},{12,8},{1,5},{5,1},{9,13},{13,9},{2,6},{6,2},{1... | collective-permute-start | bytes 393224 | tf_op jit(solution)/shard_map/ppermute | solution.py:264
  7.8 2.5 %collective-permute-start.3 = (f32[16,8,256]{2,1,0:T(8,128)S(1)}, f32[16,8,256]{2,1,0:T(8,128)S(1)}, u32[]{:S(2)}, u32[]{:S(2)}) collective-permute-start(f32[16,8,256]{2,1,0:T(8,128)S(1)} %get-tuple-element.17), channel_id=1, source_target_pairs={{4,8},{8,4},{0,12},{12,0},{5,9},{9,5},{1,13},{13,1},{6,10},{10,6},... | collective-permute-start | bytes 393224 | tf_op jit(solution)/shard_map/ppermute | solution.py:265
  10.3 1.5 %collective-permute-done.2.ya_ref = f32[16,8,256]{2,1,0:T(8,128)S(1)} collective-permute-done((f32[16,8,256]{2,1,0:T(8,128)S(1)}, f32[16,8,256]{2,1,0:T(8,128)S(1)}, u32[]{:S(2)}, u32[]{:S(2)}) %collective-permute-start.2) | collective-permute-done | bytes 131104 | tf_op jit(solution)/shard_map/ppermute | solution.py:264
  11.8 4.9 %collective-permute-done.3.yb_ref = f32[16,8,256]{2,1,0:T(8,128)S(1)} collective-permute-done((f32[16,8,256]{2,1,0:T(8,128)S(1)}, f32[16,8,256]{2,1,0:T(8,128)S(1)}, u32[]{:S(2)}, u32[]{:S(2)}) %collective-permute-start.3) | collective-permute-done | bytes 131104 | tf_op jit(solution)/shard_map/ppermute | solution.py:265
  16.8 0.0 collective-permute-done.4.e_ref
  16.8 0.0 copy-done.1
  16.8 4.6 %inner.1 = (f32[5,128,256]{2,1,0:T(8,128)S(1)}, f32[4,2,128,256]{3,2,1,0:T(8,128)S(1)}) custom-call(f32[16,128,256]{2,1,0:T(8,128)S(1)} %copy-done.1, f32[16,8,256]{2,1,0:T(8,128)S(1)} %collective-permute-done.2.ya_ref, f32[16,8,256]{2,1,0:T(8,128)S(1)} %collective-permute-done.3.yb_ref, f32[16,128,128]{2,1,0:T(8,128)S(1)} %collective-permute-done.4.e_ref), custom_call_target="tpu_custom_call" | custom-call | flops 52428800 | bytes 4194304 | tf_op jit(solution)/shard_map/inner/pallas_call | solution.py:268
  21.4 0.0 collective-permute-done.za_ref
  21.4 0.0 collective-permute-done.1.zb_ref
  21.4 0.8 %outer.1 = (f32[5,32,256]{2,1,0:T(8,128)S(1)}, f32[5,32,256]{2,1,0:T(8,128)S(1)}, f32[5,32,256]{2,1,0:T(8,128)S(1)}, f32[5,32,256]{2,1,0:T(8,128)S(1)}) custom-call(f32[16,128,256]{2,1,0:T(8,128)S(1)} %copy-done.1, f32[2,128,256]{2,1,0:T(8,128)S(1)} %collective-permute-done.za_ref, f32[2,128,256]{2,1,0:T(8,128)S(1)} %collective-permute-done.1.zb_ref, ...), custom_call_target="tpu_custom_call" | custom-call | tf_op jit(solution)/shard_map/outer/pallas_call | solution.py:285
  22.2 4.0 %collective-permute-start.5 = (f32[5,32,256]{2,1,0:T(8,128)S(1)}, f32[5,32,256]{2,1,0:T(8,128)S(1)}, u32[]{:S(2)}, u32[]{:S(2)}) collective-permute-start(f32[5,32,256]{2,1,0:T(8,128)S(1)} %get-tuple-element.22), channel_id=1, source_target_pairs={{0,1},{1,0},{2,3},{3,2},{4,5},{5,4},{6,7},{7,6},{8,9},{9,8},{10,11... | collective-permute-start | bytes 491528 | tf_op jit(solution)/shard_map/ppermute | solution.py:298
  26.2 0.0 collective-permute-start.6
  26.2 1.5 %collective-permute-start.7 = (f32[5,32,256]{2,1,0:T(8,128)S(1)}, f32[5,32,256]{2,1,0:T(8,128)S(1)}, u32[]{:S(2)}, u32[]{:S(2)}) collective-permute-start(f32[5,32,256]{2,1,0:T(8,128)S(1)} %get-tuple-element.24), channel_id=1, source_target_pairs={{0,3},{1,2},{2,1},{3,0},{4,7},{5,6},{6,5},{7,4},{8,11},{9,10},{10,... | collective-permute-start | bytes 491528 | tf_op jit(solution)/shard_map/ppermute | solution.py:298
  27.8 2.7 %collective-permute-done.5.one_ref = f32[5,32,256]{2,1,0:T(8,128)S(1)} collective-permute-done((f32[5,32,256]{2,1,0:T(8,128)S(1)}, f32[5,32,256]{2,1,0:T(8,128)S(1)}, u32[]{:S(2)}, u32[]{:S(2)}) %collective-permute-start.5) | collective-permute-done | bytes 163872 | tf_op jit(solution)/shard_map/ppermute | solution.py:298
  30.5 4.0 %collective-permute-done.6.two_ref = f32[5,32,256]{2,1,0:T(8,128)S(1)} collective-permute-done((f32[5,32,256]{2,1,0:T(8,128)S(1)}, f32[5,32,256]{2,1,0:T(8,128)S(1)}, u32[]{:S(2)}, u32[]{:S(2)}) %collective-permute-start.6) | collective-permute-done | bytes 163872 | tf_op jit(solution)/shard_map/ppermute | solution.py:298
  34.5 0.0 collective-permute-done.7.three_ref
  34.5 0.7 %blend.1 = (f32[3,32,256]{2,1,0:T(8,128)}, f32[32,256]{1,0:T(8,128)}, f32[32,256]{1,0:T(8,128)}) custom-call(f32[5,32,256]{2,1,0:T(8,128)S(1)} %get-tuple-element.21.own_ref, f32[5,32,256]{2,1,0:T(8,128)S(1)} %collective-permute-done.5.one_ref, f32[5,32,256]{2,1,0:T(8,128)S(1)} %collective-permute-done.6.two_ref, ...), custom_call_target="tpu_custom_call" | custom-call | tf_op jit(solution)/shard_map/blend/pallas_call | solution.py:300
Async XLA Ops:
  0.6 1.6 %copy-start = (f32[16,128,256]{2,1,0:T(8,128)S(1)}, f32[16,128,256]{2,1,0:T(8,128)}, u32[]{:S(2)}) copy-start(f32[16,128,256]{2,1,0:T(8,128)} %x_ref.5) | copy-start | bytes 6291460
  2.2 14.5 %copy-start.1 = (f32[16,128,256]{2,1,0:T(8,128)S(1)}, f32[16,128,256]{2,1,0:T(8,128)}, u32[]{:S(2)}) copy-start(f32[16,128,256]{2,1,0:T(8,128)} %x_ref.5) | copy-start | bytes 6291460
  2.4 14.3 %collective-permute-start.4 = (f32[16,128,128]{2,1,0:T(8,128)S(1)}, f32[16,128,128]{2,1,0:T(8,128)S(1)}, u32[]{:S(2)}, u32[]{:S(2)}) collective-permute-start(f32[16,128,128]{2,1,0:T(8,128)S(1)} %get-tuple-element.18), channel_id=1, source_target_pairs={{0,16},{16,0},{1,17},{17,1},{2,18},{18,2},{3,19},{19,3},{4,20},{20... | collective-permute-start | bytes 3145736 | tf_op jit(solution)/shard_map/ppermute | solution.py:266
  2.9 18.5 %collective-permute-start = (f32[2,128,256]{2,1,0:T(8,128)S(1)}, f32[2,128,256]{2,1,0:T(8,128)S(1)}, u32[]{:S(2)}, u32[]{:S(2)}) collective-permute-start(f32[2,128,256]{2,1,0:T(8,128)S(1)} %get-tuple-element.14), channel_id=1, source_target_pairs={{0,1},{1,0},{2,3},{3,2},{4,5},{5,4},{6,7},{7,6},{8,9},{9,8},{10,11... | collective-permute-start | bytes 786440 | tf_op jit(solution)/shard_map/ppermute | solution.py:262
  5.5 15.9 %collective-permute-start.1 = (f32[2,128,256]{2,1,0:T(8,128)S(1)}, f32[2,128,256]{2,1,0:T(8,128)S(1)}, u32[]{:S(2)}, u32[]{:S(2)}) collective-permute-start(f32[2,128,256]{2,1,0:T(8,128)S(1)} %get-tuple-element.15), channel_id=1, source_target_pairs={{1,2},{2,1},{0,0},{3,3},{5,6},{6,5},{4,4},{7,7},{9,10},{10,9},{8,8... | collective-permute-start | bytes 786440 | tf_op jit(solution)/shard_map/ppermute | solution.py:263
  6.2 5.6 %collective-permute-start.2 = (f32[16,8,256]{2,1,0:T(8,128)S(1)}, f32[16,8,256]{2,1,0:T(8,128)S(1)}, u32[]{:S(2)}, u32[]{:S(2)}) collective-permute-start(f32[16,8,256]{2,1,0:T(8,128)S(1)} %get-tuple-element.16), channel_id=1, source_target_pairs={{0,4},{4,0},{8,12},{12,8},{1,5},{5,1},{9,13},{13,9},{2,6},{6,2},{1... | collective-permute-start | bytes 393224 | tf_op jit(solution)/shard_map/ppermute | solution.py:264
  7.8 8.9 %collective-permute-start.3 = (f32[16,8,256]{2,1,0:T(8,128)S(1)}, f32[16,8,256]{2,1,0:T(8,128)S(1)}, u32[]{:S(2)}, u32[]{:S(2)}) collective-permute-start(f32[16,8,256]{2,1,0:T(8,128)S(1)} %get-tuple-element.17), channel_id=1, source_target_pairs={{4,8},{8,4},{0,12},{12,0},{5,9},{9,5},{1,13},{13,1},{6,10},{10,6},... | collective-permute-start | bytes 393224 | tf_op jit(solution)/shard_map/ppermute | solution.py:265
  22.2 8.3 %collective-permute-start.5 = (f32[5,32,256]{2,1,0:T(8,128)S(1)}, f32[5,32,256]{2,1,0:T(8,128)S(1)}, u32[]{:S(2)}, u32[]{:S(2)}) collective-permute-start(f32[5,32,256]{2,1,0:T(8,128)S(1)} %get-tuple-element.22), channel_id=1, source_target_pairs={{0,1},{1,0},{2,3},{3,2},{4,5},{5,4},{6,7},{7,6},{8,9},{9,8},{10,11... | collective-permute-start | bytes 491528 | tf_op jit(solution)/shard_map/ppermute | solution.py:298
  26.2 8.2 %collective-permute-start.6 = (f32[5,32,256]{2,1,0:T(8,128)S(1)}, f32[5,32,256]{2,1,0:T(8,128)S(1)}, u32[]{:S(2)}, u32[]{:S(2)}) collective-permute-start(f32[5,32,256]{2,1,0:T(8,128)S(1)} %get-tuple-element.23), channel_id=1, source_target_pairs={{0,2},{1,3},{2,0},{3,1},{4,6},{5,7},{6,4},{7,5},{8,10},{9,11},{10,... | collective-permute-start | bytes 491528 | tf_op jit(solution)/shard_map/ppermute | solution.py:298
  26.2 8.2 %collective-permute-start.7 = (f32[5,32,256]{2,1,0:T(8,128)S(1)}, f32[5,32,256]{2,1,0:T(8,128)S(1)}, u32[]{:S(2)}, u32[]{:S(2)}) collective-permute-start(f32[5,32,256]{2,1,0:T(8,128)S(1)} %get-tuple-element.24), channel_id=1, source_target_pairs={{0,3},{1,2},{2,1},{3,0},{4,7},{5,6},{6,5},{7,4},{8,11},{9,10},{10,... | collective-permute-start | bytes 491528 | tf_op jit(solution)/shard_map/ppermute | solution.py:298

commit v3 on v2

--- a/solution.py
+++ b/solution.py
@@ -7,7 +7,7 @@
 from jax.experimental.pallas import tpu as pltpu
 from jax.sharding import PartitionSpec as P
 
-EDGE = 8
+HALO = 2
 
 
 def band(offset):
@@ -46,29 +46,25 @@
     cells_z, rows, cols = x_ref.shape
     at_x, at_y, at_z = place()
     strip = e_ref.shape[2]
-
-    def starts(position, low, high):
-        even = position % 2 == 0
-        return jnp.where(even, high, low), jnp.where(even, low, high)
-
-    z_one, z_two = starts(at_z, 0, cells_z - 2)
-    y_one, y_two = (pl.multiple_of(v, EDGE) for v in starts(at_y, 0, rows - EDGE))
+    even_z, even_y = at_z % 2 == 0, at_y % 2 == 0
+    high = cells_z - HALO
     x_one = pl.multiple_of(jnp.where(at_x == 0, cols - strip, 0), strip)
     copies = [
-        pltpu.make_async_copy(x_ref.at[pl.ds(z_one, 2)], za_ref, sems.at[0]),
-        pltpu.make_async_copy(x_ref.at[pl.ds(z_two, 2)], zb_ref, sems.at[1]),
-        pltpu.make_async_copy(x_ref.at[:, pl.ds(y_one, EDGE)], ya_ref, sems.at[2]),
-        pltpu.make_async_copy(x_ref.at[:, pl.ds(y_two, EDGE)], yb_ref, sems.at[3]),
-        pltpu.make_async_copy(x_ref.at[:, :, pl.ds(x_one, strip)], e_ref, sems.at[4]),
+        pltpu.make_async_copy(x_ref.at[pl.ds(jnp.where(even_z, high, 0), HALO)], za_ref, sems.at[0]),
+        pltpu.make_async_copy(x_ref.at[pl.ds(jnp.where(even_z, 0, high), HALO)], zb_ref, sems.at[1]),
+        pltpu.make_async_copy(x_ref.at[:, :, pl.ds(x_one, strip)], e_ref, sems.at[2]),
     ]
     for copy in copies:
         copy.start()
+    top, bottom = x_ref[:, :HALO, :], x_ref[:, rows - HALO :, :]
+    ya_ref[...] = jnp.where(even_y, bottom, top)
+    yb_ref[...] = jnp.where(even_y, top, bottom)
     for copy in copies:
         copy.wait()
 
 
 def inner_kernel(
-    x_ref, ya_ref, yb_ref, e_ref, image_ref, part_ref, gx0, gx1, gy0, gy1, wx_ref, wy_ref, *, total_z, last_y
+    x_ref, ya_ref, yb_ref, e_ref, image_ref, part_ref, gx0, gx1, gy0, gy1, wx_ref, wy_ref, rim_ref, *, total_z, last_y
 ):
     cells_z, rows, cols = x_ref.shape
     strip = e_ref.shape[2]
@@ -80,20 +76,26 @@
     lane = iota((strip, cols), 0) - iota((strip, cols), 1)
     beyond_x = band(lane + jnp.where(at_x == 0, cols, -strip))
     along_y = band(iota((rows, rows), 1) - iota((rows, rows), 0))
-    out_row, slot = iota((rows, 2 * EDGE), 0), iota((rows, 2 * EDGE), 1)
-    first = slot < EDGE
-    cell = slot % EDGE
-    below = jnp.where(first, even.astype(jnp.int32), 1 - even.astype(jnp.int32)) > 0
-    top = jnp.where(at_y > 0, -EDGE, -4 * EDGE)
-    bottom = jnp.where(at_y < last_y, rows, rows + 4 * EDGE)
-    beyond_y = band(cell + jnp.where(below, bottom, top) - out_row)
+    out_row, slot = iota((rows, 4 * HALO), 0), iota((rows, 4 * HALO), 1)
+    none = rows * 4
+    top = jnp.where(at_y > 0, -HALO, none)
+    bottom = jnp.where(at_y < last_y, rows, none)
+    offset = jnp.where(
+        slot < HALO,
+        slot + jnp.where(even, bottom, top),
+        slot - HALO + jnp.where(even, top, bottom),
+    )
+    beyond_y = band(jnp.where(slot < 2 * HALO, offset, none) - out_row)
+    rim_ref[:, :HALO, :] = ya_ref[...]
+    rim_ref[:, HALO : 2 * HALO, :] = yb_ref[...]
+    rim_ref[:, 2 * HALO :, :] = jnp.zeros((cells_z, 2 * HALO, cols), jnp.float32)
     wx_ref[...] = jnp.concatenate([along_x, along_x, beyond_x, beyond_x], axis=0)
     wy_ref[...] = jnp.concatenate([along_y, along_y, beyond_y, beyond_y], axis=1)
 
     def gradients(k, gx_ref, gy_ref):
         high, low = split(x_ref[k])
         edge_high, edge_low = split(e_ref[k])
-        rim_high, rim_low = split(jnp.concatenate([ya_ref[k], yb_ref[k]], axis=0))
+        rim_high, rim_low = split(rim_ref[k])
         gx_ref[...] = dot(jnp.concatenate([high, low, edge_high, edge_low], axis=1), wx_ref[...])
         gy_ref[...] = dot(wy_ref[...], jnp.concatenate([high, low, rim_high, rim_low], axis=0))
 
@@ -247,13 +249,13 @@
     edges = pl.pallas_call(
         edges_kernel,
         out_shape=(
-            shaped(2, rows, cols), shaped(2, rows, cols),
-            shaped(cells_z, EDGE, cols), shaped(cells_z, EDGE, cols),
+            shaped(HALO, rows, cols), shaped(HALO, rows, cols),
+            shaped(cells_z, HALO, cols), shaped(cells_z, HALO, cols),
             shaped(cells_z, rows, strip),
         ),
-        in_specs=[pl.BlockSpec(memory_space=pltpu.HBM)],
+        in_specs=[vmem],
         out_specs=(vmem,) * 5,
-        scratch_shapes=[pltpu.SemaphoreType.DMA((5,))],
+        scratch_shapes=[pltpu.SemaphoreType.DMA((3,))],
         compiler_params=pltpu.CompilerParams(vmem_limit_bytes=4 * 1024 * 1024),
         name="edges",
     )(block)
@@ -273,7 +275,8 @@
         scratch_shapes=[pltpu.VMEM((rows, cols), f32)] * 4
         + [
             pltpu.VMEM((2 * (cols + strip), cols), jnp.bfloat16),
-            pltpu.VMEM((rows, 2 * (rows + 2 * EDGE)), jnp.bfloat16),
+            pltpu.VMEM((rows, 2 * (rows + 4 * HALO)), jnp.bfloat16),
+            pltpu.VMEM((cells_z, 4 * HALO, cols), f32),
         ],
         compiler_params=pltpu.CompilerParams(vmem_limit_bytes=16 * 1024 * 1024),
         cost_estimate=pl.CostEstimate(

time: 35.4 us -> 32.3 us (0.912)
  waiting for transfers between devices: 13.2 us -> 9.83 us
    ppermute x1, waiting for transfers between devices: 4.94 us -> 3.23 us  [on_device(): yb = lax.ppermute(edges[3], 'gy', y_second)]
    ppermute x1, waiting for transfers between devices: 1.52 us -> 0.01 us  [on_device(): ya = lax.ppermute(edges[2], 'gy', y_first)]
  transfers between devices with their start and end apart: 8 -> 8, of which waited for: 4 -> 3; matrix products, arithmetic and copies ran while one was open for 0% -> 0% of each run, Pallas kernels for 13% -> 15%
where the time goes in v3:
time: 32.3 us; the launch traced here: 32.1 us
  starting transfers between devices  13.7 us (42%)
  waiting for transfers between devices  9.83 us (30%)
  Pallas kernels  6.36 us (20%)
  local copies, waits for them, and re-layouts  1.59 us (5%)
  between operations  0.69 us (2%)
    ppermute x3, waiting for transfers between devices, on_device(): lax.ppermute(parts[s], 'gz', [(i, i ^ s) for i in range(count_z)])  6.59 us
    ppermute x3, starting transfers between devices, on_device(): lax.ppermute(parts[s], 'gz', [(i, i ^ s) for i in range(count_z)])  5.82 us
    pallas_call x1, Pallas kernels, on_device(): pl.pallas_call(functools.partial(inner_kernel, total_z=total_z, last_y=co...  4.67 us
    ppermute x1, waiting for transfers between devices, on_device(): yb = lax.ppermute(edges[3], 'gy', y_second)  3.23 us
    ppermute x1, starting transfers between devices, on_device(): za = lax.ppermute(edges[0], 'gz', z_first)  2.56 us
    ppermute x1, starting transfers between devices, on_device(): yb = lax.ppermute(edges[3], 'gy', y_second)  2.47 us
    ppermute x1, starting transfers between devices, on_device(): ya = lax.ppermute(edges[2], 'gy', y_first)  1.64 us
    unnamed x4, local copies, waits for them, and re-layouts  1.59 us
  transfers between devices with their start and end apart: 8, of which 3 were waited for; matrix products, arithmetic and copies ran while one was open for 0% of the time, Pallas kernels for 15%

profile of v3, /device:TPU:0, one launch (start us, length us, event | category | flops | bytes accessed | tf_op | source)
XLA Modules:
  0.0 32.1 jit_solution(16794843370714232443)
XLA Ops:
  0.6 0.0 copy-start
  0.6 1.6 %copy-done = f32[16,128,256]{2,1,0:T(8,128)S(1)} copy-done((f32[16,128,256]{2,1,0:T(8,128)S(1)}, f32[16,128,256]{2,1,0:T(8,128)}, u32[]{:S(2)}) %copy-start) | copy-done | bytes 2097176
  2.2 0.0 copy-start.1
  2.2 0.2 edges.1
  2.4 0.5 %collective-permute-start.4 = (f32[16,128,128]{2,1,0:T(8,128)S(1)}, f32[16,128,128]{2,1,0:T(8,128)S(1)}, u32[]{:S(2)}, u32[]{:S(2)}) collective-permute-start(f32[16,128,128]{2,1,0:T(8,128)S(1)} %get-tuple-element.18), channel_id=1, source_target_pairs={{0,16},{16,0},{1,17},{17,1},{2,18},{18,2},{3,19},{19,3},{4,20},{20... | collective-permute-start | bytes 3145736 | tf_op jit(solution)/shard_map/ppermute | solution.py:268
  2.9 2.6 %collective-permute-start = (f32[2,128,256]{2,1,0:T(8,128)S(1)}, f32[2,128,256]{2,1,0:T(8,128)S(1)}, u32[]{:S(2)}, u32[]{:S(2)}) collective-permute-start(f32[2,128,256]{2,1,0:T(8,128)S(1)} %get-tuple-element.14), channel_id=1, source_target_pairs={{0,1},{1,0},{2,3},{3,2},{4,5},{5,4},{6,7},{7,6},{8,9},{9,8},{10,11... | collective-permute-start | bytes 786440 | tf_op jit(solution)/shard_map/ppermute | solution.py:264
  5.5 0.7 %collective-permute-start.1 = (f32[2,128,256]{2,1,0:T(8,128)S(1)}, f32[2,128,256]{2,1,0:T(8,128)S(1)}, u32[]{:S(2)}, u32[]{:S(2)}) collective-permute-start(f32[2,128,256]{2,1,0:T(8,128)S(1)} %get-tuple-element.15), channel_id=1, source_target_pairs={{1,2},{2,1},{0,0},{3,3},{5,6},{6,5},{4,4},{7,7},{9,10},{10,9},{8,8... | collective-permute-start | bytes 786440 | tf_op jit(solution)/shard_map/ppermute | solution.py:265
  6.2 1.6 %collective-permute-start.2 = (f32[16,2,256]{2,1,0:T(2,128)S(1)}, f32[16,2,256]{2,1,0:T(2,128)S(1)}, u32[]{:S(2)}, u32[]{:S(2)}) collective-permute-start(f32[16,2,256]{2,1,0:T(2,128)S(1)} %get-tuple-element.16), channel_id=1, source_target_pairs={{0,4},{4,0},{8,12},{12,8},{1,5},{5,1},{9,13},{13,9},{2,6},{6,2},{1... | collective-permute-start | bytes 98312 | tf_op jit(solution)/shard_map/ppermute | solution.py:266
  7.8 2.5 %collective-permute-start.3 = (f32[16,2,256]{2,1,0:T(2,128)S(1)}, f32[16,2,256]{2,1,0:T(2,128)S(1)}, u32[]{:S(2)}, u32[]{:S(2)}) collective-permute-start(f32[16,2,256]{2,1,0:T(2,128)S(1)} %get-tuple-element.17), channel_id=1, source_target_pairs={{4,8},{8,4},{0,12},{12,0},{5,9},{9,5},{1,13},{13,1},{6,10},{10,6},... | collective-permute-start | bytes 98312 | tf_op jit(solution)/shard_map/ppermute | solution.py:267
  10.3 0.0 collective-permute-done.2.ya_ref
  10.3 3.2 %collective-permute-done.3.yb_ref = f32[16,2,256]{2,1,0:T(2,128)S(1)} collective-permute-done((f32[16,2,256]{2,1,0:T(2,128)S(1)}, f32[16,2,256]{2,1,0:T(2,128)S(1)}, u32[]{:S(2)}, u32[]{:S(2)}) %collective-permute-start.3) | collective-permute-done | bytes 32800 | tf_op jit(solution)/shard_map/ppermute | solution.py:267
  13.5 0.0 collective-permute-done.4.e_ref
  13.5 0.0 copy-done.1
  13.5 4.7 %inner.1 = (f32[5,128,256]{2,1,0:T(8,128)S(1)}, f32[4,2,128,256]{3,2,1,0:T(8,128)S(1)}) custom-call(f32[16,128,256]{2,1,0:T(8,128)S(1)} %copy-done.1, f32[16,2,256]{2,1,0:T(2,128)S(1)} %collective-permute-done.2.ya_ref, f32[16,2,256]{2,1,0:T(2,128)S(1)} %collective-permute-done.3.yb_ref, f32[16,128,128]{2,1,0:T(8,128)S(1)} %collective-permute-done.4.e_ref), custom_call_target="tpu_custom_call" | custom-call | flops 52428800 | bytes 4194304 | tf_op jit(solution)/shard_map/inner/pallas_call | solution.py:270
  18.2 0.0 collective-permute-done.za_ref
  18.2 0.0 collective-permute-done.1.zb_ref
  18.2 0.8 %outer.1 = (f32[5,32,256]{2,1,0:T(8,128)S(1)}, f32[5,32,256]{2,1,0:T(8,128)S(1)}, f32[5,32,256]{2,1,0:T(8,128)S(1)}, f32[5,32,256]{2,1,0:T(8,128)S(1)}) custom-call(f32[16,128,256]{2,1,0:T(8,128)S(1)} %copy-done.1, f32[2,128,256]{2,1,0:T(8,128)S(1)} %collective-permute-done.za_ref, f32[2,128,256]{2,1,0:T(8,128)S(1)} %collective-permute-done.1.zb_ref, ...), custom_call_target="tpu_custom_call" | custom-call | tf_op jit(solution)/shard_map/outer/pallas_call | solution.py:288
  19.0 4.3 %collective-permute-start.5 = (f32[5,32,256]{2,1,0:T(8,128)S(1)}, f32[5,32,256]{2,1,0:T(8,128)S(1)}, u32[]{:S(2)}, u32[]{:S(2)}) collective-permute-start(f32[5,32,256]{2,1,0:T(8,128)S(1)} %get-tuple-element.22), channel_id=1, source_target_pairs={{0,1},{1,0},{2,3},{3,2},{4,5},{5,4},{6,7},{7,6},{8,9},{9,8},{10,11... | collective-permute-start | bytes 491528 | tf_op jit(solution)/shard_map/ppermute | solution.py:301
  23.3 0.0 collective-permute-start.6
  23.3 1.5 %collective-permute-start.7 = (f32[5,32,256]{2,1,0:T(8,128)S(1)}, f32[5,32,256]{2,1,0:T(8,128)S(1)}, u32[]{:S(2)}, u32[]{:S(2)}) collective-permute-start(f32[5,32,256]{2,1,0:T(8,128)S(1)} %get-tuple-element.24), channel_id=1, source_target_pairs={{0,3},{1,2},{2,1},{3,0},{4,7},{5,6},{6,5},{7,4},{8,11},{9,10},{10,... | collective-permute-start | bytes 491528 | tf_op jit(solution)/shard_map/ppermute | solution.py:301
  24.8 2.8 %collective-permute-done.5.one_ref = f32[5,32,256]{2,1,0:T(8,128)S(1)} collective-permute-done((f32[5,32,256]{2,1,0:T(8,128)S(1)}, f32[5,32,256]{2,1,0:T(8,128)S(1)}, u32[]{:S(2)}, u32[]{:S(2)}) %collective-permute-start.5) | collective-permute-done | bytes 163872 | tf_op jit(solution)/shard_map/ppermute | solution.py:301
  27.6 3.8 %collective-permute-done.6.two_ref = f32[5,32,256]{2,1,0:T(8,128)S(1)} collective-permute-done((f32[5,32,256]{2,1,0:T(8,128)S(1)}, f32[5,32,256]{2,1,0:T(8,128)S(1)}, u32[]{:S(2)}, u32[]{:S(2)}) %collective-permute-start.6) | collective-permute-done | bytes 163872 | tf_op jit(solution)/shard_map/ppermute | solution.py:301
  31.4 0.0 collective-permute-done.7.three_ref
  31.4 0.7 %blend.1 = (f32[3,32,256]{2,1,0:T(8,128)}, f32[32,256]{1,0:T(8,128)}, f32[32,256]{1,0:T(8,128)}) custom-call(f32[5,32,256]{2,1,0:T(8,128)S(1)} %get-tuple-element.21.own_ref, f32[5,32,256]{2,1,0:T(8,128)S(1)} %collective-permute-done.5.one_ref, f32[5,32,256]{2,1,0:T(8,128)S(1)} %collective-permute-done.6.two_ref, ...), custom_call_target="tpu_custom_call" | custom-call | tf_op jit(solution)/shard_map/blend/pallas_call | solution.py:303
Async XLA Ops:
  0.6 1.6 %copy-start = (f32[16,128,256]{2,1,0:T(8,128)S(1)}, f32[16,128,256]{2,1,0:T(8,128)}, u32[]{:S(2)}) copy-start(f32[16,128,256]{2,1,0:T(8,128)} %x_ref.5) | copy-start | bytes 6291460
  2.2 11.3 %copy-start.1 = (f32[16,128,256]{2,1,0:T(8,128)S(1)}, f32[16,128,256]{2,1,0:T(8,128)}, u32[]{:S(2)}) copy-start(f32[16,128,256]{2,1,0:T(8,128)} %x_ref.5) | copy-start | bytes 6291460
  2.4 11.1 %collective-permute-start.4 = (f32[16,128,128]{2,1,0:T(8,128)S(1)}, f32[16,128,128]{2,1,0:T(8,128)S(1)}, u32[]{:S(2)}, u32[]{:S(2)}) collective-permute-start(f32[16,128,128]{2,1,0:T(8,128)S(1)} %get-tuple-element.18), channel_id=1, source_target_pairs={{0,16},{16,0},{1,17},{17,1},{2,18},{18,2},{3,19},{19,3},{4,20},{20... | collective-permute-start | bytes 3145736 | tf_op jit(solution)/shard_map/ppermute | solution.py:268
  2.9 15.3 %collective-permute-start = (f32[2,128,256]{2,1,0:T(8,128)S(1)}, f32[2,128,256]{2,1,0:T(8,128)S(1)}, u32[]{:S(2)}, u32[]{:S(2)}) collective-permute-start(f32[2,128,256]{2,1,0:T(8,128)S(1)} %get-tuple-element.14), channel_id=1, source_target_pairs={{0,1},{1,0},{2,3},{3,2},{4,5},{5,4},{6,7},{7,6},{8,9},{9,8},{10,11... | collective-permute-start | bytes 786440 | tf_op jit(solution)/shard_map/ppermute | solution.py:264
  5.5 12.7 %collective-permute-start.1 = (f32[2,128,256]{2,1,0:T(8,128)S(1)}, f32[2,128,256]{2,1,0:T(8,128)S(1)}, u32[]{:S(2)}, u32[]{:S(2)}) collective-permute-start(f32[2,128,256]{2,1,0:T(8,128)S(1)} %get-tuple-element.15), channel_id=1, source_target_pairs={{1,2},{2,1},{0,0},{3,3},{5,6},{6,5},{4,4},{7,7},{9,10},{10,9},{8,8... | collective-permute-start | bytes 786440 | tf_op jit(solution)/shard_map/ppermute | solution.py:265
  6.2 4.1 %collective-permute-start.2 = (f32[16,2,256]{2,1,0:T(2,128)S(1)}, f32[16,2,256]{2,1,0:T(2,128)S(1)}, u32[]{:S(2)}, u32[]{:S(2)}) collective-permute-start(f32[16,2,256]{2,1,0:T(2,128)S(1)} %get-tuple-element.16), channel_id=1, source_target_pairs={{0,4},{4,0},{8,12},{12,8},{1,5},{5,1},{9,13},{13,9},{2,6},{6,2},{1... | collective-permute-start | bytes 98312 | tf_op jit(solution)/shard_map/ppermute | solution.py:266
  7.8 5.7 %collective-permute-start.3 = (f32[16,2,256]{2,1,0:T(2,128)S(1)}, f32[16,2,256]{2,1,0:T(2,128)S(1)}, u32[]{:S(2)}, u32[]{:S(2)}) collective-permute-start(f32[16,2,256]{2,1,0:T(2,128)S(1)} %get-tuple-element.17), channel_id=1, source_target_pairs={{4,8},{8,4},{0,12},{12,0},{5,9},{9,5},{1,13},{13,1},{6,10},{10,6},... | collective-permute-start | bytes 98312 | tf_op jit(solution)/shard_map/ppermute | solution.py:267
  19.0 8.6 %collective-permute-start.5 = (f32[5,32,256]{2,1,0:T(8,128)S(1)}, f32[5,32,256]{2,1,0:T(8,128)S(1)}, u32[]{:S(2)}, u32[]{:S(2)}) collective-permute-start(f32[5,32,256]{2,1,0:T(8,128)S(1)} %get-tuple-element.22), channel_id=1, source_target_pairs={{0,1},{1,0},{2,3},{3,2},{4,5},{5,4},{6,7},{7,6},{8,9},{9,8},{10,11... | collective-permute-start | bytes 491528 | tf_op jit(solution)/shard_map/ppermute | solution.py:301
  23.3 8.1 %collective-permute-start.6 = (f32[5,32,256]{2,1,0:T(8,128)S(1)}, f32[5,32,256]{2,1,0:T(8,128)S(1)}, u32[]{:S(2)}, u32[]{:S(2)}) collective-permute-start(f32[5,32,256]{2,1,0:T(8,128)S(1)} %get-tuple-element.23), channel_id=1, source_target_pairs={{0,2},{1,3},{2,0},{3,1},{4,6},{5,7},{6,4},{7,5},{8,10},{9,11},{10,... | collective-permute-start | bytes 491528 | tf_op jit(solution)/shard_map/ppermute | solution.py:301
  23.3 8.1 %collective-permute-start.7 = (f32[5,32,256]{2,1,0:T(8,128)S(1)}, f32[5,32,256]{2,1,0:T(8,128)S(1)}, u32[]{:S(2)}, u32[]{:S(2)}) collective-permute-start(f32[5,32,256]{2,1,0:T(8,128)S(1)} %get-tuple-element.24), channel_id=1, source_target_pairs={{0,3},{1,2},{2,1},{3,0},{4,7},{5,6},{6,5},{7,4},{8,11},{9,10},{10,... | collective-permute-start | bytes 491528 | tf_op jit(solution)/shard_map/ppermute | solution.py:301

commit v4 on v3

--- a/solution.py
+++ b/solution.py
@@ -8,6 +8,7 @@
 from jax.sharding import PartitionSpec as P
 
 HALO = 2
+RIM = 8
 
 
 def band(offset):
@@ -42,83 +43,82 @@
     return tuple(lax.axis_index(a) for a in ("gx", "gy", "gz"))
 
 
-def edges_kernel(x_ref, za_ref, zb_ref, ya_ref, yb_ref, e_ref, sems):
+def edges_kernel(x_ref, za_ref, zb_ref, ya_ref, yb_ref, e_ref, top_ref, bottom_ref, sems):
     cells_z, rows, cols = x_ref.shape
     at_x, at_y, at_z = place()
     strip = e_ref.shape[2]
     even_z, even_y = at_z % 2 == 0, at_y % 2 == 0
     high = cells_z - HALO
-    x_one = pl.multiple_of(jnp.where(at_x == 0, cols - strip, 0), strip)
+    start = pl.multiple_of(jnp.where(at_x == 0, cols - strip, 0), strip)
     copies = [
-        pltpu.make_async_copy(x_ref.at[pl.ds(jnp.where(even_z, high, 0), HALO)], za_ref, sems.at[0]),
-        pltpu.make_async_copy(x_ref.at[pl.ds(jnp.where(even_z, 0, high), HALO)], zb_ref, sems.at[1]),
-        pltpu.make_async_copy(x_ref.at[:, :, pl.ds(x_one, strip)], e_ref, sems.at[2]),
+        pltpu.make_async_copy(source, target, sems.at[i])
+        for i, (source, target) in enumerate(
+            (
+                (x_ref.at[pl.ds(jnp.where(even_z, high, 0), HALO)], za_ref),
+                (x_ref.at[pl.ds(jnp.where(even_z, 0, high), HALO)], zb_ref),
+                (x_ref.at[:, pl.ds(0, RIM)], top_ref),
+                (x_ref.at[:, pl.ds(rows - RIM, RIM)], bottom_ref),
+                (x_ref.at[:, :, pl.ds(start, strip)], e_ref),
+            )
+        )
     ]
     for copy in copies:
         copy.start()
-    top, bottom = x_ref[:, :HALO, :], x_ref[:, rows - HALO :, :]
+    for copy in copies:
+        copy.wait()
+    top, bottom = top_ref[:, :HALO, :], bottom_ref[:, RIM - HALO :, :]
     ya_ref[...] = jnp.where(even_y, bottom, top)
     yb_ref[...] = jnp.where(even_y, top, bottom)
-    for copy in copies:
-        copy.wait()
+
+
+def pair(grad_x, grad_y):
+    base = 1.0 + (grad_x * grad_x + grad_y * grad_y) * (1.0 / 144.0)
+    lin = grad_x * (0.48 * 0.7 / 12.0) + grad_y * (0.6 * 0.7 / 12.0)
+    return base, lin
 
 
 def inner_kernel(
-    x_ref, ya_ref, yb_ref, e_ref, image_ref, part_ref, gx0, gx1, gy0, gy1, wx_ref, wy_ref, rim_ref, *, total_z, last_y
+    x_ref, e_ref, image_ref, part_ref, rim_ref, gx0, gx1, gy0, gy1, wx_ref, wy_ref, *, total_z
 ):
     cells_z, rows, cols = x_ref.shape
     strip = e_ref.shape[2]
     depth_step = 2.0 / total_z
-    at_x, at_y, at_z = place()
-    even = at_y % 2 == 0
+    at_x, _, at_z = place()
     iota = functools.partial(lax.broadcasted_iota, jnp.int32)
     along_x = band(iota((cols, cols), 0) - iota((cols, cols), 1))
     lane = iota((strip, cols), 0) - iota((strip, cols), 1)
     beyond_x = band(lane + jnp.where(at_x == 0, cols, -strip))
     along_y = band(iota((rows, rows), 1) - iota((rows, rows), 0))
-    out_row, slot = iota((rows, 4 * HALO), 0), iota((rows, 4 * HALO), 1)
-    none = rows * 4
-    top = jnp.where(at_y > 0, -HALO, none)
-    bottom = jnp.where(at_y < last_y, rows, none)
-    offset = jnp.where(
-        slot < HALO,
-        slot + jnp.where(even, bottom, top),
-        slot - HALO + jnp.where(even, top, bottom),
-    )
-    beyond_y = band(jnp.where(slot < 2 * HALO, offset, none) - out_row)
-    rim_ref[:, :HALO, :] = ya_ref[...]
-    rim_ref[:, HALO : 2 * HALO, :] = yb_ref[...]
-    rim_ref[:, 2 * HALO :, :] = jnp.zeros((cells_z, 2 * HALO, cols), jnp.float32)
     wx_ref[...] = jnp.concatenate([along_x, along_x, beyond_x, beyond_x], axis=0)
-    wy_ref[...] = jnp.concatenate([along_y, along_y, beyond_y, beyond_y], axis=1)
-
-    def gradients(k, gx_ref, gy_ref):
+    wy_ref[...] = jnp.concatenate([along_y, along_y], axis=1)
+
+    chunk = 16
+    spans = [pl.ds(r, chunk) for r in range(RIM, rows - RIM, chunk)]
+    slots = ((gx0, gy0), (gx1, gy1))
+
+    def gradients(k, slot):
         high, low = split(x_ref[k])
         edge_high, edge_low = split(e_ref[k])
-        rim_high, rim_low = split(rim_ref[k])
-        gx_ref[...] = dot(jnp.concatenate([high, low, edge_high, edge_low], axis=1), wx_ref[...])
-        gy_ref[...] = dot(wy_ref[...], jnp.concatenate([high, low, rim_high, rim_low], axis=0))
-
-    def pair(at, gx_ref, gy_ref):
-        grad_x, grad_y = gx_ref[at], gy_ref[at]
-        base = 1.0 + (grad_x * grad_x + grad_y * grad_y) * (1.0 / 144.0)
-        lin = grad_x * (0.48 * 0.7 / 12.0) + grad_y * (0.6 * 0.7 / 12.0)
-        return base, lin
-
-    chunk = 16
-    spans = [pl.ds(r, chunk) for r in range(0, rows, chunk)]
-    slots = ((gx0, gy0), (gx1, gy1))
-
-    def keep(index, pairs):
+        for axis, value in enumerate(
+            (
+                dot(jnp.concatenate([high, low, edge_high, edge_low], axis=1), wx_ref[...]),
+                dot(wy_ref[...], jnp.concatenate([high, low], axis=0)),
+            )
+        ):
+            slots[slot][axis][...] = value
+            rim_ref[k, axis, :RIM] = value[:RIM]
+            rim_ref[k, axis, RIM:] = value[rows - RIM :]
+
+    def keep(index, slot):
+        grad_x, grad_y = slots[slot]
         for at in spans:
-            base, lin = pair(at, *pairs)
-            part_ref[index, 0, at] = base
-            part_ref[index, 1, at] = lin
-
-    def shade(k, pairs):
+            part_ref[index, 0, at], part_ref[index, 1, at] = pair(grad_x[at], grad_y[at])
+
+    def shade(k, slot):
+        grad_x, grad_y = slots[slot]
         position = ((at_z * cells_z + k).astype(jnp.float32) + 0.5) / total_z
         for at in spans:
-            base, lin = pair(at, *pairs)
+            base, lin = pair(grad_x[at], grad_y[at])
             grad_z = (x_ref[k - 2, at] - x_ref[k + 2, at]) + 8.0 * (x_ref[k + 1, at] - x_ref[k - 1, at])
             through, adds = emit(x_ref[k, at], base, lin, grad_z, depth_step, image_ref[4, at], position)
             image_ref[4, at] = through
@@ -129,23 +129,65 @@
         image_ref[channel] = jnp.zeros((rows, cols), jnp.float32)
     image_ref[4] = jnp.ones((rows, cols), jnp.float32)
 
-    gradients(0, *slots[0])
-    gradients(1, *slots[1])
-    keep(0, slots[0])
-    gradients(2, *slots[0])
-    keep(1, slots[1])
+    gradients(0, 0)
+    gradients(1, 1)
+    keep(0, 0)
+    gradients(2, 0)
+    keep(1, 1)
 
     @pl.loop(0, (cells_z - 4) // 2)
     def _(step):
         k = 2 + 2 * step
-        gradients(k + 1, *slots[1])
-        shade(k, slots[0])
-        gradients(k + 2, *slots[0])
-        shade(k + 1, slots[1])
-
-    gradients(cells_z - 1, *slots[1])
-    keep(2, slots[0])
-    keep(3, slots[1])
+        gradients(k + 1, 1)
+        shade(k, 0)
+        gradients(k + 2, 0)
+        shade(k + 1, 1)
+
+    gradients(cells_z - 1, 1)
+    keep(2, 0)
+    keep(3, 1)
+
+
+def rim_kernel(x_ref, ya_ref, yb_ref, rim_ref, image_in, part_in, image_ref, part_ref, *, total_z, last_y):
+    del image_in, part_in
+    cells_z, rows, cols = x_ref.shape
+    depth_step = 2.0 / total_z
+    _, at_y, at_z = place()
+    even = at_y % 2 == 0
+    row = lax.broadcasted_iota(jnp.int32, (RIM, cols), 0)
+    zero = jnp.zeros((RIM, cols), jnp.float32)
+
+    def weights(position, there):
+        offset = position - row
+        one = jnp.where(offset == 1, 8.0, jnp.where(offset == -1, -8.0, 0.0))
+        two = jnp.where(offset == 2, -1.0, jnp.where(offset == -2, 1.0, 0.0))
+        return jnp.where(there, one + two, zero)
+
+    sides = (
+        (0, 0, even, [weights(-HALO + i, at_y > 0) for i in range(HALO)]),
+        (RIM, rows - RIM, ~even, [weights(RIM + i, at_y < last_y) for i in range(HALO)]),
+    )
+    for start, first_row, second, scale in sides:
+        at, to = pl.ds(start, RIM), pl.ds(first_row, RIM)
+
+        def planes(k):
+            grad_y = rim_ref[k, 1, at]
+            for i in range(HALO):
+                cell = jnp.where(second, yb_ref[k, i : i + 1], ya_ref[k, i : i + 1])
+                grad_y = grad_y + scale[i] * jnp.broadcast_to(cell, (RIM, cols))
+            return pair(rim_ref[k, 0, at], grad_y)
+
+        for index, k in enumerate((0, 1, cells_z - 2, cells_z - 1)):
+            part_ref[index, 0, to], part_ref[index, 1, to] = planes(k)
+        through, sums = zero + 1.0, [zero] * 4
+        for k in range(2, cells_z - 2):
+            position = ((at_z * cells_z + k).astype(jnp.float32) + 0.5) / total_z
+            grad_z = (x_ref[k - 2, to] - x_ref[k + 2, to]) + 8.0 * (x_ref[k + 1, to] - x_ref[k - 1, to])
+            base, lin = planes(k)
+            through, adds = emit(x_ref[k, to], base, lin, grad_z, depth_step, through, position)
+            sums = [s + a for s, a in zip(sums, adds)]
+        for channel, value in enumerate(sums + [through]):
+            image_ref[channel, to] = value
 
 
 def outer_kernel(x_ref, za_ref, zb_ref, image_ref, part_ref, *out_refs, total_z):
@@ -246,6 +288,9 @@
         return jax.ShapeDtypeStruct(shape, f32)
 
     vmem = pl.BlockSpec(memory_space=pltpu.VMEM)
+    def limit(mebibytes):
+        return pltpu.CompilerParams(vmem_limit_bytes=mebibytes * 1024 * 1024)
+
     edges = pl.pallas_call(
         edges_kernel,
         out_shape=(
@@ -253,13 +298,13 @@
             shaped(cells_z, HALO, cols), shaped(cells_z, HALO, cols),
             shaped(cells_z, rows, strip),
         ),
-        in_specs=[vmem],
+        in_specs=[pl.BlockSpec(memory_space=pltpu.HBM)],
         out_specs=(vmem,) * 5,
-        scratch_shapes=[pltpu.SemaphoreType.DMA((3,))],
-        compiler_params=pltpu.CompilerParams(vmem_limit_bytes=4 * 1024 * 1024),
+        scratch_shapes=[pltpu.VMEM((cells_z, RIM, cols), f32)] * 2 + [pltpu.SemaphoreType.DMA((5,))],
+        compiler_params=limit(4),
         name="edges",
-    )(block)
-    z_first, z_second = pairs(count_z, False)
+    )(pltpu.with_memory_space_constraint(block, pltpu.HBM))
+    z_first, z_second = pairs(count_z, True)
     y_first, y_second = pairs(count_y, True)
     za = lax.ppermute(edges[0], "gz", z_first)
     zb = lax.ppermute(edges[1], "gz", z_second)
@@ -267,35 +312,47 @@
     yb = lax.ppermute(edges[3], "gy", y_second)
     edge = lax.ppermute(edges[4], "gx", [(0, 1), (1, 0)])
 
-    image, part = pl.pallas_call(
-        functools.partial(inner_kernel, total_z=total_z, last_y=count_y - 1),
-        out_shape=(shaped(5, rows, cols), shaped(4, 2, rows, cols)),
-        in_specs=[vmem] * 4,
-        out_specs=(vmem, vmem),
+    image_shape, part_shape = shaped(5, rows, cols), shaped(4, 2, rows, cols)
+    image, part, rim = pl.pallas_call(
+        functools.partial(inner_kernel, total_z=total_z),
+        out_shape=(image_shape, part_shape, shaped(cells_z, 2, 2 * RIM, cols)),
+        in_specs=[vmem] * 2,
+        out_specs=(vmem,) * 3,
         scratch_shapes=[pltpu.VMEM((rows, cols), f32)] * 4
         + [
             pltpu.VMEM((2 * (cols + strip), cols), jnp.bfloat16),
-            pltpu.VMEM((rows, 2 * (rows + 4 * HALO)), jnp.bfloat16),
-            pltpu.VMEM((cells_z, 4 * HALO, cols), f32),
+            pltpu.VMEM((rows, 2 * rows), jnp.bfloat16),
         ],
-        compiler_params=pltpu.CompilerParams(vmem_limit_bytes=16 * 1024 * 1024),
+        compiler_params=limit(16),
         cost_estimate=pl.CostEstimate(
             flops=100 * block.size, bytes_accessed=8 * block.size, transcendentals=6 * block.size
         ),
         name="inner",
-    )(block, ya, yb, edge)
+    )(block, edge)
+    image, part = pl.pallas_call(
+        functools.partial(rim_kernel, total_z=total_z, last_y=count_y - 1),
+        out_shape=(image_shape, part_shape),
+        in_specs=[vmem] * 6,
+        out_specs=(vmem,) * 2,
+        input_output_aliases={4: 0, 5: 1},
+        compiler_params=limit(16),
+        cost_estimate=pl.CostEstimate(
+            flops=12 * block.size, bytes_accessed=block.size, transcendentals=block.size
+        ),
+        name="rim",
+    )(block, ya, yb, rim, image, part)
 
     parts = pl.pallas_call(
         functools.partial(outer_kernel, total_z=total_z),
         out_shape=[shaped(5, piece, cols)] * count_z,
         in_specs=[vmem] * 5,
         out_specs=[vmem] * count_z,
-        compiler_params=pltpu.CompilerParams(vmem_limit_bytes=16 * 1024 * 1024),
+        compiler_params=limit(16),
         name="outer",
     )(block, za, zb, image, part)
 
     out_shape = (shaped(3, piece, cols), shaped(piece, cols), shaped(piece, cols))
-    small = pltpu.CompilerParams(vmem_limit_bytes=8 * 1024 * 1024)
+    small = limit(8)
     if count_z == 4:
         peers = [
             lax.ppermute(parts[s], "gz", [(i, i ^ s) for i in range(count_z)]) for s in (1, 2, 3)

time: 32.3 us -> 31.4 us (0.972)
  local copies, waits for them, and re-layouts: 1.59 us -> 0.01 us
  starting transfers between devices: 13.7 us -> 12.2 us
  Pallas kernels: 6.36 us -> 7.79 us
  waiting for transfers between devices: 9.83 us -> 10.6 us
    ppermute x1, waiting for transfers between devices: 0.01 us -> 3.57 us  [on_device(): zb = lax.ppermute(edges[1], 'gz', z_second)]
    ppermute x1, waiting for transfers between devices: 3.23 us -> 0.01 us  [on_device(): yb = lax.ppermute(edges[3], 'gy', y_second)]
    ppermute x3, starting transfers between devices: 5.82 us -> 3.55 us  [on_device(): lax.ppermute(parts[s], 'gz', [(i, i ^ s) for i in range(count_z)])]
    unnamed x4 -> x2, local copies, waits for them, and re-layouts: 1.59 us -> 0.01 us
    pallas_call x1, Pallas kernels: 0.17 us -> 1.7 us  [on_device(): pl.pallas_call(edges_kernel, out_shape=(shaped(HALO, rows, cols), shaped(...]
    ppermute x1, starting transfers between devices: 0.67 us -> 1.49 us  [on_device(): zb = lax.ppermute(edges[1], 'gz', z_second)]
    ppermute x3, waiting for transfers between devices: 6.59 us -> 7 us  [on_device(): lax.ppermute(parts[s], 'gz', [(i, i ^ s) for i in range(count_z)])]
    pallas_call x1 -> x2, Pallas kernels: 4.67 us -> 4.57 us  [the longest x1 4.15 us: on_device(): pl.pallas_call(functools.partial(inner_kernel, total_z=total_z), out_shap...]
where the time goes in v4:
time: 31.4 us; the launch traced here: 31.2 us
  starting transfers between devices  12.2 us (39%)
  waiting for transfers between devices  10.6 us (34%)
  Pallas kernels  7.79 us (25%)
  between operations  0.69 us (2%)
    ppermute x3, waiting for transfers between devices, on_device(): lax.ppermute(parts[s], 'gz', [(i, i ^ s) for i in range(count_z)])  7 us
    pallas_call x1, Pallas kernels, on_device(): pl.pallas_call(functools.partial(inner_kernel, total_z=total_z), out_shap...  4.15 us
    ppermute x1, waiting for transfers between devices, on_device(): zb = lax.ppermute(edges[1], 'gz', z_second)  3.57 us
    ppermute x3, starting transfers between devices, on_device(): lax.ppermute(parts[s], 'gz', [(i, i ^ s) for i in range(count_z)])  3.55 us
    ppermute x1, starting transfers between devices, on_device(): za = lax.ppermute(edges[0], 'gz', z_first)  2.56 us
    ppermute x1, starting transfers between devices, on_device(): yb = lax.ppermute(edges[3], 'gy', y_second)  2.47 us
    pallas_call x1, Pallas kernels, on_device(): pl.pallas_call(edges_kernel, out_shape=(shaped(HALO, rows, cols), shaped(...  1.7 us
    ppermute x1, starting transfers between devices, on_device(): ya = lax.ppermute(edges[2], 'gy', y_first)  1.58 us
  transfers between devices with their start and end apart: 8, of which 3 were waited for; matrix products, arithmetic and copies ran while one was open for 0% of the time, Pallas kernels for 15%

profile of v4, /device:TPU:0, one launch (start us, length us, event | category | flops | bytes accessed | tf_op | source)
XLA Modules:
  0.0 31.2 jit_solution(498623730436532329)
XLA Ops:
  0.6 0.0 copy-start
  0.6 1.7 %edges.1 = (f32[2,128,256]{2,1,0:T(8,128)S(1)}, f32[2,128,256]{2,1,0:T(8,128)S(1)}, f32[16,2,256]{2,1,0:T(2,128)S(1)}, f32[16,2,256]{2,1,0:T(2,128)S(1)}, f32[16,128,128]{2,1,0:T(8,128)S(1)}) custom-call(f32[16,128,256]{2,1,0:T(8,128)} %x_ref.7), custom_call_target="tpu_custom_call" | custom-call | tf_op jit(solution)/shard_map/edges/pallas_call | solution.py:294
  2.3 0.5 %collective-permute-start.4 = (f32[16,128,128]{2,1,0:T(8,128)S(1)}, f32[16,128,128]{2,1,0:T(8,128)S(1)}, u32[]{:S(2)}, u32[]{:S(2)}) collective-permute-start(f32[16,128,128]{2,1,0:T(8,128)S(1)} %get-tuple-element.21), channel_id=1, source_target_pairs={{0,16},{16,0},{1,17},{17,1},{2,18},{18,2},{3,19},{19,3},{4,20},{20... | collective-permute-start | bytes 3145736 | tf_op jit(solution)/shard_map/ppermute | solution.py:313
  2.9 2.6 %collective-permute-start = (f32[2,128,256]{2,1,0:T(8,128)S(1)}, f32[2,128,256]{2,1,0:T(8,128)S(1)}, u32[]{:S(2)}, u32[]{:S(2)}) collective-permute-start(f32[2,128,256]{2,1,0:T(8,128)S(1)} %get-tuple-element.17), channel_id=1, source_target_pairs={{0,1},{1,0},{2,3},{3,2},{4,5},{5,4},{6,7},{7,6},{8,9},{9,8},{10,11... | collective-permute-start | bytes 786440 | tf_op jit(solution)/shard_map/ppermute | solution.py:309
  5.4 1.5 %collective-permute-start.1 = (f32[2,128,256]{2,1,0:T(8,128)S(1)}, f32[2,128,256]{2,1,0:T(8,128)S(1)}, u32[]{:S(2)}, u32[]{:S(2)}) collective-permute-start(f32[2,128,256]{2,1,0:T(8,128)S(1)} %get-tuple-element.18), channel_id=1, source_target_pairs={{1,2},{2,1},{0,3},{3,0},{5,6},{6,5},{4,7},{7,4},{9,10},{10,9},{8,1... | collective-permute-start | bytes 786440 | tf_op jit(solution)/shard_map/ppermute | solution.py:310
  6.9 1.6 %collective-permute-start.2 = (f32[16,2,256]{2,1,0:T(2,128)S(1)}, f32[16,2,256]{2,1,0:T(2,128)S(1)}, u32[]{:S(2)}, u32[]{:S(2)}) collective-permute-start(f32[16,2,256]{2,1,0:T(2,128)S(1)} %get-tuple-element.19), channel_id=1, source_target_pairs={{0,4},{4,0},{8,12},{12,8},{1,5},{5,1},{9,13},{13,9},{2,6},{6,2},{1... | collective-permute-start | bytes 98312 | tf_op jit(solution)/shard_map/ppermute | solution.py:311
  8.5 2.5 %collective-permute-start.3 = (f32[16,2,256]{2,1,0:T(2,128)S(1)}, f32[16,2,256]{2,1,0:T(2,128)S(1)}, u32[]{:S(2)}, u32[]{:S(2)}) collective-permute-start(f32[16,2,256]{2,1,0:T(2,128)S(1)} %get-tuple-element.20), channel_id=1, source_target_pairs={{4,8},{8,4},{0,12},{12,0},{5,9},{9,5},{1,13},{13,1},{6,10},{10,6},... | collective-permute-start | bytes 98312 | tf_op jit(solution)/shard_map/ppermute | solution.py:312
  11.0 0.0 collective-permute-done.4.e_ref
  11.0 0.0 copy-done
  11.0 4.1 %inner.1 = (f32[5,128,256]{2,1,0:T(8,128)S(1)}, f32[4,2,128,256]{3,2,1,0:T(8,128)S(1)}, f32[16,2,16,256]{3,2,1,0:T(8,128)S(1)}) custom-call(f32[16,128,256]{2,1,0:T(8,128)S(1)} %copy-done, f32[16,128,128]{2,1,0:T(8,128)S(1)} %collective-permute-done.4.e_ref), custom_call_target="tpu_custom_call" | custom-call | flops 52428800 | bytes 4194304 | tf_op jit(solution)/shard_map/inner/pallas_call | solution.py:316
  15.1 0.0 collective-permute-done.2.ya_ref
  15.1 0.0 collective-permute-done.3.yb_ref
  15.2 0.4 %rim.1 = (f32[5,128,256]{2,1,0:T(8,128)S(1)}, f32[4,2,128,256]{3,2,1,0:T(8,128)S(1)}) custom-call(f32[16,128,256]{2,1,0:T(8,128)S(1)} %copy-done, f32[16,2,256]{2,1,0:T(2,128)S(1)} %collective-permute-done.2.ya_ref, f32[16,2,256]{2,1,0:T(2,128)S(1)} %collective-permute-done.3.yb_ref, ...), custom_call_target="tpu_custom_call", output_to_operand_aliasing={{0}: (4, {}), {1}: (5, {})} | custom-call | flops 6291456 | bytes 524288 | tf_op jit(solution)/shard_map/rim/pallas_call | solution.py:332
  15.6 0.0 collective-permute-done.za_ref
  15.6 3.6 %collective-permute-done.1.zb_ref = f32[2,128,256]{2,1,0:T(8,128)S(1)} collective-permute-done((f32[2,128,256]{2,1,0:T(8,128)S(1)}, f32[2,128,256]{2,1,0:T(8,128)S(1)}, u32[]{:S(2)}, u32[]{:S(2)}) %collective-permute-start.1) | collective-permute-done | bytes 262176 | tf_op jit(solution)/shard_map/ppermute | solution.py:310
  19.2 0.8 %outer.1 = (f32[5,32,256]{2,1,0:T(8,128)S(1)}, f32[5,32,256]{2,1,0:T(8,128)S(1)}, f32[5,32,256]{2,1,0:T(8,128)S(1)}, f32[5,32,256]{2,1,0:T(8,128)S(1)}) custom-call(f32[16,128,256]{2,1,0:T(8,128)S(1)} %copy-done, f32[2,128,256]{2,1,0:T(8,128)S(1)} %collective-permute-done.za_ref, f32[2,128,256]{2,1,0:T(8,128)S(1)} %collective-permute-done.1.zb_ref, ...), custom_call_target="tpu_custom_call" | custom-call | tf_op jit(solution)/shard_map/outer/pallas_call | solution.py:345
  20.0 1.6 %collective-permute-start.5 = (f32[5,32,256]{2,1,0:T(8,128)S(1)}, f32[5,32,256]{2,1,0:T(8,128)S(1)}, u32[]{:S(2)}, u32[]{:S(2)}) collective-permute-start(f32[5,32,256]{2,1,0:T(8,128)S(1)} %get-tuple-element.28), channel_id=1, source_target_pairs={{0,1},{1,0},{2,3},{3,2},{4,5},{5,4},{6,7},{7,6},{8,9},{9,8},{10,11... | collective-permute-start | bytes 491528 | tf_op jit(solution)/shard_map/ppermute | solution.py:358
  21.5 0.5 %collective-permute-start.6 = (f32[5,32,256]{2,1,0:T(8,128)S(1)}, f32[5,32,256]{2,1,0:T(8,128)S(1)}, u32[]{:S(2)}, u32[]{:S(2)}) collective-permute-start(f32[5,32,256]{2,1,0:T(8,128)S(1)} %get-tuple-element.29), channel_id=1, source_target_pairs={{0,2},{1,3},{2,0},{3,1},{4,6},{5,7},{6,4},{7,5},{8,10},{9,11},{10,... | collective-permute-start | bytes 491528 | tf_op jit(solution)/shard_map/ppermute | solution.py:358
  22.0 1.5 %collective-permute-start.7 = (f32[5,32,256]{2,1,0:T(8,128)S(1)}, f32[5,32,256]{2,1,0:T(8,128)S(1)}, u32[]{:S(2)}, u32[]{:S(2)}) collective-permute-start(f32[5,32,256]{2,1,0:T(8,128)S(1)} %get-tuple-element.30), channel_id=1, source_target_pairs={{0,3},{1,2},{2,1},{3,0},{4,7},{5,6},{6,5},{7,4},{8,11},{9,10},{10,... | collective-permute-start | bytes 491528 | tf_op jit(solution)/shard_map/ppermute | solution.py:358
  23.5 3.4 %collective-permute-done.5.one_ref = f32[5,32,256]{2,1,0:T(8,128)S(1)} collective-permute-done((f32[5,32,256]{2,1,0:T(8,128)S(1)}, f32[5,32,256]{2,1,0:T(8,128)S(1)}, u32[]{:S(2)}, u32[]{:S(2)}) %collective-permute-start.5) | collective-permute-done | bytes 163872 | tf_op jit(solution)/shard_map/ppermute | solution.py:358
  26.9 3.6 %collective-permute-done.6.two_ref = f32[5,32,256]{2,1,0:T(8,128)S(1)} collective-permute-done((f32[5,32,256]{2,1,0:T(8,128)S(1)}, f32[5,32,256]{2,1,0:T(8,128)S(1)}, u32[]{:S(2)}, u32[]{:S(2)}) %collective-permute-start.6) | collective-permute-done | bytes 163872 | tf_op jit(solution)/shard_map/ppermute | solution.py:358
  30.5 0.0 collective-permute-done.7.three_ref
  30.5 0.7 %blend.1 = (f32[3,32,256]{2,1,0:T(8,128)}, f32[32,256]{1,0:T(8,128)}, f32[32,256]{1,0:T(8,128)}) custom-call(f32[5,32,256]{2,1,0:T(8,128)S(1)} %get-tuple-element.27.own_ref, f32[5,32,256]{2,1,0:T(8,128)S(1)} %collective-permute-done.5.one_ref, f32[5,32,256]{2,1,0:T(8,128)S(1)} %collective-permute-done.6.two_ref, ...), custom_call_target="tpu_custom_call" | custom-call | tf_op jit(solution)/shard_map/blend/pallas_call | solution.py:360
Async XLA Ops:
  0.6 10.3 %copy-start = (f32[16,128,256]{2,1,0:T(8,128)S(1)}, f32[16,128,256]{2,1,0:T(8,128)}, u32[]{:S(2)}) copy-start(f32[16,128,256]{2,1,0:T(8,128)} %x_ref.7) | copy-start | bytes 6291460
  2.3 8.6 %collective-permute-start.4 = (f32[16,128,128]{2,1,0:T(8,128)S(1)}, f32[16,128,128]{2,1,0:T(8,128)S(1)}, u32[]{:S(2)}, u32[]{:S(2)}) collective-permute-start(f32[16,128,128]{2,1,0:T(8,128)S(1)} %get-tuple-element.21), channel_id=1, source_target_pairs={{0,16},{16,0},{1,17},{17,1},{2,18},{18,2},{3,19},{19,3},{4,20},{20... | collective-permute-start | bytes 3145736 | tf_op jit(solution)/shard_map/ppermute | solution.py:313
  2.9 12.7 %collective-permute-start = (f32[2,128,256]{2,1,0:T(8,128)S(1)}, f32[2,128,256]{2,1,0:T(8,128)S(1)}, u32[]{:S(2)}, u32[]{:S(2)}) collective-permute-start(f32[2,128,256]{2,1,0:T(8,128)S(1)} %get-tuple-element.17), channel_id=1, source_target_pairs={{0,1},{1,0},{2,3},{3,2},{4,5},{5,4},{6,7},{7,6},{8,9},{9,8},{10,11... | collective-permute-start | bytes 786440 | tf_op jit(solution)/shard_map/ppermute | solution.py:309
  5.4 13.7 %collective-permute-start.1 = (f32[2,128,256]{2,1,0:T(8,128)S(1)}, f32[2,128,256]{2,1,0:T(8,128)S(1)}, u32[]{:S(2)}, u32[]{:S(2)}) collective-permute-start(f32[2,128,256]{2,1,0:T(8,128)S(1)} %get-tuple-element.18), channel_id=1, source_target_pairs={{1,2},{2,1},{0,3},{3,0},{5,6},{6,5},{4,7},{7,4},{9,10},{10,9},{8,1... | collective-permute-start | bytes 786440 | tf_op jit(solution)/shard_map/ppermute | solution.py:310
  6.9 8.2 %collective-permute-start.2 = (f32[16,2,256]{2,1,0:T(2,128)S(1)}, f32[16,2,256]{2,1,0:T(2,128)S(1)}, u32[]{:S(2)}, u32[]{:S(2)}) collective-permute-start(f32[16,2,256]{2,1,0:T(2,128)S(1)} %get-tuple-element.19), channel_id=1, source_target_pairs={{0,4},{4,0},{8,12},{12,8},{1,5},{5,1},{9,13},{13,9},{2,6},{6,2},{1... | collective-permute-start | bytes 98312 | tf_op jit(solution)/shard_map/ppermute | solution.py:311
  8.5 6.7 %collective-permute-start.3 = (f32[16,2,256]{2,1,0:T(2,128)S(1)}, f32[16,2,256]{2,1,0:T(2,128)S(1)}, u32[]{:S(2)}, u32[]{:S(2)}) collective-permute-start(f32[16,2,256]{2,1,0:T(2,128)S(1)} %get-tuple-element.20), channel_id=1, source_target_pairs={{4,8},{8,4},{0,12},{12,0},{5,9},{9,5},{1,13},{13,1},{6,10},{10,6},... | collective-permute-start | bytes 98312 | tf_op jit(solution)/shard_map/ppermute | solution.py:312
  20.0 6.9 %collective-permute-start.5 = (f32[5,32,256]{2,1,0:T(8,128)S(1)}, f32[5,32,256]{2,1,0:T(8,128)S(1)}, u32[]{:S(2)}, u32[]{:S(2)}) collective-permute-start(f32[5,32,256]{2,1,0:T(8,128)S(1)} %get-tuple-element.28), channel_id=1, source_target_pairs={{0,1},{1,0},{2,3},{3,2},{4,5},{5,4},{6,7},{7,6},{8,9},{9,8},{10,11... | collective-permute-start | bytes 491528 | tf_op jit(solution)/shard_map/ppermute | solution.py:358
  21.5 9.0 %collective-permute-start.6 = (f32[5,32,256]{2,1,0:T(8,128)S(1)}, f32[5,32,256]{2,1,0:T(8,128)S(1)}, u32[]{:S(2)}, u32[]{:S(2)}) collective-permute-start(f32[5,32,256]{2,1,0:T(8,128)S(1)} %get-tuple-element.29), channel_id=1, source_target_pairs={{0,2},{1,3},{2,0},{3,1},{4,6},{5,7},{6,4},{7,5},{8,10},{9,11},{10,... | collective-permute-start | bytes 491528 | tf_op jit(solution)/shard_map/ppermute | solution.py:358
  22.0 8.5 %collective-permute-start.7 = (f32[5,32,256]{2,1,0:T(8,128)S(1)}, f32[5,32,256]{2,1,0:T(8,128)S(1)}, u32[]{:S(2)}, u32[]{:S(2)}) collective-permute-start(f32[5,32,256]{2,1,0:T(8,128)S(1)} %get-tuple-element.30), channel_id=1, source_target_pairs={{0,3},{1,2},{2,1},{3,0},{4,7},{5,6},{6,5},{7,4},{8,11},{9,10},{10,... | collective-permute-start | bytes 491528 | tf_op jit(solution)/shard_map/ppermute | solution.py:358

commit v5 on v4

--- a/solution.py
+++ b/solution.py
@@ -43,25 +43,37 @@
     return tuple(lax.axis_index(a) for a in ("gx", "gy", "gz"))
 
 
-def edges_kernel(x_ref, za_ref, zb_ref, ya_ref, yb_ref, e_ref, top_ref, bottom_ref, sems):
+def block_of(offset, swapped, at_z):
+    return at_z ^ offset if swapped else offset
+
+
+def edges_kernel(x_ref, *refs, groups, swapped, count_z):
+    z_refs, (ya_ref, yb_ref, e_ref, top_ref, bottom_ref, sems) = refs[:-6], refs[-6:]
     cells_z, rows, cols = x_ref.shape
     at_x, at_y, at_z = place()
-    strip = e_ref.shape[2]
+    strip, piece = e_ref.shape[2], z_refs[0].shape[2]
     even_z, even_y = at_z % 2 == 0, at_y % 2 == 0
     high = cells_z - HALO
     start = pl.multiple_of(jnp.where(at_x == 0, cols - strip, 0), strip)
-    copies = [
-        pltpu.make_async_copy(source, target, sems.at[i])
-        for i, (source, target) in enumerate(
-            (
-                (x_ref.at[pl.ds(jnp.where(even_z, high, 0), HALO)], za_ref),
-                (x_ref.at[pl.ds(jnp.where(even_z, 0, high), HALO)], zb_ref),
-                (x_ref.at[:, pl.ds(0, RIM)], top_ref),
-                (x_ref.at[:, pl.ds(rows - RIM, RIM)], bottom_ref),
-                (x_ref.at[:, :, pl.ds(start, strip)], e_ref),
-            )
-        )
+    after = lax.rem(at_z + 1, count_z)
+    before = lax.rem(at_z + count_z - 1, count_z)
+    sides = (
+        (jnp.where(even_z, after, before), jnp.where(even_z, high, 0)),
+        (jnp.where(even_z, before, after), jnp.where(even_z, 0, high)),
+    )
+    moves = []
+    for group, offsets in enumerate(groups):
+        for side, (peer, layer) in enumerate(sides):
+            for slot, offset in enumerate(offsets):
+                row = pl.multiple_of(block_of(offset, swapped, peer) * piece, 8)
+                source = x_ref.at[pl.ds(layer, HALO), pl.ds(row, piece)]
+                moves.append((source, z_refs[2 * group + side].at[slot]))
+    moves += [
+        (x_ref.at[:, pl.ds(0, RIM)], top_ref),
+        (x_ref.at[:, pl.ds(rows - RIM, RIM)], bottom_ref),
+        (x_ref.at[:, :, pl.ds(start, strip)], e_ref),
     ]
+    copies = [pltpu.make_async_copy(*move, sems.at[i]) for i, move in enumerate(moves)]
     for copy in copies:
         copy.start()
     for copy in copies:
@@ -190,24 +202,26 @@
             image_ref[channel, to] = value
 
 
-def outer_kernel(x_ref, za_ref, zb_ref, image_ref, part_ref, *out_refs, total_z):
+def outer_kernel(x_ref, za_ref, zb_ref, image_ref, part_ref, *refs, total_z, offsets, swapped):
     cells_z, _, cols = x_ref.shape
     depth_step = 2.0 / total_z
     at_z = place()[2]
     last_z = total_z // cells_z - 1
     even = at_z % 2 == 0
-    count, piece = len(out_refs), out_refs[0].shape[1]
+    out_refs = refs[-len(offsets) :]
+    piece = out_refs[0].shape[1]
     chunk = min(piece, 16)
     none = jnp.zeros((chunk, cols), jnp.float32)
-    for out, start in [(o, s) for o in range(count) for s in range(0, piece, chunk)]:
-        block = at_z ^ out if count == 4 else out
+    for out, start in [(o, s) for o in range(len(offsets)) for s in range(0, piece, chunk)]:
+        block = block_of(offsets[out], swapped, at_z)
+        part = pl.ds(start, chunk)
         at = pl.ds(pl.multiple_of(block * piece + start, 8), chunk)
 
         def before(layer):
-            return jnp.where(at_z > 0, jnp.where(even, zb_ref[layer, at], za_ref[layer, at]), none)
+            return jnp.where(at_z > 0, jnp.where(even, zb_ref[out, layer, part], za_ref[out, layer, part]), none)
 
         def after(layer):
-            return jnp.where(at_z < last_z, jnp.where(even, za_ref[layer, at], zb_ref[layer, at]), none)
+            return jnp.where(at_z < last_z, jnp.where(even, za_ref[out, layer, part], zb_ref[out, layer, part]), none)
 
         f = [x_ref[k, at] for k in range(4)]
         b = [x_ref[cells_z - 4 + k, at] for k in range(4)]
@@ -230,7 +244,7 @@
             )
             sums = [s + a for s, a in zip(sums, adds)]
         for channel, value in enumerate(sums + [through]):
-            out_refs[out][channel, pl.ds(start, chunk)] = value
+            out_refs[out][channel, part] = value
 
 
 def join(front, back):
@@ -291,26 +305,29 @@
     def limit(mebibytes):
         return pltpu.CompilerParams(vmem_limit_bytes=mebibytes * 1024 * 1024)
 
+    swapped = count_z == 4
+    groups = ((2, 3), (1, 0)) if swapped else (tuple(range(count_z)),)
+    payloads = [shaped(len(g), HALO, piece, cols) for g in groups for _ in range(2)]
     edges = pl.pallas_call(
-        edges_kernel,
-        out_shape=(
-            shaped(HALO, rows, cols), shaped(HALO, rows, cols),
-            shaped(cells_z, HALO, cols), shaped(cells_z, HALO, cols),
-            shaped(cells_z, rows, strip),
-        ),
+        functools.partial(edges_kernel, groups=groups, swapped=swapped, count_z=count_z),
+        out_shape=payloads
+        + [shaped(cells_z, HALO, cols)] * 2
+        + [shaped(cells_z, rows, strip)],
         in_specs=[pl.BlockSpec(memory_space=pltpu.HBM)],
-        out_specs=(vmem,) * 5,
-        scratch_shapes=[pltpu.VMEM((cells_z, RIM, cols), f32)] * 2 + [pltpu.SemaphoreType.DMA((5,))],
+        out_specs=[vmem] * (len(payloads) + 3),
+        scratch_shapes=[pltpu.VMEM((cells_z, RIM, cols), f32)] * 2
+        + [pltpu.SemaphoreType.DMA((2 * sum(len(g) for g in groups) + 3,))],
         compiler_params=limit(4),
         name="edges",
     )(pltpu.with_memory_space_constraint(block, pltpu.HBM))
-    z_first, z_second = pairs(count_z, True)
-    y_first, y_second = pairs(count_y, True)
-    za = lax.ppermute(edges[0], "gz", z_first)
-    zb = lax.ppermute(edges[1], "gz", z_second)
-    ya = lax.ppermute(edges[2], "gy", y_first)
-    yb = lax.ppermute(edges[3], "gy", y_second)
-    edge = lax.ppermute(edges[4], "gx", [(0, 1), (1, 0)])
+    z_pairs, (y_first, y_second) = pairs(count_z, True), pairs(count_y, True)
+    halos = [
+        [lax.ppermute(edges[2 * g + side], "gz", z_pairs[side]) for side in range(2)]
+        for g in range(len(groups))
+    ]
+    ya = lax.ppermute(edges[-3], "gy", y_first)
+    yb = lax.ppermute(edges[-2], "gy", y_second)
+    edge = lax.ppermute(edges[-1], "gx", [(0, 1), (1, 0)])
 
     image_shape, part_shape = shaped(5, rows, cols), shaped(4, 2, rows, cols)
     image, part, rim = pl.pallas_call(
@@ -342,36 +359,38 @@
         name="rim",
     )(block, ya, yb, rim, image, part)
 
-    parts = pl.pallas_call(
-        functools.partial(outer_kernel, total_z=total_z),
-        out_shape=[shaped(5, piece, cols)] * count_z,
-        in_specs=[vmem] * 5,
-        out_specs=[vmem] * count_z,
-        compiler_params=limit(16),
-        name="outer",
-    )(block, za, zb, image, part)
-
+    received = {}
+    for offsets, (za, zb) in zip(groups, halos):
+        made = pl.pallas_call(
+            functools.partial(outer_kernel, total_z=total_z, offsets=offsets, swapped=swapped),
+            out_shape=[shaped(5, piece, cols)] * len(offsets),
+            in_specs=[vmem] * 5,
+            out_specs=[vmem] * len(offsets),
+            compiler_params=limit(16),
+            name="outer",
+        )(block, za, zb, image, part)
+        received.update(zip(offsets, made))
     out_shape = (shaped(3, piece, cols), shaped(piece, cols), shaped(piece, cols))
-    small = limit(8)
-    if count_z == 4:
-        peers = [
-            lax.ppermute(parts[s], "gz", [(i, i ^ s) for i in range(count_z)]) for s in (1, 2, 3)
-        ]
+    if swapped:
+        for offset in (3, 2, 1):
+            swap = [(i, i ^ offset) for i in range(count_z)]
+            received[offset] = lax.ppermute(received[offset], "gz", swap)
         return pl.pallas_call(
             blend_four,
             out_shape=out_shape,
             in_specs=[vmem] * 4,
             out_specs=(vmem, vmem, vmem),
-            compiler_params=small,
+            compiler_params=limit(8),
             name="blend",
-        )(parts[0], *peers)
-    gathered = lax.all_to_all(jnp.stack(parts), "gz", split_axis=0, concat_axis=0, tiled=True)
+        )(*(received[offset] for offset in range(4)))
+    parts = jnp.stack([received[k] for k in range(count_z)])
+    gathered = lax.all_to_all(parts, "gz", split_axis=0, concat_axis=0, tiled=True)
     return pl.pallas_call(
         blend_all,
         out_shape=out_shape,
         in_specs=[vmem],
         out_specs=(vmem, vmem, vmem),
-        compiler_params=small,
+        compiler_params=limit(8),
         name="blend",
     )(gathered)
 

time: 31.4 us -> 29.6 us (0.943)
  waiting for transfers between devices: 10.6 us -> 5.58 us
  starting transfers between devices: 12.2 us -> 15.2 us
    ppermute x8 -> x10, waiting for transfers between devices: 10.6 us -> 5.58 us  [the longest x3 5.57 us: on_device(): received[offset] = lax.ppermute(received[offset], 'gz', swap)]
    ppermute x8 -> x10, starting transfers between devices: 12.2 us -> 15.2 us  [the longest x4 4.95 us: on_device(): lax.ppermute(edges[2 * g + side], 'gz', z_pairs[side])]
    pallas_call x2 -> x3, Pallas kernels: 2.5 us -> 2.68 us  [the longest x1 1.86 us: on_device(): pl.pallas_call(functools.partial(edges_kernel, groups=groups, swapped=swa...]
  transfers between devices with their start and end apart: 8 -> 10, of which waited for: 3 -> 2; matrix products, arithmetic and copies ran while one was open for 0% -> 0% of each run, Pallas kernels for 15% -> 18%
where the time goes in v5:
time: 29.6 us; the launch traced here: 29.4 us
  starting transfers between devices  15.2 us (51%)
  Pallas kernels  7.97 us (27%)
  waiting for transfers between devices  5.58 us (19%)
  between operations  0.71 us (2%)
    ppermute x3, waiting for transfers between devices, on_device(): received[offset] = lax.ppermute(received[offset], 'gz', swap)  5.57 us
    ppermute x4, starting transfers between devices, on_device(): lax.ppermute(edges[2 * g + side], 'gz', z_pairs[side])  4.95 us
    pallas_call x1, Pallas kernels, on_device(): pl.pallas_call(functools.partial(inner_kernel, total_z=total_z), out_shap...  4.15 us
    ppermute x3, starting transfers between devices, on_device(): received[offset] = lax.ppermute(received[offset], 'gz', swap)  3.62 us
    ppermute x1, starting transfers between devices, on_device(): yb = lax.ppermute(edges[-2], 'gy', y_second)  3.43 us
    ppermute x1, starting transfers between devices, on_device(): ya = lax.ppermute(edges[-3], 'gy', y_first)  2.65 us
    pallas_call x1, Pallas kernels, on_device(): pl.pallas_call(functools.partial(edges_kernel, groups=groups, swapped=swa...  1.86 us
    pallas_call x2, Pallas kernels, on_device(): pl.pallas_call(functools.partial(outer_kernel, total_z=total_z, offsets=o...  0.82 us
  transfers between devices with their start and end apart: 10, of which 2 were waited for; matrix products, arithmetic and copies ran while one was open for 0% of the time, Pallas kernels for 18%

profile of v5, /device:TPU:0, one launch (start us, length us, event | category | flops | bytes accessed | tf_op | source)
XLA Modules:
  0.0 29.4 jit_solution(1210949515872349692)
XLA Ops:
  0.6 1.9 %edges.1 = (f32[2,2,32,256]{3,2,1,0:T(8,128)S(1)}, f32[2,2,32,256]{3,2,1,0:T(8,128)S(1)}, f32[2,2,32,256]{3,2,1,0:T(8,128)S(1)}, f32[2,2,32,256]{3,2,1,0:T(8,128...) custom-call(f32[16,128,256]{2,1,0:T(8,128)} %x_ref.9), custom_call_target="tpu_custom_call" | custom-call | tf_op jit(solution)/shard_map/edges/pallas_call | solution.py:311
  2.5 0.5 %collective-permute-start.4 = (f32[16,128,128]{2,1,0:T(8,128)S(1)}, f32[16,128,128]{2,1,0:T(8,128)S(1)}, u32[]{:S(2)}, u32[]{:S(2)}) collective-permute-start(f32[16,128,128]{2,1,0:T(8,128)S(1)} %get-tuple-element.23), channel_id=1, source_target_pairs={{0,16},{16,0},{1,17},{17,1},{2,18},{18,2},{3,19},{19,3},{4,20},{20... | collective-permute-start | bytes 3145736 | tf_op jit(solution)/shard_map/ppermute | solution.py:330
  3.0 2.6 %collective-permute-start.2 = (f32[16,2,256]{2,1,0:T(2,128)S(1)}, f32[16,2,256]{2,1,0:T(2,128)S(1)}, u32[]{:S(2)}, u32[]{:S(2)}) collective-permute-start(f32[16,2,256]{2,1,0:T(2,128)S(1)} %get-tuple-element.21), channel_id=1, source_target_pairs={{0,4},{4,0},{8,12},{12,8},{1,5},{5,1},{9,13},{13,9},{2,6},{6,2},{1... | collective-permute-start | bytes 98312 | tf_op jit(solution)/shard_map/ppermute | solution.py:328
  5.7 1.5 %collective-permute-start.6 = (f32[2,2,32,256]{3,2,1,0:T(8,128)S(1)}, f32[2,2,32,256]{3,2,1,0:T(8,128)S(1)}, u32[]{:S(2)}, u32[]{:S(2)}) collective-permute-start(f32[2,2,32,256]{3,2,1,0:T(8,128)S(1)} %get-tuple-element.31), channel_id=1, source_target_pairs={{0,1},{1,0},{2,3},{3,2},{4,5},{5,4},{6,7},{7,6},{8,9},{9,8},{10,11... | collective-permute-start | bytes 393224 | tf_op jit(solution)/shard_map/ppermute | solution.py:325
  7.2 1.5 %collective-permute-start.7 = (f32[2,2,32,256]{3,2,1,0:T(8,128)S(1)}, f32[2,2,32,256]{3,2,1,0:T(8,128)S(1)}, u32[]{:S(2)}, u32[]{:S(2)}) collective-permute-start(f32[2,2,32,256]{3,2,1,0:T(8,128)S(1)} %get-tuple-element.32), channel_id=1, source_target_pairs={{1,2},{2,1},{0,3},{3,0},{5,6},{6,5},{4,7},{7,4},{9,10},{10,9},{8,1... | collective-permute-start | bytes 393224 | tf_op jit(solution)/shard_map/ppermute | solution.py:325
  8.7 1.5 %collective-permute-start = (f32[2,2,32,256]{3,2,1,0:T(8,128)S(1)}, f32[2,2,32,256]{3,2,1,0:T(8,128)S(1)}, u32[]{:S(2)}, u32[]{:S(2)}) collective-permute-start(f32[2,2,32,256]{3,2,1,0:T(8,128)S(1)} %get-tuple-element.19), channel_id=1, source_target_pairs={{0,1},{1,0},{2,3},{3,2},{4,5},{5,4},{6,7},{7,6},{8,9},{9,8},{10,11... | collective-permute-start | bytes 393224 | tf_op jit(solution)/shard_map/ppermute | solution.py:325
  10.1 0.0 collective-permute-done.2.ya_ref
  10.1 0.5 %collective-permute-start.1 = (f32[2,2,32,256]{3,2,1,0:T(8,128)S(1)}, f32[2,2,32,256]{3,2,1,0:T(8,128)S(1)}, u32[]{:S(2)}, u32[]{:S(2)}) collective-permute-start(f32[2,2,32,256]{3,2,1,0:T(8,128)S(1)} %get-tuple-element.20), channel_id=1, source_target_pairs={{1,2},{2,1},{0,3},{3,0},{5,6},{6,5},{4,7},{7,4},{9,10},{10,9},{8,1... | collective-permute-start | bytes 393224 | tf_op jit(solution)/shard_map/ppermute | solution.py:325
  10.6 0.0 collective-permute-done.4.e_ref
  10.6 3.4 %collective-permute-start.3 = (f32[16,2,256]{2,1,0:T(2,128)S(1)}, f32[16,2,256]{2,1,0:T(2,128)S(1)}, u32[]{:S(2)}, u32[]{:S(2)}) collective-permute-start(f32[16,2,256]{2,1,0:T(2,128)S(1)} %get-tuple-element.22), channel_id=1, source_target_pairs={{4,8},{8,4},{0,12},{12,0},{5,9},{9,5},{1,13},{13,1},{6,10},{10,6},... | collective-permute-start | bytes 98312 | tf_op jit(solution)/shard_map/ppermute | solution.py:329
  14.1 4.1 %inner.1 = (f32[5,128,256]{2,1,0:T(8,128)S(1)}, f32[4,2,128,256]{3,2,1,0:T(8,128)S(1)}, f32[16,2,16,256]{3,2,1,0:T(8,128)S(1)}) custom-call(f32[16,128,256]{2,1,0:T(8,128)S(1)} %copy-done, f32[16,128,128]{2,1,0:T(8,128)S(1)} %collective-permute-done.4.e_ref), custom_call_target="tpu_custom_call" | custom-call | flops 52428800 | bytes 4194304 | tf_op jit(solution)/shard_map/inner/pallas_call | solution.py:333
  18.2 0.0 collective-permute-done.3.yb_ref
  18.2 0.4 %rim.1 = (f32[5,128,256]{2,1,0:T(8,128)S(1)}, f32[4,2,128,256]{3,2,1,0:T(8,128)S(1)}) custom-call(f32[16,128,256]{2,1,0:T(8,128)S(1)} %copy-done, f32[16,2,256]{2,1,0:T(2,128)S(1)} %collective-permute-done.2.ya_ref, f32[16,2,256]{2,1,0:T(2,128)S(1)} %collective-permute-done.3.yb_ref, ...), custom_call_target="tpu_custom_call", output_to_operand_aliasing={{0}: (4, {}), {1}: (5, {})} | custom-call | flops 6291456 | bytes 524288 | tf_op jit(solution)/shard_map/rim/pallas_call | solution.py:349
  18.7 0.0 collective-permute-done.6.za_ref
  18.7 0.0 collective-permute-done.7.zb_ref
  18.7 0.4 %outer.3 = (f32[5,32,256]{2,1,0:T(8,128)S(1)}, f32[5,32,256]{2,1,0:T(8,128)S(1)}) custom-call(f32[16,128,256]{2,1,0:T(8,128)S(1)} %copy-done, f32[2,2,32,256]{3,2,1,0:T(8,128)S(1)} %collective-permute-done.6.za_ref, f32[2,2,32,256]{3,2,1,0:T(8,128)S(1)} %collective-permute-done.7.zb_ref, f32[5,128,256]{2,1,0:T(8,128)S(1)} %get-tuple-element.27.image_ref, ...), custom_call_target="tpu_custom_call" | custom-call | tf_op jit(solution)/shard_map/outer/pallas_call | solution.py:364
  19.1 0.6 %collective-permute-start.8 = (f32[5,32,256]{2,1,0:T(8,128)S(1)}, f32[5,32,256]{2,1,0:T(8,128)S(1)}, u32[]{:S(2)}, u32[]{:S(2)}) collective-permute-start(f32[5,32,256]{2,1,0:T(8,128)S(1)} %get-tuple-element.33), channel_id=1, source_target_pairs={{0,2},{1,3},{2,0},{3,1},{4,6},{5,7},{6,4},{7,5},{8,10},{9,11},{10,... | collective-permute-start | bytes 491528 | tf_op jit(solution)/shard_map/ppermute | solution.py:377
  19.7 1.4 %collective-permute-start.9 = (f32[5,32,256]{2,1,0:T(8,128)S(1)}, f32[5,32,256]{2,1,0:T(8,128)S(1)}, u32[]{:S(2)}, u32[]{:S(2)}) collective-permute-start(f32[5,32,256]{2,1,0:T(8,128)S(1)} %get-tuple-element.34), channel_id=1, source_target_pairs={{0,3},{1,2},{2,1},{3,0},{4,7},{5,6},{6,5},{7,4},{8,11},{9,10},{10,... | collective-permute-start | bytes 491528 | tf_op jit(solution)/shard_map/ppermute | solution.py:377
  21.2 0.4 %outer.2 = (f32[5,32,256]{2,1,0:T(8,128)S(1)}, f32[5,32,256]{2,1,0:T(8,128)S(1)}) custom-call(f32[16,128,256]{2,1,0:T(8,128)S(1)} %copy-done, f32[2,2,32,256]{3,2,1,0:T(8,128)S(1)} %collective-permute-done.za_ref, f32[2,2,32,256]{3,2,1,0:T(8,128)S(1)} %collective-permute-done.1.zb_ref, f32[5,128,256]{2,1,0:T(8,128)S(1)} %get-tuple-element.27.image_ref, ...), custom_call_target="tpu_custom_call" | custom-call | tf_op jit(solution)/shard_map/outer/pallas_call | solution.py:364
  21.6 1.6 %collective-permute-start.5 = (f32[5,32,256]{2,1,0:T(8,128)S(1)}, f32[5,32,256]{2,1,0:T(8,128)S(1)}, u32[]{:S(2)}, u32[]{:S(2)}) collective-permute-start(f32[5,32,256]{2,1,0:T(8,128)S(1)} %get-tuple-element.30), channel_id=1, source_target_pairs={{0,1},{1,0},{2,3},{3,2},{4,5},{5,4},{6,7},{7,6},{8,9},{9,8},{10,11... | collective-permute-start | bytes 491528 | tf_op jit(solution)/shard_map/ppermute | solution.py:377
  23.1 4.5 %collective-permute-done.8.two_ref = f32[5,32,256]{2,1,0:T(8,128)S(1)} collective-permute-done((f32[5,32,256]{2,1,0:T(8,128)S(1)}, f32[5,32,256]{2,1,0:T(8,128)S(1)}, u32[]{:S(2)}, u32[]{:S(2)}) %collective-permute-start.8) | collective-permute-done | bytes 163872 | tf_op jit(solution)/shard_map/ppermute | solution.py:377
  27.6 0.0 collective-permute-done.9.three_ref
  27.6 1.1 %collective-permute-done.5.one_ref = f32[5,32,256]{2,1,0:T(8,128)S(1)} collective-permute-done((f32[5,32,256]{2,1,0:T(8,128)S(1)}, f32[5,32,256]{2,1,0:T(8,128)S(1)}, u32[]{:S(2)}, u32[]{:S(2)}) %collective-permute-start.5) | collective-permute-done | bytes 163872 | tf_op jit(solution)/shard_map/ppermute | solution.py:377
  28.7 0.7 %blend.1 = (f32[3,32,256]{2,1,0:T(8,128)}, f32[32,256]{1,0:T(8,128)}, f32[32,256]{1,0:T(8,128)}) custom-call(f32[5,32,256]{2,1,0:T(8,128)S(1)} %get-tuple-element.29.own_ref, f32[5,32,256]{2,1,0:T(8,128)S(1)} %collective-permute-done.5.one_ref, f32[5,32,256]{2,1,0:T(8,128)S(1)} %collective-permute-done.8.two_ref, ...), custom_call_target="tpu_custom_call" | custom-call | tf_op jit(solution)/shard_map/blend/pallas_call | solution.py:378
  (4 shorter events, 0.0 us)
Async XLA Ops:
  0.6 13.4 %copy-start = (f32[16,128,256]{2,1,0:T(8,128)S(1)}, f32[16,128,256]{2,1,0:T(8,128)}, u32[]{:S(2)}) copy-start(f32[16,128,256]{2,1,0:T(8,128)} %x_ref.9) | copy-start | bytes 6291460
  2.5 8.1 %collective-permute-start.4 = (f32[16,128,128]{2,1,0:T(8,128)S(1)}, f32[16,128,128]{2,1,0:T(8,128)S(1)}, u32[]{:S(2)}, u32[]{:S(2)}) collective-permute-start(f32[16,128,128]{2,1,0:T(8,128)S(1)} %get-tuple-element.23), channel_id=1, source_target_pairs={{0,16},{16,0},{1,17},{17,1},{2,18},{18,2},{3,19},{19,3},{4,20},{20... | collective-permute-start | bytes 3145736 | tf_op jit(solution)/shard_map/ppermute | solution.py:330
  3.0 7.1 %collective-permute-start.2 = (f32[16,2,256]{2,1,0:T(2,128)S(1)}, f32[16,2,256]{2,1,0:T(2,128)S(1)}, u32[]{:S(2)}, u32[]{:S(2)}) collective-permute-start(f32[16,2,256]{2,1,0:T(2,128)S(1)} %get-tuple-element.21), channel_id=1, source_target_pairs={{0,4},{4,0},{8,12},{12,8},{1,5},{5,1},{9,13},{13,9},{2,6},{6,2},{1... | collective-permute-start | bytes 98312 | tf_op jit(solution)/shard_map/ppermute | solution.py:328
  5.7 13.0 %collective-permute-start.6 = (f32[2,2,32,256]{3,2,1,0:T(8,128)S(1)}, f32[2,2,32,256]{3,2,1,0:T(8,128)S(1)}, u32[]{:S(2)}, u32[]{:S(2)}) collective-permute-start(f32[2,2,32,256]{3,2,1,0:T(8,128)S(1)} %get-tuple-element.31), channel_id=1, source_target_pairs={{0,1},{1,0},{2,3},{3,2},{4,5},{5,4},{6,7},{7,6},{8,9},{9,8},{10,11... | collective-permute-start | bytes 393224 | tf_op jit(solution)/shard_map/ppermute | solution.py:325
  7.2 11.5 %collective-permute-start.7 = (f32[2,2,32,256]{3,2,1,0:T(8,128)S(1)}, f32[2,2,32,256]{3,2,1,0:T(8,128)S(1)}, u32[]{:S(2)}, u32[]{:S(2)}) collective-permute-start(f32[2,2,32,256]{3,2,1,0:T(8,128)S(1)} %get-tuple-element.32), channel_id=1, source_target_pairs={{1,2},{2,1},{0,3},{3,0},{5,6},{6,5},{4,7},{7,4},{9,10},{10,9},{8,1... | collective-permute-start | bytes 393224 | tf_op jit(solution)/shard_map/ppermute | solution.py:325
  8.7 12.5 %collective-permute-start = (f32[2,2,32,256]{3,2,1,0:T(8,128)S(1)}, f32[2,2,32,256]{3,2,1,0:T(8,128)S(1)}, u32[]{:S(2)}, u32[]{:S(2)}) collective-permute-start(f32[2,2,32,256]{3,2,1,0:T(8,128)S(1)} %get-tuple-element.19), channel_id=1, source_target_pairs={{0,1},{1,0},{2,3},{3,2},{4,5},{5,4},{6,7},{7,6},{8,9},{9,8},{10,11... | collective-permute-start | bytes 393224 | tf_op jit(solution)/shard_map/ppermute | solution.py:325
  10.1 11.0 %collective-permute-start.1 = (f32[2,2,32,256]{3,2,1,0:T(8,128)S(1)}, f32[2,2,32,256]{3,2,1,0:T(8,128)S(1)}, u32[]{:S(2)}, u32[]{:S(2)}) collective-permute-start(f32[2,2,32,256]{3,2,1,0:T(8,128)S(1)} %get-tuple-element.20), channel_id=1, source_target_pairs={{1,2},{2,1},{0,3},{3,0},{5,6},{6,5},{4,7},{7,4},{9,10},{10,9},{8,1... | collective-permute-start | bytes 393224 | tf_op jit(solution)/shard_map/ppermute | solution.py:325
  10.6 7.6 %collective-permute-start.3 = (f32[16,2,256]{2,1,0:T(2,128)S(1)}, f32[16,2,256]{2,1,0:T(2,128)S(1)}, u32[]{:S(2)}, u32[]{:S(2)}) collective-permute-start(f32[16,2,256]{2,1,0:T(2,128)S(1)} %get-tuple-element.22), channel_id=1, source_target_pairs={{4,8},{8,4},{0,12},{12,0},{5,9},{9,5},{1,13},{13,1},{6,10},{10,6},... | collective-permute-start | bytes 98312 | tf_op jit(solution)/shard_map/ppermute | solution.py:329
  19.1 8.5 %collective-permute-start.8 = (f32[5,32,256]{2,1,0:T(8,128)S(1)}, f32[5,32,256]{2,1,0:T(8,128)S(1)}, u32[]{:S(2)}, u32[]{:S(2)}) collective-permute-start(f32[5,32,256]{2,1,0:T(8,128)S(1)} %get-tuple-element.33), channel_id=1, source_target_pairs={{0,2},{1,3},{2,0},{3,1},{4,6},{5,7},{6,4},{7,5},{8,10},{9,11},{10,... | collective-permute-start | bytes 491528 | tf_op jit(solution)/shard_map/ppermute | solution.py:377
  19.7 7.9 %collective-permute-start.9 = (f32[5,32,256]{2,1,0:T(8,128)S(1)}, f32[5,32,256]{2,1,0:T(8,128)S(1)}, u32[]{:S(2)}, u32[]{:S(2)}) collective-permute-start(f32[5,32,256]{2,1,0:T(8,128)S(1)} %get-tuple-element.34), channel_id=1, source_target_pairs={{0,3},{1,2},{2,1},{3,0},{4,7},{5,6},{6,5},{7,4},{8,11},{9,10},{10,... | collective-permute-start | bytes 491528 | tf_op jit(solution)/shard_map/ppermute | solution.py:377
  21.6 7.1 %collective-permute-start.5 = (f32[5,32,256]{2,1,0:T(8,128)S(1)}, f32[5,32,256]{2,1,0:T(8,128)S(1)}, u32[]{:S(2)}, u32[]{:S(2)}) collective-permute-start(f32[5,32,256]{2,1,0:T(8,128)S(1)} %get-tuple-element.30), channel_id=1, source_target_pairs={{0,1},{1,0},{2,3},{3,2},{4,5},{5,4},{6,7},{7,6},{8,9},{9,8},{10,11... | collective-permute-start | bytes 491528 | tf_op jit(solution)/shard_map/ppermute | solution.py:377

commit v6 on v5

--- a/solution.py
+++ b/solution.py
@@ -320,7 +320,7 @@
         compiler_params=limit(4),
         name="edges",
     )(pltpu.with_memory_space_constraint(block, pltpu.HBM))
-    z_pairs, (y_first, y_second) = pairs(count_z, True), pairs(count_y, True)
+    z_pairs, (y_first, y_second) = pairs(count_z, True), pairs(count_y, False)
     halos = [
         [lax.ppermute(edges[2 * g + side], "gz", z_pairs[side]) for side in range(2)]
         for g in range(len(groups))

time: 29.6 us -> 28.3 us (0.956)
  starting transfers between devices: 15.2 us -> 13.3 us
  waiting for transfers between devices: 5.58 us -> 6.07 us
    ppermute x1, starting transfers between devices: 3.43 us -> 0.65 us  [on_device(): yb = lax.ppermute(edges[-2], 'gy', y_second)]
    ppermute x4, waiting for transfers between devices: 0.01 us -> 1.78 us  [on_device(): lax.ppermute(edges[2 * g + side], 'gz', z_pairs[side])]
    ppermute x3, waiting for transfers between devices: 5.57 us -> 4.28 us  [on_device(): received[offset] = lax.ppermute(received[offset], 'gz', swap)]
    ppermute x3, starting transfers between devices: 3.62 us -> 4.57 us  [on_device(): received[offset] = lax.ppermute(received[offset], 'gz', swap)]
  transfers between devices with their start and end apart: 10 -> 10, of which waited for: 2 -> 2; matrix products, arithmetic and copies ran while one was open for 0% -> 0% of each run, Pallas kernels for 18% -> 19%
where the time goes in v6:
time: 28.3 us; the launch traced here: 28.1 us
  starting transfers between devices  13.3 us (47%)
  Pallas kernels  7.97 us (28%)
  waiting for transfers between devices  6.07 us (21%)
  between operations  0.72 us (3%)
    ppermute x4, starting transfers between devices, on_device(): lax.ppermute(edges[2 * g + side], 'gz', z_pairs[side])  4.95 us
    ppermute x3, starting transfers between devices, on_device(): received[offset] = lax.ppermute(received[offset], 'gz', swap)  4.57 us
    ppermute x3, waiting for transfers between devices, on_device(): received[offset] = lax.ppermute(received[offset], 'gz', swap)  4.28 us
    pallas_call x1, Pallas kernels, on_device(): pl.pallas_call(functools.partial(inner_kernel, total_z=total_z), out_shap...  4.15 us
    ppermute x1, starting transfers between devices, on_device(): ya = lax.ppermute(edges[-3], 'gy', y_first)  2.65 us
    pallas_call x1, Pallas kernels, on_device(): pl.pallas_call(functools.partial(edges_kernel, groups=groups, swapped=swa...  1.86 us
    ppermute x4, waiting for transfers between devices, on_device(): lax.ppermute(edges[2 * g + side], 'gz', z_pairs[side])  1.78 us
    pallas_call x2, Pallas kernels, on_device(): pl.pallas_call(functools.partial(outer_kernel, total_z=total_z, offsets=o...  0.82 us
  transfers between devices with their start and end apart: 10, of which 2 were waited for; matrix products, arithmetic and copies ran while one was open for 0% of the time, Pallas kernels for 19%

profile of v6, /device:TPU:0, one launch (start us, length us, event | category | flops | bytes accessed | tf_op | source)
XLA Modules:
  0.0 28.1 jit_solution(13326435659373579535)
XLA Ops:
  0.6 1.9 %edges.1 = (f32[2,2,32,256]{3,2,1,0:T(8,128)S(1)}, f32[2,2,32,256]{3,2,1,0:T(8,128)S(1)}, f32[2,2,32,256]{3,2,1,0:T(8,128)S(1)}, f32[2,2,32,256]{3,2,1,0:T(8,128...) custom-call(f32[16,128,256]{2,1,0:T(8,128)} %x_ref.9), custom_call_target="tpu_custom_call" | custom-call | tf_op jit(solution)/shard_map/edges/pallas_call | solution.py:311
  2.5 0.5 %collective-permute-start.4 = (f32[16,128,128]{2,1,0:T(8,128)S(1)}, f32[16,128,128]{2,1,0:T(8,128)S(1)}, u32[]{:S(2)}, u32[]{:S(2)}) collective-permute-start(f32[16,128,128]{2,1,0:T(8,128)S(1)} %get-tuple-element.23), channel_id=1, source_target_pairs={{0,16},{16,0},{1,17},{17,1},{2,18},{18,2},{3,19},{19,3},{4,20},{20... | collective-permute-start | bytes 3145736 | tf_op jit(solution)/shard_map/ppermute | solution.py:330
  3.0 2.6 %collective-permute-start.2 = (f32[16,2,256]{2,1,0:T(2,128)S(1)}, f32[16,2,256]{2,1,0:T(2,128)S(1)}, u32[]{:S(2)}, u32[]{:S(2)}) collective-permute-start(f32[16,2,256]{2,1,0:T(2,128)S(1)} %get-tuple-element.21), channel_id=1, source_target_pairs={{0,4},{4,0},{8,12},{12,8},{1,5},{5,1},{9,13},{13,9},{2,6},{6,2},{1... | collective-permute-start | bytes 98312 | tf_op jit(solution)/shard_map/ppermute | solution.py:328
  5.7 1.5 %collective-permute-start.6 = (f32[2,2,32,256]{3,2,1,0:T(8,128)S(1)}, f32[2,2,32,256]{3,2,1,0:T(8,128)S(1)}, u32[]{:S(2)}, u32[]{:S(2)}) collective-permute-start(f32[2,2,32,256]{3,2,1,0:T(8,128)S(1)} %get-tuple-element.31), channel_id=1, source_target_pairs={{0,1},{1,0},{2,3},{3,2},{4,5},{5,4},{6,7},{7,6},{8,9},{9,8},{10,11... | collective-permute-start | bytes 393224 | tf_op jit(solution)/shard_map/ppermute | solution.py:325
  7.2 1.5 %collective-permute-start.7 = (f32[2,2,32,256]{3,2,1,0:T(8,128)S(1)}, f32[2,2,32,256]{3,2,1,0:T(8,128)S(1)}, u32[]{:S(2)}, u32[]{:S(2)}) collective-permute-start(f32[2,2,32,256]{3,2,1,0:T(8,128)S(1)} %get-tuple-element.32), channel_id=1, source_target_pairs={{1,2},{2,1},{0,3},{3,0},{5,6},{6,5},{4,7},{7,4},{9,10},{10,9},{8,1... | collective-permute-start | bytes 393224 | tf_op jit(solution)/shard_map/ppermute | solution.py:325
  8.7 1.5 %collective-permute-start = (f32[2,2,32,256]{3,2,1,0:T(8,128)S(1)}, f32[2,2,32,256]{3,2,1,0:T(8,128)S(1)}, u32[]{:S(2)}, u32[]{:S(2)}) collective-permute-start(f32[2,2,32,256]{3,2,1,0:T(8,128)S(1)} %get-tuple-element.19), channel_id=1, source_target_pairs={{0,1},{1,0},{2,3},{3,2},{4,5},{5,4},{6,7},{7,6},{8,9},{9,8},{10,11... | collective-permute-start | bytes 393224 | tf_op jit(solution)/shard_map/ppermute | solution.py:325
  10.1 0.0 collective-permute-done.2.ya_ref
  10.1 0.5 %collective-permute-start.1 = (f32[2,2,32,256]{3,2,1,0:T(8,128)S(1)}, f32[2,2,32,256]{3,2,1,0:T(8,128)S(1)}, u32[]{:S(2)}, u32[]{:S(2)}) collective-permute-start(f32[2,2,32,256]{3,2,1,0:T(8,128)S(1)} %get-tuple-element.20), channel_id=1, source_target_pairs={{1,2},{2,1},{0,3},{3,0},{5,6},{6,5},{4,7},{7,4},{9,10},{10,9},{8,1... | collective-permute-start | bytes 393224 | tf_op jit(solution)/shard_map/ppermute | solution.py:325
  10.6 0.0 collective-permute-done.4.e_ref
  10.6 0.7 %collective-permute-start.3 = (f32[16,2,256]{2,1,0:T(2,128)S(1)}, f32[16,2,256]{2,1,0:T(2,128)S(1)}, u32[]{:S(2)}, u32[]{:S(2)}) collective-permute-start(f32[16,2,256]{2,1,0:T(2,128)S(1)} %get-tuple-element.22), channel_id=1, source_target_pairs={{4,8},{8,4},{0,0},{12,12},{5,9},{9,5},{1,1},{13,13},{6,10},{10,6},... | collective-permute-start | bytes 98312 | tf_op jit(solution)/shard_map/ppermute | solution.py:329
  11.3 4.2 %inner.1 = (f32[5,128,256]{2,1,0:T(8,128)S(1)}, f32[4,2,128,256]{3,2,1,0:T(8,128)S(1)}, f32[16,2,16,256]{3,2,1,0:T(8,128)S(1)}) custom-call(f32[16,128,256]{2,1,0:T(8,128)S(1)} %copy-done, f32[16,128,128]{2,1,0:T(8,128)S(1)} %collective-permute-done.4.e_ref), custom_call_target="tpu_custom_call" | custom-call | flops 52428800 | bytes 4194304 | tf_op jit(solution)/shard_map/inner/pallas_call | solution.py:333
  15.5 0.0 collective-permute-done.3.yb_ref
  15.5 0.4 %rim.1 = (f32[5,128,256]{2,1,0:T(8,128)S(1)}, f32[4,2,128,256]{3,2,1,0:T(8,128)S(1)}) custom-call(f32[16,128,256]{2,1,0:T(8,128)S(1)} %copy-done, f32[16,2,256]{2,1,0:T(2,128)S(1)} %collective-permute-done.2.ya_ref, f32[16,2,256]{2,1,0:T(2,128)S(1)} %collective-permute-done.3.yb_ref, ...), custom_call_target="tpu_custom_call", output_to_operand_aliasing={{0}: (4, {}), {1}: (5, {})} | custom-call | flops 6291456 | bytes 524288 | tf_op jit(solution)/shard_map/rim/pallas_call | solution.py:349
  15.9 0.0 collective-permute-done.7.zb_ref
  15.9 0.4 %outer.3 = (f32[5,32,256]{2,1,0:T(8,128)S(1)}, f32[5,32,256]{2,1,0:T(8,128)S(1)}) custom-call(f32[16,128,256]{2,1,0:T(8,128)S(1)} %copy-done, f32[2,2,32,256]{3,2,1,0:T(8,128)S(1)} %collective-permute-done.6.za_ref, f32[2,2,32,256]{3,2,1,0:T(8,128)S(1)} %collective-permute-done.7.zb_ref, f32[5,128,256]{2,1,0:T(8,128)S(1)} %get-tuple-element.27.image_ref, ...), custom_call_target="tpu_custom_call" | custom-call | tf_op jit(solution)/shard_map/outer/pallas_call | solution.py:364
  16.3 1.6 %collective-permute-start.8 = (f32[5,32,256]{2,1,0:T(8,128)S(1)}, f32[5,32,256]{2,1,0:T(8,128)S(1)}, u32[]{:S(2)}, u32[]{:S(2)}) collective-permute-start(f32[5,32,256]{2,1,0:T(8,128)S(1)} %get-tuple-element.33), channel_id=1, source_target_pairs={{0,2},{1,3},{2,0},{3,1},{4,6},{5,7},{6,4},{7,5},{8,10},{9,11},{10,... | collective-permute-start | bytes 491528 | tf_op jit(solution)/shard_map/ppermute | solution.py:377
  17.9 1.4 %collective-permute-start.9 = (f32[5,32,256]{2,1,0:T(8,128)S(1)}, f32[5,32,256]{2,1,0:T(8,128)S(1)}, u32[]{:S(2)}, u32[]{:S(2)}) collective-permute-start(f32[5,32,256]{2,1,0:T(8,128)S(1)} %get-tuple-element.34), channel_id=1, source_target_pairs={{0,3},{1,2},{2,1},{3,0},{4,7},{5,6},{6,5},{7,4},{8,11},{9,10},{10,... | collective-permute-start | bytes 491528 | tf_op jit(solution)/shard_map/ppermute | solution.py:377
  19.4 1.8 %collective-permute-done.1.zb_ref = f32[2,2,32,256]{3,2,1,0:T(8,128)S(1)} collective-permute-done((f32[2,2,32,256]{3,2,1,0:T(8,128)S(1)}, f32[2,2,32,256]{3,2,1,0:T(8,128)S(1)}, u32[]{:S(2)}, u32[]{:S(2)}) %collective-permute-start.1) | collective-permute-done | bytes 131104 | tf_op jit(solution)/shard_map/ppermute | solution.py:325
  21.1 0.4 %outer.2 = (f32[5,32,256]{2,1,0:T(8,128)S(1)}, f32[5,32,256]{2,1,0:T(8,128)S(1)}) custom-call(f32[16,128,256]{2,1,0:T(8,128)S(1)} %copy-done, f32[2,2,32,256]{3,2,1,0:T(8,128)S(1)} %collective-permute-done.za_ref, f32[2,2,32,256]{3,2,1,0:T(8,128)S(1)} %collective-permute-done.1.zb_ref, f32[5,128,256]{2,1,0:T(8,128)S(1)} %get-tuple-element.27.image_ref, ...), custom_call_target="tpu_custom_call" | custom-call | tf_op jit(solution)/shard_map/outer/pallas_call | solution.py:364
  21.5 1.6 %collective-permute-start.5 = (f32[5,32,256]{2,1,0:T(8,128)S(1)}, f32[5,32,256]{2,1,0:T(8,128)S(1)}, u32[]{:S(2)}, u32[]{:S(2)}) collective-permute-start(f32[5,32,256]{2,1,0:T(8,128)S(1)} %get-tuple-element.30), channel_id=1, source_target_pairs={{0,1},{1,0},{2,3},{3,2},{4,5},{5,4},{6,7},{7,6},{8,9},{9,8},{10,11... | collective-permute-start | bytes 491528 | tf_op jit(solution)/shard_map/ppermute | solution.py:377
  23.1 4.3 %collective-permute-done.8.two_ref = f32[5,32,256]{2,1,0:T(8,128)S(1)} collective-permute-done((f32[5,32,256]{2,1,0:T(8,128)S(1)}, f32[5,32,256]{2,1,0:T(8,128)S(1)}, u32[]{:S(2)}, u32[]{:S(2)}) %collective-permute-start.8) | collective-permute-done | bytes 163872 | tf_op jit(solution)/shard_map/ppermute | solution.py:377
  27.4 0.0 collective-permute-done.9.three_ref
  27.4 0.0 collective-permute-done.5.one_ref
  27.4 0.7 %blend.1 = (f32[3,32,256]{2,1,0:T(8,128)}, f32[32,256]{1,0:T(8,128)}, f32[32,256]{1,0:T(8,128)}) custom-call(f32[5,32,256]{2,1,0:T(8,128)S(1)} %get-tuple-element.29.own_ref, f32[5,32,256]{2,1,0:T(8,128)S(1)} %collective-permute-done.5.one_ref, f32[5,32,256]{2,1,0:T(8,128)S(1)} %collective-permute-done.8.two_ref, ...), custom_call_target="tpu_custom_call" | custom-call | tf_op jit(solution)/shard_map/blend/pallas_call | solution.py:378
  (4 shorter events, 0.0 us)
Async XLA Ops:
  0.6 10.7 %copy-start = (f32[16,128,256]{2,1,0:T(8,128)S(1)}, f32[16,128,256]{2,1,0:T(8,128)}, u32[]{:S(2)}) copy-start(f32[16,128,256]{2,1,0:T(8,128)} %x_ref.9) | copy-start | bytes 6291460
  2.5 8.1 %collective-permute-start.4 = (f32[16,128,128]{2,1,0:T(8,128)S(1)}, f32[16,128,128]{2,1,0:T(8,128)S(1)}, u32[]{:S(2)}, u32[]{:S(2)}) collective-permute-start(f32[16,128,128]{2,1,0:T(8,128)S(1)} %get-tuple-element.23), channel_id=1, source_target_pairs={{0,16},{16,0},{1,17},{17,1},{2,18},{18,2},{3,19},{19,3},{4,20},{20... | collective-permute-start | bytes 3145736 | tf_op jit(solution)/shard_map/ppermute | solution.py:330
  3.0 7.1 %collective-permute-start.2 = (f32[16,2,256]{2,1,0:T(2,128)S(1)}, f32[16,2,256]{2,1,0:T(2,128)S(1)}, u32[]{:S(2)}, u32[]{:S(2)}) collective-permute-start(f32[16,2,256]{2,1,0:T(2,128)S(1)} %get-tuple-element.21), channel_id=1, source_target_pairs={{0,4},{4,0},{8,12},{12,8},{1,5},{5,1},{9,13},{13,9},{2,6},{6,2},{1... | collective-permute-start | bytes 98312 | tf_op jit(solution)/shard_map/ppermute | solution.py:328
  5.7 10.2 %collective-permute-start.6 = (f32[2,2,32,256]{3,2,1,0:T(8,128)S(1)}, f32[2,2,32,256]{3,2,1,0:T(8,128)S(1)}, u32[]{:S(2)}, u32[]{:S(2)}) collective-permute-start(f32[2,2,32,256]{3,2,1,0:T(8,128)S(1)} %get-tuple-element.31), channel_id=1, source_target_pairs={{0,1},{1,0},{2,3},{3,2},{4,5},{5,4},{6,7},{7,6},{8,9},{9,8},{10,11... | collective-permute-start | bytes 393224 | tf_op jit(solution)/shard_map/ppermute | solution.py:325
  7.2 8.7 %collective-permute-start.7 = (f32[2,2,32,256]{3,2,1,0:T(8,128)S(1)}, f32[2,2,32,256]{3,2,1,0:T(8,128)S(1)}, u32[]{:S(2)}, u32[]{:S(2)}) collective-permute-start(f32[2,2,32,256]{3,2,1,0:T(8,128)S(1)} %get-tuple-element.32), channel_id=1, source_target_pairs={{1,2},{2,1},{0,3},{3,0},{5,6},{6,5},{4,7},{7,4},{9,10},{10,9},{8,1... | collective-permute-start | bytes 393224 | tf_op jit(solution)/shard_map/ppermute | solution.py:325
  8.7 10.7 %collective-permute-start = (f32[2,2,32,256]{3,2,1,0:T(8,128)S(1)}, f32[2,2,32,256]{3,2,1,0:T(8,128)S(1)}, u32[]{:S(2)}, u32[]{:S(2)}) collective-permute-start(f32[2,2,32,256]{3,2,1,0:T(8,128)S(1)} %get-tuple-element.19), channel_id=1, source_target_pairs={{0,1},{1,0},{2,3},{3,2},{4,5},{5,4},{6,7},{7,6},{8,9},{9,8},{10,11... | collective-permute-start | bytes 393224 | tf_op jit(solution)/shard_map/ppermute | solution.py:325
  10.1 11.0 %collective-permute-start.1 = (f32[2,2,32,256]{3,2,1,0:T(8,128)S(1)}, f32[2,2,32,256]{3,2,1,0:T(8,128)S(1)}, u32[]{:S(2)}, u32[]{:S(2)}) collective-permute-start(f32[2,2,32,256]{3,2,1,0:T(8,128)S(1)} %get-tuple-element.20), channel_id=1, source_target_pairs={{1,2},{2,1},{0,3},{3,0},{5,6},{6,5},{4,7},{7,4},{9,10},{10,9},{8,1... | collective-permute-start | bytes 393224 | tf_op jit(solution)/shard_map/ppermute | solution.py:325
  10.6 4.8 %collective-permute-start.3 = (f32[16,2,256]{2,1,0:T(2,128)S(1)}, f32[16,2,256]{2,1,0:T(2,128)S(1)}, u32[]{:S(2)}, u32[]{:S(2)}) collective-permute-start(f32[16,2,256]{2,1,0:T(2,128)S(1)} %get-tuple-element.22), channel_id=1, source_target_pairs={{4,8},{8,4},{0,0},{12,12},{5,9},{9,5},{1,1},{13,13},{6,10},{10,6},... | collective-permute-start | bytes 98312 | tf_op jit(solution)/shard_map/ppermute | solution.py:329
  16.3 11.0 %collective-permute-start.8 = (f32[5,32,256]{2,1,0:T(8,128)S(1)}, f32[5,32,256]{2,1,0:T(8,128)S(1)}, u32[]{:S(2)}, u32[]{:S(2)}) collective-permute-start(f32[5,32,256]{2,1,0:T(8,128)S(1)} %get-tuple-element.33), channel_id=1, source_target_pairs={{0,2},{1,3},{2,0},{3,1},{4,6},{5,7},{6,4},{7,5},{8,10},{9,11},{10,... | collective-permute-start | bytes 491528 | tf_op jit(solution)/shard_map/ppermute | solution.py:377
  17.9 9.4 %collective-permute-start.9 = (f32[5,32,256]{2,1,0:T(8,128)S(1)}, f32[5,32,256]{2,1,0:T(8,128)S(1)}, u32[]{:S(2)}, u32[]{:S(2)}) collective-permute-start(f32[5,32,256]{2,1,0:T(8,128)S(1)} %get-tuple-element.34), channel_id=1, source_target_pairs={{0,3},{1,2},{2,1},{3,0},{4,7},{5,6},{6,5},{7,4},{8,11},{9,10},{10,... | collective-permute-start | bytes 491528 | tf_op jit(solution)/shard_map/ppermute | solution.py:377
  21.5 5.8 %collective-permute-start.5 = (f32[5,32,256]{2,1,0:T(8,128)S(1)}, f32[5,32,256]{2,1,0:T(8,128)S(1)}, u32[]{:S(2)}, u32[]{:S(2)}) collective-permute-start(f32[5,32,256]{2,1,0:T(8,128)S(1)} %get-tuple-element.30), channel_id=1, source_target_pairs={{0,1},{1,0},{2,3},{3,2},{4,5},{5,4},{6,7},{7,6},{8,9},{9,8},{10,11... | collective-permute-start | bytes 491528 | tf_op jit(solution)/shard_map/ppermute | solution.py:377

commit v7 on v6

--- a/solution.py
+++ b/solution.py
@@ -47,7 +47,7 @@
     return at_z ^ offset if swapped else offset
 
 
-def edges_kernel(x_ref, *refs, groups, swapped, count_z):
+def edges_kernel(x_ref, *refs, sends, swapped, count_z):
     z_refs, (ya_ref, yb_ref, e_ref, top_ref, bottom_ref, sems) = refs[:-6], refs[-6:]
     cells_z, rows, cols = x_ref.shape
     at_x, at_y, at_z = place()
@@ -62,12 +62,11 @@
         (jnp.where(even_z, before, after), jnp.where(even_z, 0, high)),
     )
     moves = []
-    for group, offsets in enumerate(groups):
-        for side, (peer, layer) in enumerate(sides):
-            for slot, offset in enumerate(offsets):
-                row = pl.multiple_of(block_of(offset, swapped, peer) * piece, 8)
-                source = x_ref.at[pl.ds(layer, HALO), pl.ds(row, piece)]
-                moves.append((source, z_refs[2 * group + side].at[slot]))
+    for z_ref, (side, offsets) in zip(z_refs, sends):
+        peer, layer = sides[side]
+        for slot, offset in enumerate(offsets):
+            row = pl.multiple_of(block_of(offset, swapped, peer) * piece, 8)
+            moves.append((x_ref.at[pl.ds(layer, HALO), pl.ds(row, piece)], z_ref.at[slot]))
     moves += [
         (x_ref.at[:, pl.ds(0, RIM)], top_ref),
         (x_ref.at[:, pl.ds(rows - RIM, RIM)], bottom_ref),
@@ -202,7 +201,7 @@
             image_ref[channel, to] = value
 
 
-def outer_kernel(x_ref, za_ref, zb_ref, image_ref, part_ref, *refs, total_z, offsets, swapped):
+def outer_kernel(x_ref, za_ref, zb_ref, image_ref, part_ref, *refs, total_z, offsets, swapped, base):
     cells_z, _, cols = x_ref.shape
     depth_step = 2.0 / total_z
     at_z = place()[2]
@@ -218,10 +217,10 @@
         at = pl.ds(pl.multiple_of(block * piece + start, 8), chunk)
 
         def before(layer):
-            return jnp.where(at_z > 0, jnp.where(even, zb_ref[out, layer, part], za_ref[out, layer, part]), none)
+            return jnp.where(at_z > 0, jnp.where(even, zb_ref[out, layer, part], za_ref[base + out, layer, part]), none)
 
         def after(layer):
-            return jnp.where(at_z < last_z, jnp.where(even, za_ref[out, layer, part], zb_ref[out, layer, part]), none)
+            return jnp.where(at_z < last_z, jnp.where(even, za_ref[base + out, layer, part], zb_ref[out, layer, part]), none)
 
         f = [x_ref[k, at] for k in range(4)]
         b = [x_ref[cells_z - 4 + k, at] for k in range(4)]
@@ -283,11 +282,18 @@
     put(image, colour_ref, depth_ref, clear_ref)
 
 
-def pairs(count, closed):
-    ends = [(0, count - 1), (count - 1, 0)] if closed else [(0, 0), (count - 1, count - 1)]
-    first = [(i, i ^ 1) for i in range(count)]
-    second = [(i, (i - 1 if i % 2 == 0 else i + 1)) for i in range(1, count - 1)]
-    return first, second + ends
+def swap_pairs(value, axis, second):
+    count = lax.axis_size(axis)
+    if not second:
+        return lax.ppermute(value, axis, [(i, i ^ 1) for i in range(count)])
+    pairs = []
+    for core in range(2):
+        for i in range(count):
+            peer = i - 1 if i % 2 == 0 else i + 1
+            inside = 0 <= peer < count
+            to = core * count + peer if inside else (1 - core) * count + i
+            pairs.append((core * count + i, to))
+    return lax.ppermute(value, ("gx", axis), pairs)
 
 
 def on_device(block):
@@ -307,26 +313,26 @@
 
     swapped = count_z == 4
     groups = ((2, 3), (1, 0)) if swapped else (tuple(range(count_z)),)
-    payloads = [shaped(len(g), HALO, piece, cols) for g in groups for _ in range(2)]
+    every = sum(groups, ())
+    sends = [(0, every)] + [(1, g) for g in groups]
+    payloads = [shaped(len(g), HALO, piece, cols) for _, g in sends]
     edges = pl.pallas_call(
-        functools.partial(edges_kernel, groups=groups, swapped=swapped, count_z=count_z),
+        functools.partial(edges_kernel, sends=sends, swapped=swapped, count_z=count_z),
         out_shape=payloads
         + [shaped(cells_z, HALO, cols)] * 2
         + [shaped(cells_z, rows, strip)],
         in_specs=[pl.BlockSpec(memory_space=pltpu.HBM)],
         out_specs=[vmem] * (len(payloads) + 3),
         scratch_shapes=[pltpu.VMEM((cells_z, RIM, cols), f32)] * 2
-        + [pltpu.SemaphoreType.DMA((2 * sum(len(g) for g in groups) + 3,))],
+        + [pltpu.SemaphoreType.DMA((2 * len(every) + 3,))],
         compiler_params=limit(4),
         name="edges",
     )(pltpu.with_memory_space_constraint(block, pltpu.HBM))
-    z_pairs, (y_first, y_second) = pairs(count_z, True), pairs(count_y, False)
-    halos = [
-        [lax.ppermute(edges[2 * g + side], "gz", z_pairs[side]) for side in range(2)]
-        for g in range(len(groups))
+    whole, *cut = [
+        swap_pairs(value, "gz", side) for value, (side, _) in zip(edges, sends)
     ]
-    ya = lax.ppermute(edges[-3], "gy", y_first)
-    yb = lax.ppermute(edges[-2], "gy", y_second)
+    ya = swap_pairs(edges[-3], "gy", False)
+    yb = swap_pairs(edges[-2], "gy", True)
     edge = lax.ppermute(edges[-1], "gx", [(0, 1), (1, 0)])
 
     image_shape, part_shape = shaped(5, rows, cols), shaped(4, 2, rows, cols)
@@ -360,9 +366,10 @@
     )(block, ya, yb, rim, image, part)
 
     received = {}
-    for offsets, (za, zb) in zip(groups, halos):
+    for offsets, own in zip(groups, cut):
+        za, zb = whole, own
         made = pl.pallas_call(
-            functools.partial(outer_kernel, total_z=total_z, offsets=offsets, swapped=swapped),
+            functools.partial(outer_kernel, total_z=total_z, offsets=offsets, swapped=swapped, base=every.index(offsets[0])),
             out_shape=[shaped(5, piece, cols)] * len(offsets),
             in_specs=[vmem] * 5,
             out_specs=[vmem] * len(offsets),

time: 28.3 us -> 27.4 us (0.968)
  starting transfers between devices: 13.3 us -> 12.9 us
  waiting for transfers between devices: 6.07 us -> 5.67 us
    ppermute x6 -> x5, starting transfers between devices: 8.25 us -> 4.65 us  [the longest x2 4.14 us: swap_pairs(): return lax.ppermute(value, axis, [(i, i ^ 1) for i in range(count)])]
    ppermute x3, starting transfers between devices: 4.57 us -> 7.73 us  [on_device(): received[offset] = lax.ppermute(received[offset], 'gz', swap)]
    ppermute x6 -> x5, waiting for transfers between devices: 1.79 us -> 0.45 us  [the longest x2 0.44 us: swap_pairs(): return lax.ppermute(value, axis, [(i, i ^ 1) for i in range(count)])]
    ppermute x3, waiting for transfers between devices: 4.28 us -> 5.21 us  [on_device(): received[offset] = lax.ppermute(received[offset], 'gz', swap)]
  transfers between devices with their start and end apart: 10 -> 9, of which waited for: 2 -> 4; matrix products, arithmetic and copies ran while one was open for 0% -> 0% of each run, Pallas kernels for 19% -> 20%
where the time goes in v7:
time: 27.4 us; the launch traced here: 27.2 us
  starting transfers between devices  12.9 us (47%)
  Pallas kernels  7.95 us (29%)
  waiting for transfers between devices  5.67 us (21%)
  between operations  0.7 us (3%)
    ppermute x3, starting transfers between devices, on_device(): received[offset] = lax.ppermute(received[offset], 'gz', swap)  7.73 us
    ppermute x3, waiting for transfers between devices, on_device(): received[offset] = lax.ppermute(received[offset], 'gz', swap)  5.21 us
    pallas_call x1, Pallas kernels, on_device(): pl.pallas_call(functools.partial(inner_kernel, total_z=total_z), out_shap...  4.15 us
    ppermute x2, starting transfers between devices, swap_pairs(): return lax.ppermute(value, axis, [(i, i ^ 1) for i in range(count)])  4.14 us
    pallas_call x1, Pallas kernels, on_device(): pl.pallas_call(functools.partial(edges_kernel, sends=sends, swapped=swapp...  1.86 us
    pallas_call x2, Pallas kernels, on_device(): pl.pallas_call(functools.partial(outer_kernel, total_z=total_z, offsets=o...  0.81 us
    pallas_call x1, Pallas kernels, on_device(): pl.pallas_call(blend_four, out_shape=out_shape, in_specs=[vmem] * 4, out_...  0.72 us
  transfers between devices with their start and end apart: 9, of which 4 were waited for; matrix products, arithmetic and copies ran while one was open for 0% of the time, Pallas kernels for 20%

profile of v7, /device:TPU:0, one launch (start us, length us, event | category | flops | bytes accessed | tf_op | source)
XLA Modules:
  0.0 27.2 jit_solution(5950754769534477088)
XLA Ops:
  0.6 1.9 %edges.1 = (f32[4,2,32,256]{3,2,1,0:T(8,128)S(1)}, f32[2,2,32,256]{3,2,1,0:T(8,128)S(1)}, f32[2,2,32,256]{3,2,1,0:T(8,128)S(1)}, f32[16,2,256]{2,1,0:T(2,128)S(1...) custom-call(f32[16,128,256]{2,1,0:T(8,128)} %x_ref.9), custom_call_target="tpu_custom_call" | custom-call | tf_op jit(solution)/shard_map/edges/pallas_call | solution.py:319
  2.5 0.5 %collective-permute-start.4 = (f32[16,128,128]{2,1,0:T(8,128)S(1)}, f32[16,128,128]{2,1,0:T(8,128)S(1)}, u32[]{:S(2)}, u32[]{:S(2)}) collective-permute-start(f32[16,128,128]{2,1,0:T(8,128)S(1)} %get-tuple-element.22), channel_id=1, source_target_pairs={{0,16},{16,0},{1,17},{17,1},{2,18},{18,2},{3,19},{19,3},{4,20},{20... | collective-permute-start | bytes 3145736 | tf_op jit(solution)/shard_map/ppermute | solution.py:336
  3.0 2.6 %collective-permute-start = (f32[4,2,32,256]{3,2,1,0:T(8,128)S(1)}, f32[4,2,32,256]{3,2,1,0:T(8,128)S(1)}, u32[]{:S(2)}, u32[]{:S(2)}) collective-permute-start(f32[4,2,32,256]{3,2,1,0:T(8,128)S(1)} %get-tuple-element.18), channel_id=1, source_target_pairs={{0,1},{1,0},{2,3},{3,2},{4,5},{5,4},{6,7},{7,6},{8,9},{9,8},{10,11... | collective-permute-start | bytes 786440 | tf_op jit(solution)/shard_map/ppermute | solution.py:288
  5.6 0.2 collective-permute-start.6
  5.8 0.3 %collective-permute-start.1 = (f32[2,2,32,256]{3,2,1,0:T(8,128)S(1)}, f32[2,2,32,256]{3,2,1,0:T(8,128)S(1)}, u32[]{:S(2)}, u32[]{:S(2)}) collective-permute-start(f32[2,2,32,256]{3,2,1,0:T(8,128)S(1)} %get-tuple-element.19), channel_id=1, source_target_pairs={{0,16},{1,2},{2,1},{3,19},{16,0},{17,18},{18,17},{19,3},{4,20},{5,... | collective-permute-start | bytes 393224 | tf_op jit(solution)/shard_map/ppermute | solution.py:296
  6.1 1.6 %collective-permute-start.2 = (f32[16,2,256]{2,1,0:T(2,128)S(1)}, f32[16,2,256]{2,1,0:T(2,128)S(1)}, u32[]{:S(2)}, u32[]{:S(2)}) collective-permute-start(f32[16,2,256]{2,1,0:T(2,128)S(1)} %get-tuple-element.20), channel_id=1, source_target_pairs={{0,4},{4,0},{8,12},{12,8},{1,5},{5,1},{9,13},{13,9},{2,6},{6,2},{1... | collective-permute-start | bytes 98312 | tf_op jit(solution)/shard_map/ppermute | solution.py:288
  7.7 0.0 collective-permute-done.4.e_ref
  7.7 0.0 collective-permute-start.3
  7.7 4.2 %inner.1 = (f32[5,128,256]{2,1,0:T(8,128)S(1)}, f32[4,2,128,256]{3,2,1,0:T(8,128)S(1)}, f32[16,2,16,256]{3,2,1,0:T(8,128)S(1)}) custom-call(f32[16,128,256]{2,1,0:T(8,128)S(1)} %copy-done, f32[16,128,128]{2,1,0:T(8,128)S(1)} %collective-permute-done.4.e_ref), custom_call_target="tpu_custom_call" | custom-call | flops 52428800 | bytes 4194304 | tf_op jit(solution)/shard_map/inner/pallas_call | solution.py:339
  11.8 0.0 collective-permute-done.2.ya_ref
  11.9 0.0 collective-permute-done.3.yb_ref
  11.9 0.4 %rim.1 = (f32[5,128,256]{2,1,0:T(8,128)S(1)}, f32[4,2,128,256]{3,2,1,0:T(8,128)S(1)}) custom-call(f32[16,128,256]{2,1,0:T(8,128)S(1)} %copy-done, f32[16,2,256]{2,1,0:T(2,128)S(1)} %collective-permute-done.2.ya_ref, f32[16,2,256]{2,1,0:T(2,128)S(1)} %collective-permute-done.3.yb_ref, ...), custom_call_target="tpu_custom_call", output_to_operand_aliasing={{0}: (4, {}), {1}: (5, {})} | custom-call | flops 6291456 | bytes 524288 | tf_op jit(solution)/shard_map/rim/pallas_call | solution.py:355
  12.3 0.0 collective-permute-done.6.zb_ref
  12.3 0.4 %collective-permute-done.za_ref = f32[4,2,32,256]{3,2,1,0:T(8,128)S(1)} collective-permute-done((f32[4,2,32,256]{3,2,1,0:T(8,128)S(1)}, f32[4,2,32,256]{3,2,1,0:T(8,128)S(1)}, u32[]{:S(2)}, u32[]{:S(2)}) %collective-permute-start) | collective-permute-done | bytes 262176 | tf_op jit(solution)/shard_map/ppermute | solution.py:288
  12.7 0.4 %outer.3 = (f32[5,32,256]{2,1,0:T(8,128)S(1)}, f32[5,32,256]{2,1,0:T(8,128)S(1)}) custom-call(f32[16,128,256]{2,1,0:T(8,128)S(1)} %copy-done, f32[4,2,32,256]{3,2,1,0:T(8,128)S(1)} %collective-permute-done.za_ref, f32[2,2,32,256]{3,2,1,0:T(8,128)S(1)} %collective-permute-done.6.zb_ref, f32[5,128,256]{2,1,0:T(8,128)S(1)} %get-tuple-element.26.image_ref, ...), custom_call_target="tpu_custom_call" | custom-call | tf_op jit(solution)/shard_map/outer/pallas_call | solution.py:371
  13.2 4.3 %collective-permute-start.7 = (f32[5,32,256]{2,1,0:T(8,128)S(1)}, f32[5,32,256]{2,1,0:T(8,128)S(1)}, u32[]{:S(2)}, u32[]{:S(2)}) collective-permute-start(f32[5,32,256]{2,1,0:T(8,128)S(1)} %get-tuple-element.31), channel_id=1, source_target_pairs={{0,2},{1,3},{2,0},{3,1},{4,6},{5,7},{6,4},{7,5},{8,10},{9,11},{10,... | collective-permute-start | bytes 491528 | tf_op jit(solution)/shard_map/ppermute | solution.py:384
  17.5 2.9 %collective-permute-start.8 = (f32[5,32,256]{2,1,0:T(8,128)S(1)}, f32[5,32,256]{2,1,0:T(8,128)S(1)}, u32[]{:S(2)}, u32[]{:S(2)}) collective-permute-start(f32[5,32,256]{2,1,0:T(8,128)S(1)} %get-tuple-element.32), channel_id=1, source_target_pairs={{0,3},{1,2},{2,1},{3,0},{4,7},{5,6},{6,5},{7,4},{8,11},{9,10},{10,... | collective-permute-start | bytes 491528 | tf_op jit(solution)/shard_map/ppermute | solution.py:384
  20.4 0.0 collective-permute-done.1.zb_ref
  20.4 0.4 %outer.2 = (f32[5,32,256]{2,1,0:T(8,128)S(1)}, f32[5,32,256]{2,1,0:T(8,128)S(1)}) custom-call(f32[16,128,256]{2,1,0:T(8,128)S(1)} %copy-done, f32[4,2,32,256]{3,2,1,0:T(8,128)S(1)} %collective-permute-done.za_ref, f32[2,2,32,256]{3,2,1,0:T(8,128)S(1)} %collective-permute-done.1.zb_ref, f32[5,128,256]{2,1,0:T(8,128)S(1)} %get-tuple-element.26.image_ref, ...), custom_call_target="tpu_custom_call" | custom-call | tf_op jit(solution)/shard_map/outer/pallas_call | solution.py:371
  20.8 0.5 %collective-permute-start.5 = (f32[5,32,256]{2,1,0:T(8,128)S(1)}, f32[5,32,256]{2,1,0:T(8,128)S(1)}, u32[]{:S(2)}, u32[]{:S(2)}) collective-permute-start(f32[5,32,256]{2,1,0:T(8,128)S(1)} %get-tuple-element.29), channel_id=1, source_target_pairs={{0,1},{1,0},{2,3},{3,2},{4,5},{5,4},{6,7},{7,6},{8,9},{9,8},{10,11... | collective-permute-start | bytes 491528 | tf_op jit(solution)/shard_map/ppermute | solution.py:384
  21.3 3.4 %collective-permute-done.7.two_ref = f32[5,32,256]{2,1,0:T(8,128)S(1)} collective-permute-done((f32[5,32,256]{2,1,0:T(8,128)S(1)}, f32[5,32,256]{2,1,0:T(8,128)S(1)}, u32[]{:S(2)}, u32[]{:S(2)}) %collective-permute-start.7) | collective-permute-done | bytes 163872 | tf_op jit(solution)/shard_map/ppermute | solution.py:384
  24.7 0.8 %collective-permute-done.8.three_ref = f32[5,32,256]{2,1,0:T(8,128)S(1)} collective-permute-done((f32[5,32,256]{2,1,0:T(8,128)S(1)}, f32[5,32,256]{2,1,0:T(8,128)S(1)}, u32[]{:S(2)}, u32[]{:S(2)}) %collective-permute-start.8) | collective-permute-done | bytes 163872 | tf_op jit(solution)/shard_map/ppermute | solution.py:384
  25.5 1.0 %collective-permute-done.5.one_ref = f32[5,32,256]{2,1,0:T(8,128)S(1)} collective-permute-done((f32[5,32,256]{2,1,0:T(8,128)S(1)}, f32[5,32,256]{2,1,0:T(8,128)S(1)}, u32[]{:S(2)}, u32[]{:S(2)}) %collective-permute-start.5) | collective-permute-done | bytes 163872 | tf_op jit(solution)/shard_map/ppermute | solution.py:384
  26.5 0.7 %blend.1 = (f32[3,32,256]{2,1,0:T(8,128)}, f32[32,256]{1,0:T(8,128)}, f32[32,256]{1,0:T(8,128)}) custom-call(f32[5,32,256]{2,1,0:T(8,128)S(1)} %get-tuple-element.28.own_ref, f32[5,32,256]{2,1,0:T(8,128)S(1)} %collective-permute-done.5.one_ref, f32[5,32,256]{2,1,0:T(8,128)S(1)} %collective-permute-done.7.two_ref, ...), custom_call_target="tpu_custom_call" | custom-call | tf_op jit(solution)/shard_map/blend/pallas_call | solution.py:385
  (2 shorter events, 0.0 us)
Async XLA Ops:
  0.6 7.1 %copy-start = (f32[16,128,256]{2,1,0:T(8,128)S(1)}, f32[16,128,256]{2,1,0:T(8,128)}, u32[]{:S(2)}) copy-start(f32[16,128,256]{2,1,0:T(8,128)} %x_ref.9) | copy-start | bytes 6291460
  2.5 5.2 %collective-permute-start.4 = (f32[16,128,128]{2,1,0:T(8,128)S(1)}, f32[16,128,128]{2,1,0:T(8,128)S(1)}, u32[]{:S(2)}, u32[]{:S(2)}) collective-permute-start(f32[16,128,128]{2,1,0:T(8,128)S(1)} %get-tuple-element.22), channel_id=1, source_target_pairs={{0,16},{16,0},{1,17},{17,1},{2,18},{18,2},{3,19},{19,3},{4,20},{20... | collective-permute-start | bytes 3145736 | tf_op jit(solution)/shard_map/ppermute | solution.py:336
  3.0 9.7 %collective-permute-start = (f32[4,2,32,256]{3,2,1,0:T(8,128)S(1)}, f32[4,2,32,256]{3,2,1,0:T(8,128)S(1)}, u32[]{:S(2)}, u32[]{:S(2)}) collective-permute-start(f32[4,2,32,256]{3,2,1,0:T(8,128)S(1)} %get-tuple-element.18), channel_id=1, source_target_pairs={{0,1},{1,0},{2,3},{3,2},{4,5},{5,4},{6,7},{7,6},{8,9},{9,8},{10,11... | collective-permute-start | bytes 786440 | tf_op jit(solution)/shard_map/ppermute | solution.py:288
  5.6 6.7 %collective-permute-start.6 = (f32[2,2,32,256]{3,2,1,0:T(8,128)S(1)}, f32[2,2,32,256]{3,2,1,0:T(8,128)S(1)}, u32[]{:S(2)}, u32[]{:S(2)}) collective-permute-start(f32[2,2,32,256]{3,2,1,0:T(8,128)S(1)} %get-tuple-element.30), channel_id=1, source_target_pairs={{0,16},{1,2},{2,1},{3,19},{16,0},{17,18},{18,17},{19,3},{4,20},{5,... | collective-permute-start | bytes 393224 | tf_op jit(solution)/shard_map/ppermute | solution.py:296
  5.8 14.6 %collective-permute-start.1 = (f32[2,2,32,256]{3,2,1,0:T(8,128)S(1)}, f32[2,2,32,256]{3,2,1,0:T(8,128)S(1)}, u32[]{:S(2)}, u32[]{:S(2)}) collective-permute-start(f32[2,2,32,256]{3,2,1,0:T(8,128)S(1)} %get-tuple-element.19), channel_id=1, source_target_pairs={{0,16},{1,2},{2,1},{3,19},{16,0},{17,18},{18,17},{19,3},{4,20},{5,... | collective-permute-start | bytes 393224 | tf_op jit(solution)/shard_map/ppermute | solution.py:296
  6.1 5.7 %collective-permute-start.2 = (f32[16,2,256]{2,1,0:T(2,128)S(1)}, f32[16,2,256]{2,1,0:T(2,128)S(1)}, u32[]{:S(2)}, u32[]{:S(2)}) collective-permute-start(f32[16,2,256]{2,1,0:T(2,128)S(1)} %get-tuple-element.20), channel_id=1, source_target_pairs={{0,4},{4,0},{8,12},{12,8},{1,5},{5,1},{9,13},{13,9},{2,6},{6,2},{1... | collective-permute-start | bytes 98312 | tf_op jit(solution)/shard_map/ppermute | solution.py:288
  7.7 4.2 %collective-permute-start.3 = (f32[16,2,256]{2,1,0:T(2,128)S(1)}, f32[16,2,256]{2,1,0:T(2,128)S(1)}, u32[]{:S(2)}, u32[]{:S(2)}) collective-permute-start(f32[16,2,256]{2,1,0:T(2,128)S(1)} %get-tuple-element.21), channel_id=1, source_target_pairs={{0,16},{4,8},{8,4},{12,28},{16,0},{20,24},{24,20},{28,12},{1,17},{... | collective-permute-start | bytes 98312 | tf_op jit(solution)/shard_map/ppermute | solution.py:296
  13.2 11.6 %collective-permute-start.7 = (f32[5,32,256]{2,1,0:T(8,128)S(1)}, f32[5,32,256]{2,1,0:T(8,128)S(1)}, u32[]{:S(2)}, u32[]{:S(2)}) collective-permute-start(f32[5,32,256]{2,1,0:T(8,128)S(1)} %get-tuple-element.31), channel_id=1, source_target_pairs={{0,2},{1,3},{2,0},{3,1},{4,6},{5,7},{6,4},{7,5},{8,10},{9,11},{10,... | collective-permute-start | bytes 491528 | tf_op jit(solution)/shard_map/ppermute | solution.py:384
  17.5 8.0 %collective-permute-start.8 = (f32[5,32,256]{2,1,0:T(8,128)S(1)}, f32[5,32,256]{2,1,0:T(8,128)S(1)}, u32[]{:S(2)}, u32[]{:S(2)}) collective-permute-start(f32[5,32,256]{2,1,0:T(8,128)S(1)} %get-tuple-element.32), channel_id=1, source_target_pairs={{0,3},{1,2},{2,1},{3,0},{4,7},{5,6},{6,5},{7,4},{8,11},{9,10},{10,... | collective-permute-start | bytes 491528 | tf_op jit(solution)/shard_map/ppermute | solution.py:384
  20.8 5.7 %collective-permute-start.5 = (f32[5,32,256]{2,1,0:T(8,128)S(1)}, f32[5,32,256]{2,1,0:T(8,128)S(1)}, u32[]{:S(2)}, u32[]{:S(2)}) collective-permute-start(f32[5,32,256]{2,1,0:T(8,128)S(1)} %get-tuple-element.29), channel_id=1, source_target_pairs={{0,1},{1,0},{2,3},{3,2},{4,5},{5,4},{6,7},{7,6},{8,9},{9,8},{10,11... | collective-permute-start | bytes 491528 | tf_op jit(solution)/shard_map/ppermute | solution.py:384

commit v8 on v7

--- a/solution.py
+++ b/solution.py
@@ -47,19 +47,16 @@
     return at_z ^ offset if swapped else offset
 
 
-def edges_kernel(x_ref, *refs, sends, swapped, count_z):
-    z_refs, (ya_ref, yb_ref, e_ref, top_ref, bottom_ref, sems) = refs[:-6], refs[-6:]
-    cells_z, rows, cols = x_ref.shape
-    at_x, at_y, at_z = place()
-    strip, piece = e_ref.shape[2], z_refs[0].shape[2]
-    even_z, even_y = at_z % 2 == 0, at_y % 2 == 0
-    high = cells_z - HALO
-    start = pl.multiple_of(jnp.where(at_x == 0, cols - strip, 0), strip)
+def depth_moves(x_ref, z_refs, sends, swapped, count_z):
+    piece = z_refs[0].shape[2]
+    at_z = place()[2]
+    even = at_z % 2 == 0
+    high = x_ref.shape[0] - HALO
     after = lax.rem(at_z + 1, count_z)
     before = lax.rem(at_z + count_z - 1, count_z)
     sides = (
-        (jnp.where(even_z, after, before), jnp.where(even_z, high, 0)),
-        (jnp.where(even_z, before, after), jnp.where(even_z, 0, high)),
+        (jnp.where(even, after, before), jnp.where(even, high, 0)),
+        (jnp.where(even, before, after), jnp.where(even, 0, high)),
     )
     moves = []
     for z_ref, (side, offsets) in zip(z_refs, sends):
@@ -67,19 +64,39 @@
         for slot, offset in enumerate(offsets):
             row = pl.multiple_of(block_of(offset, swapped, peer) * piece, 8)
             moves.append((x_ref.at[pl.ds(layer, HALO), pl.ds(row, piece)], z_ref.at[slot]))
+    return moves
+
+
+def copy_all(moves, sems):
+    copies = [pltpu.make_async_copy(*move, sems.at[i]) for i, move in enumerate(moves)]
+    for copy in copies:
+        copy.start()
+    for copy in copies:
+        copy.wait()
+
+
+def edges_kernel(x_ref, *refs, sends, swapped, count_z):
+    z_refs, (ya_ref, yb_ref, e_ref, top_ref, bottom_ref, sems) = refs[:-6], refs[-6:]
+    _, rows, cols = x_ref.shape
+    at_x, at_y, _ = place()
+    strip = e_ref.shape[2]
+    even = at_y % 2 == 0
+    start = pl.multiple_of(jnp.where(at_x == 0, cols - strip, 0), strip)
+    moves = depth_moves(x_ref, z_refs, sends, swapped, count_z)
     moves += [
         (x_ref.at[:, pl.ds(0, RIM)], top_ref),
         (x_ref.at[:, pl.ds(rows - RIM, RIM)], bottom_ref),
         (x_ref.at[:, :, pl.ds(start, strip)], e_ref),
     ]
-    copies = [pltpu.make_async_copy(*move, sems.at[i]) for i, move in enumerate(moves)]
-    for copy in copies:
-        copy.start()
-    for copy in copies:
-        copy.wait()
+    copy_all(moves, sems)
     top, bottom = top_ref[:, :HALO, :], bottom_ref[:, RIM - HALO :, :]
-    ya_ref[...] = jnp.where(even_y, bottom, top)
-    yb_ref[...] = jnp.where(even_y, top, bottom)
+    ya_ref[...] = jnp.where(even, bottom, top)
+    yb_ref[...] = jnp.where(even, top, bottom)
+
+
+def late_edges_kernel(x_ref, *refs, sends, swapped, count_z):
+    z_refs = refs[-1 - len(sends) : -1]
+    copy_all(depth_moves(x_ref, z_refs, sends, swapped, count_z), refs[-1])
 
 
 def pair(grad_x, grad_y):
@@ -201,7 +218,7 @@
             image_ref[channel, to] = value
 
 
-def outer_kernel(x_ref, za_ref, zb_ref, image_ref, part_ref, *refs, total_z, offsets, swapped, base):
+def outer_kernel(x_ref, za_ref, zb_ref, image_ref, part_ref, *refs, total_z, offsets, swapped, base, zb_base):
     cells_z, _, cols = x_ref.shape
     depth_step = 2.0 / total_z
     at_z = place()[2]
@@ -217,10 +234,10 @@
         at = pl.ds(pl.multiple_of(block * piece + start, 8), chunk)
 
         def before(layer):
-            return jnp.where(at_z > 0, jnp.where(even, zb_ref[out, layer, part], za_ref[base + out, layer, part]), none)
+            return jnp.where(at_z > 0, jnp.where(even, zb_ref[zb_base + out, layer, part], za_ref[base + out, layer, part]), none)
 
         def after(layer):
-            return jnp.where(at_z < last_z, jnp.where(even, za_ref[base + out, layer, part], zb_ref[out, layer, part]), none)
+            return jnp.where(at_z < last_z, jnp.where(even, za_ref[base + out, layer, part], zb_ref[zb_base + out, layer, part]), none)
 
         f = [x_ref[k, at] for k in range(4)]
         b = [x_ref[cells_z - 4 + k, at] for k in range(4)]
@@ -258,7 +275,7 @@
     clear_ref[...] = image[4]
 
 
-def blend_four(own_ref, one_ref, two_ref, three_ref, colour_ref, depth_ref, clear_ref):
+def blend_four(own_ref, one_ref, three_ref, two_ref, colour_ref, depth_ref, clear_ref):
     at_z = place()[2]
     odd, high = at_z % 2 == 1, at_z >= 2
     own, one, two, three = (
@@ -315,22 +332,21 @@
     groups = ((2, 3), (1, 0)) if swapped else (tuple(range(count_z)),)
     every = sum(groups, ())
     sends = [(0, every)] + [(1, g) for g in groups]
+    early, late = sends[:2], sends[2:]
     payloads = [shaped(len(g), HALO, piece, cols) for _, g in sends]
     edges = pl.pallas_call(
-        functools.partial(edges_kernel, sends=sends, swapped=swapped, count_z=count_z),
-        out_shape=payloads
+        functools.partial(edges_kernel, sends=early, swapped=swapped, count_z=count_z),
+        out_shape=payloads[:2]
         + [shaped(cells_z, HALO, cols)] * 2
         + [shaped(cells_z, rows, strip)],
         in_specs=[pl.BlockSpec(memory_space=pltpu.HBM)],
-        out_specs=[vmem] * (len(payloads) + 3),
+        out_specs=[vmem] * 5,
         scratch_shapes=[pltpu.VMEM((cells_z, RIM, cols), f32)] * 2
-        + [pltpu.SemaphoreType.DMA((2 * len(every) + 3,))],
+        + [pltpu.SemaphoreType.DMA((sum(len(g) for _, g in early) + 3,))],
         compiler_params=limit(4),
         name="edges",
     )(pltpu.with_memory_space_constraint(block, pltpu.HBM))
-    whole, *cut = [
-        swap_pairs(value, "gz", side) for value, (side, _) in zip(edges, sends)
-    ]
+    halos = [swap_pairs(value, "gz", side) for value, (side, _) in zip(edges, early)]
     ya = swap_pairs(edges[-3], "gy", False)
     yb = swap_pairs(edges[-2], "gy", True)
     edge = lax.ppermute(edges[-1], "gx", [(0, 1), (1, 0)])
@@ -352,6 +368,18 @@
         ),
         name="inner",
     )(block, edge)
+    if late:
+        last = pl.pallas_call(
+            functools.partial(late_edges_kernel, sends=late, swapped=swapped, count_z=count_z),
+            out_shape=payloads[2:],
+            in_specs=[vmem] + [pl.BlockSpec(memory_space=pl.ANY)] * 3,
+            out_specs=[vmem] * len(late),
+            scratch_shapes=[pltpu.SemaphoreType.DMA((sum(len(g) for _, g in late),))],
+            compiler_params=limit(4),
+            name="late_edges",
+        )(block, rim, ya, yb)
+        halos += [swap_pairs(value, "gz", side) for value, (side, _) in zip(last, late)]
+    whole, *cut = halos
     image, part = pl.pallas_call(
         functools.partial(rim_kernel, total_z=total_z, last_y=count_y - 1),
         out_shape=(image_shape, part_shape),
@@ -366,16 +394,19 @@
     )(block, ya, yb, rim, image, part)
 
     received = {}
-    for offsets, own in zip(groups, cut):
-        za, zb = whole, own
+    for offsets in [(o,) for o in every] if swapped else groups:
+        base = every.index(offsets[0])
+        zb, zb_base = next((c, g.index(offsets[0])) for c, g in zip(cut, groups) if offsets[0] in g)
         made = pl.pallas_call(
-            functools.partial(outer_kernel, total_z=total_z, offsets=offsets, swapped=swapped, base=every.index(offsets[0])),
+            functools.partial(
+                outer_kernel, total_z=total_z, offsets=offsets, swapped=swapped, base=base, zb_base=zb_base
+            ),
             out_shape=[shaped(5, piece, cols)] * len(offsets),
             in_specs=[vmem] * 5,
             out_specs=[vmem] * len(offsets),
             compiler_params=limit(16),
             name="outer",
-        )(block, za, zb, image, part)
+        )(block, whole, zb, image, part)
         received.update(zip(offsets, made))
     out_shape = (shaped(3, piece, cols), shaped(piece, cols), shaped(piece, cols))
     if swapped:
@@ -389,7 +420,7 @@
             out_specs=(vmem, vmem, vmem),
             compiler_params=limit(8),
             name="blend",
-        )(*(received[offset] for offset in range(4)))
+        )(*(received[offset] for offset in (0, 1, 3, 2)))
     parts = jnp.stack([received[k] for k in range(count_z)])
     gathered = lax.all_to_all(parts, "gz", split_axis=0, concat_axis=0, tiled=True)
     return pl.pallas_call(

time: 27.4 us -> 27.1 us (0.989); the launches traced: 27.2 us -> 26.6 us
  waiting for transfers between devices: 5.67 us -> 4.63 us
  starting transfers between devices: 12.9 us -> 13.2 us
    ppermute x3, waiting for transfers between devices: 5.21 us -> 4.38 us  [on_device(): received[offset] = lax.ppermute(received[offset], 'gz', swap)]
    pallas_call x1 -> x2, Pallas kernels: 1.86 us -> 1.93 us  [the longest x1 1.8 us: on_device(): pl.pallas_call(functools.partial(edges_kernel, sends=early, swapped=swapp...]
    pallas_call x2 -> x4, Pallas kernels: 0.81 us -> 0.83 us  [on_device(): pl.pallas_call(functools.partial(outer_kernel, total_z=total_z, offsets=o...]
  transfers between devices with their start and end apart: 9 -> 9, of which waited for: 4 -> 3; matrix products, arithmetic and copies ran while one was open for 0% -> 0% of each run, Pallas kernels for 20% -> 21%
where the time goes in v8:
time: 27.1 us; the launch traced here: 26.6 us
  starting transfers between devices  13.2 us (49%)
  Pallas kernels  8.04 us (30%)
  waiting for transfers between devices  4.63 us (17%)
  between operations  0.73 us (3%)
    ppermute x3, starting transfers between devices, on_device(): received[offset] = lax.ppermute(received[offset], 'gz', swap)  7.97 us
    ppermute x3, waiting for transfers between devices, on_device(): received[offset] = lax.ppermute(received[offset], 'gz', swap)  4.38 us
    pallas_call x1, Pallas kernels, on_device(): pl.pallas_call(functools.partial(inner_kernel, total_z=total_z), out_shap...  4.15 us
    ppermute x2, starting transfers between devices, swap_pairs(): return lax.ppermute(value, axis, [(i, i ^ 1) for i in range(count)])  4.14 us
    pallas_call x1, Pallas kernels, on_device(): pl.pallas_call(functools.partial(edges_kernel, sends=early, swapped=swapp...  1.8 us
    pallas_call x4, Pallas kernels, on_device(): pl.pallas_call(functools.partial(outer_kernel, total_z=total_z, offsets=o...  0.83 us
    pallas_call x1, Pallas kernels, on_device(): pl.pallas_call(blend_four, out_shape=out_shape, in_specs=[vmem] * 4, out_...  0.72 us
    ppermute x3, starting transfers between devices, swap_pairs(): return lax.ppermute(value, ('gx', axis), pairs)  0.58 us
  transfers between devices with their start and end apart: 9, of which 3 were waited for; matrix products, arithmetic and copies ran while one was open for 0% of the time, Pallas kernels for 21%

profile of v8, /device:TPU:0, one launch (start us, length us, event | category | flops | bytes accessed | tf_op | source)
XLA Modules:
  0.0 26.6 jit_solution(17453600836602398453)
XLA Ops:
  0.6 1.8 %edges.1 = (f32[4,2,32,256]{3,2,1,0:T(8,128)S(1)}, f32[2,2,32,256]{3,2,1,0:T(8,128)S(1)}, f32[16,2,256]{2,1,0:T(2,128)S(1)}, f32[16,2,256]{2,1,0:T(2,128)S(1)}, f32[16,128,128]{2,1,0:T(8,128)S(1)}) custom-call(f32[16,128,256]{2,1,0:T(8,128)} %x_ref.15), custom_call_target="tpu_custom_call" | custom-call | tf_op jit(solution)/shard_map/edges/pallas_call | solution.py:337
  2.4 0.5 %collective-permute-start.1 = (f32[16,128,128]{2,1,0:T(8,128)S(1)}, f32[16,128,128]{2,1,0:T(8,128)S(1)}, u32[]{:S(2)}, u32[]{:S(2)}) collective-permute-start(f32[16,128,128]{2,1,0:T(8,128)S(1)} %get-tuple-element.14), channel_id=1, source_target_pairs={{0,16},{16,0},{1,17},{17,1},{2,18},{18,2},{3,19},{19,3},{4,20},{20... | collective-permute-start | bytes 3145736 | tf_op jit(solution)/shard_map/ppermute | solution.py:352
  3.0 2.6 %collective-permute-start = (f32[4,2,32,256]{3,2,1,0:T(8,128)S(1)}, f32[4,2,32,256]{3,2,1,0:T(8,128)S(1)}, u32[]{:S(2)}, u32[]{:S(2)}) collective-permute-start(f32[4,2,32,256]{3,2,1,0:T(8,128)S(1)} %get-tuple-element.13), channel_id=1, source_target_pairs={{0,1},{1,0},{2,3},{3,2},{4,5},{5,4},{6,7},{7,6},{8,9},{9,8},{10,11... | collective-permute-start | bytes 786440 | tf_op jit(solution)/shard_map/ppermute | solution.py:305
  5.5 1.6 %collective-permute-start.2 = (f32[16,2,256]{2,1,0:T(2,128)S(1)}, f32[16,2,256]{2,1,0:T(2,128)S(1)}, u32[]{:S(2)}, u32[]{:S(2)}) collective-permute-start(f32[16,2,256]{2,1,0:T(2,128)S(1)} %get-tuple-element.16), channel_id=1, source_target_pairs={{0,4},{4,0},{8,12},{12,8},{1,5},{5,1},{9,13},{13,9},{2,6},{6,2},{1... | collective-permute-start | bytes 98312 | tf_op jit(solution)/shard_map/ppermute | solution.py:305
  7.1 0.5 %collective-permute-start.6 = (f32[2,2,32,256]{3,2,1,0:T(8,128)S(1)}, f32[2,2,32,256]{3,2,1,0:T(8,128)S(1)}, u32[]{:S(2)}, u32[]{:S(2)}) collective-permute-start(f32[2,2,32,256]{3,2,1,0:T(8,128)S(1)} %get-tuple-element.22), channel_id=1, source_target_pairs={{0,16},{1,2},{2,1},{3,19},{16,0},{17,18},{18,17},{19,3},{4,20},{5,... | collective-permute-start | bytes 393224 | tf_op jit(solution)/shard_map/ppermute | solution.py:313
  7.6 0.0 collective-permute-done.1.e_ref
  7.6 4.1 %inner.1 = (f32[5,128,256]{2,1,0:T(8,128)S(1)}, f32[4,2,128,256]{3,2,1,0:T(8,128)S(1)}, f32[16,2,16,256]{3,2,1,0:T(8,128)S(1)}) custom-call(f32[16,128,256]{2,1,0:T(8,128)S(1)} %copy-done, f32[16,128,128]{2,1,0:T(8,128)S(1)} %collective-permute-done.1.e_ref), custom_call_target="tpu_custom_call" | custom-call | flops 52428800 | bytes 4194304 | tf_op jit(solution)/shard_map/inner/pallas_call | solution.py:355
  11.8 0.0 collective-permute-done.2.refs_1_.ya_ref
  11.8 0.0 collective-permute-done.3.refs_2_.yb_ref
  11.8 0.1 late_edges.1
  11.9 0.1 collective-permute-start.4
  12.0 0.4 %rim.1 = (f32[5,128,256]{2,1,0:T(8,128)S(1)}, f32[4,2,128,256]{3,2,1,0:T(8,128)S(1)}) custom-call(f32[16,128,256]{2,1,0:T(8,128)S(1)} %copy-done, f32[16,2,256]{2,1,0:T(2,128)S(1)} %collective-permute-done.2.refs_1_.ya_ref, f32[16,2,256]{2,1,0:T(2,128)S(1)} %collective-permute-done.3.refs_2_.yb_ref, ...), custom_call_target="tpu_custom_call", output_to_operand_aliasing={{0}: (4, {}), {1}: (5, {})} | custom-call | flops 6291456 | bytes 524288 | tf_op jit(solution)/shard_map/rim/pallas_call | solution.py:383
  12.5 0.2 collective-permute-done.za_ref
  12.7 0.2 outer.6
  12.9 3.0 %collective-permute-start.7 = (f32[5,32,256]{2,1,0:T(8,128)S(1)}, f32[5,32,256]{2,1,0:T(8,128)S(1)}, u32[]{:S(2)}, u32[]{:S(2)}) collective-permute-start(f32[5,32,256]{2,1,0:T(8,128)S(1)} %outer.6), channel_id=1, source_target_pairs={{0,3},{1,2},{2,1},{3,0},{4,7},{5,6},{6,5},{7,4},{8,11},{9,10},{10,... | collective-permute-start | bytes 491528 | tf_op jit(solution)/shard_map/ppermute | solution.py:415
  15.9 0.2 outer.7
  16.1 3.9 %collective-permute-start.8 = (f32[5,32,256]{2,1,0:T(8,128)S(1)}, f32[5,32,256]{2,1,0:T(8,128)S(1)}, u32[]{:S(2)}, u32[]{:S(2)}) collective-permute-start(f32[5,32,256]{2,1,0:T(8,128)S(1)} %outer.7), channel_id=1, source_target_pairs={{0,2},{1,3},{2,0},{3,1},{4,6},{5,7},{6,4},{7,5},{8,10},{9,11},{10,... | collective-permute-start | bytes 491528 | tf_op jit(solution)/shard_map/ppermute | solution.py:415
  20.0 0.0 collective-permute-done.4.zb_ref
  20.0 0.2 outer.5
  20.2 1.1 %collective-permute-start.5 = (f32[5,32,256]{2,1,0:T(8,128)S(1)}, f32[5,32,256]{2,1,0:T(8,128)S(1)}, u32[]{:S(2)}, u32[]{:S(2)}) collective-permute-start(f32[5,32,256]{2,1,0:T(8,128)S(1)} %outer.5), channel_id=1, source_target_pairs={{0,1},{1,0},{2,3},{3,2},{4,5},{5,4},{6,7},{7,6},{8,9},{9,8},{10,11... | collective-permute-start | bytes 491528 | tf_op jit(solution)/shard_map/ppermute | solution.py:415
  21.3 0.2 outer.4.own_ref
  21.5 3.4 %collective-permute-done.8.two_ref = f32[5,32,256]{2,1,0:T(8,128)S(1)} collective-permute-done((f32[5,32,256]{2,1,0:T(8,128)S(1)}, f32[5,32,256]{2,1,0:T(8,128)S(1)}, u32[]{:S(2)}, u32[]{:S(2)}) %collective-permute-start.8) | collective-permute-done | bytes 163872 | tf_op jit(solution)/shard_map/ppermute | solution.py:415
  24.9 1.0 %collective-permute-done.5.one_ref = f32[5,32,256]{2,1,0:T(8,128)S(1)} collective-permute-done((f32[5,32,256]{2,1,0:T(8,128)S(1)}, f32[5,32,256]{2,1,0:T(8,128)S(1)}, u32[]{:S(2)}, u32[]{:S(2)}) %collective-permute-start.5) | collective-permute-done | bytes 163872 | tf_op jit(solution)/shard_map/ppermute | solution.py:415
  25.9 0.7 %blend.1 = (f32[3,32,256]{2,1,0:T(8,128)}, f32[32,256]{1,0:T(8,128)}, f32[32,256]{1,0:T(8,128)}) custom-call(f32[5,32,256]{2,1,0:T(8,128)S(1)} %outer.4.own_ref, f32[5,32,256]{2,1,0:T(8,128)S(1)} %collective-permute-done.5.one_ref, f32[5,32,256]{2,1,0:T(8,128)S(1)} %collective-permute-done.7.three_ref, f32[5,32,256]{2,1,0:T(8,128)S(1)} %collective-permute-done.8.two_ref), custom_call_target="tpu_custom_call" | custom-call | tf_op jit(solution)/shard_map/blend/pallas_call | solution.py:416
  (5 shorter events, 0.0 us)
Async XLA Ops:
  0.6 7.0 %copy-start = (f32[16,128,256]{2,1,0:T(8,128)S(1)}, f32[16,128,256]{2,1,0:T(8,128)}, u32[]{:S(2)}) copy-start(f32[16,128,256]{2,1,0:T(8,128)} %x_ref.15) | copy-start | bytes 6291460
  2.4 5.2 %collective-permute-start.1 = (f32[16,128,128]{2,1,0:T(8,128)S(1)}, f32[16,128,128]{2,1,0:T(8,128)S(1)}, u32[]{:S(2)}, u32[]{:S(2)}) collective-permute-start(f32[16,128,128]{2,1,0:T(8,128)S(1)} %get-tuple-element.14), channel_id=1, source_target_pairs={{0,16},{16,0},{1,17},{17,1},{2,18},{18,2},{3,19},{19,3},{4,20},{20... | collective-permute-start | bytes 3145736 | tf_op jit(solution)/shard_map/ppermute | solution.py:352
  3.0 9.7 %collective-permute-start = (f32[4,2,32,256]{3,2,1,0:T(8,128)S(1)}, f32[4,2,32,256]{3,2,1,0:T(8,128)S(1)}, u32[]{:S(2)}, u32[]{:S(2)}) collective-permute-start(f32[4,2,32,256]{3,2,1,0:T(8,128)S(1)} %get-tuple-element.13), channel_id=1, source_target_pairs={{0,1},{1,0},{2,3},{3,2},{4,5},{5,4},{6,7},{7,6},{8,9},{9,8},{10,11... | collective-permute-start | bytes 786440 | tf_op jit(solution)/shard_map/ppermute | solution.py:305
  5.5 6.3 %collective-permute-start.2 = (f32[16,2,256]{2,1,0:T(2,128)S(1)}, f32[16,2,256]{2,1,0:T(2,128)S(1)}, u32[]{:S(2)}, u32[]{:S(2)}) collective-permute-start(f32[16,2,256]{2,1,0:T(2,128)S(1)} %get-tuple-element.16), channel_id=1, source_target_pairs={{0,4},{4,0},{8,12},{12,8},{1,5},{5,1},{9,13},{13,9},{2,6},{6,2},{1... | collective-permute-start | bytes 98312 | tf_op jit(solution)/shard_map/ppermute | solution.py:305
  7.1 4.7 %collective-permute-start.3 = (f32[16,2,256]{2,1,0:T(2,128)S(1)}, f32[16,2,256]{2,1,0:T(2,128)S(1)}, u32[]{:S(2)}, u32[]{:S(2)}) collective-permute-start(f32[16,2,256]{2,1,0:T(2,128)S(1)} %get-tuple-element.17), channel_id=1, source_target_pairs={{0,16},{4,8},{8,4},{12,28},{16,0},{20,24},{24,20},{28,12},{1,17},{... | collective-permute-start | bytes 98312 | tf_op jit(solution)/shard_map/ppermute | solution.py:313
  7.1 5.3 %collective-permute-start.6 = (f32[2,2,32,256]{3,2,1,0:T(8,128)S(1)}, f32[2,2,32,256]{3,2,1,0:T(8,128)S(1)}, u32[]{:S(2)}, u32[]{:S(2)}) collective-permute-start(f32[2,2,32,256]{3,2,1,0:T(8,128)S(1)} %get-tuple-element.22), channel_id=1, source_target_pairs={{0,16},{1,2},{2,1},{3,19},{16,0},{17,18},{18,17},{19,3},{4,20},{5,... | collective-permute-start | bytes 393224 | tf_op jit(solution)/shard_map/ppermute | solution.py:313
  11.9 8.0 %collective-permute-start.4 = (f32[2,2,32,256]{3,2,1,0:T(8,128)S(1)}, f32[2,2,32,256]{3,2,1,0:T(8,128)S(1)}, u32[]{:S(2)}, u32[]{:S(2)}) collective-permute-start(f32[2,2,32,256]{3,2,1,0:T(8,128)S(1)} %late_edges.1), channel_id=1, source_target_pairs={{0,16},{1,2},{2,1},{3,19},{16,0},{17,18},{18,17},{19,3},{4,20},{5,... | collective-permute-start | bytes 393224 | tf_op jit(solution)/shard_map/ppermute | solution.py:313
  12.9 8.6 %collective-permute-start.7 = (f32[5,32,256]{2,1,0:T(8,128)S(1)}, f32[5,32,256]{2,1,0:T(8,128)S(1)}, u32[]{:S(2)}, u32[]{:S(2)}) collective-permute-start(f32[5,32,256]{2,1,0:T(8,128)S(1)} %outer.6), channel_id=1, source_target_pairs={{0,3},{1,2},{2,1},{3,0},{4,7},{5,6},{6,5},{7,4},{8,11},{9,10},{10,... | collective-permute-start | bytes 491528 | tf_op jit(solution)/shard_map/ppermute | solution.py:415
  16.1 8.8 %collective-permute-start.8 = (f32[5,32,256]{2,1,0:T(8,128)S(1)}, f32[5,32,256]{2,1,0:T(8,128)S(1)}, u32[]{:S(2)}, u32[]{:S(2)}) collective-permute-start(f32[5,32,256]{2,1,0:T(8,128)S(1)} %outer.7), channel_id=1, source_target_pairs={{0,2},{1,3},{2,0},{3,1},{4,6},{5,7},{6,4},{7,5},{8,10},{9,11},{10,... | collective-permute-start | bytes 491528 | tf_op jit(solution)/shard_map/ppermute | solution.py:415
  20.2 5.7 %collective-permute-start.5 = (f32[5,32,256]{2,1,0:T(8,128)S(1)}, f32[5,32,256]{2,1,0:T(8,128)S(1)}, u32[]{:S(2)}, u32[]{:S(2)}) collective-permute-start(f32[5,32,256]{2,1,0:T(8,128)S(1)} %outer.5), channel_id=1, source_target_pairs={{0,1},{1,0},{2,3},{3,2},{4,5},{5,4},{6,7},{7,6},{8,9},{9,8},{10,11... | collective-permute-start | bytes 491528 | tf_op jit(solution)/shard_map/ppermute | solution.py:415

commit v9 on v8

--- a/solution.py
+++ b/solution.py
@@ -120,7 +120,7 @@
     wx_ref[...] = jnp.concatenate([along_x, along_x, beyond_x, beyond_x], axis=0)
     wy_ref[...] = jnp.concatenate([along_y, along_y], axis=1)
 
-    chunk = 16
+    chunk = 8
     spans = [pl.ds(r, chunk) for r in range(RIM, rows - RIM, chunk)]
     slots = ((gx0, gy0), (gx1, gy1))
 

time: 27.1 us -> 27.1 us (level)
  no operation moved by 1% of the time
where the time goes in v9:
time: 27.1 us; the launch traced here: 26.6 us
  starting transfers between devices  13.2 us (49%)
  Pallas kernels  8.04 us (30%)
  waiting for transfers between devices  4.63 us (17%)
  between operations  0.73 us (3%)
    ppermute x3, starting transfers between devices, on_device(): received[offset] = lax.ppermute(received[offset], 'gz', swap)  7.97 us
    ppermute x3, waiting for transfers between devices, on_device(): received[offset] = lax.ppermute(received[offset], 'gz', swap)  4.38 us
    pallas_call x1, Pallas kernels, on_device(): pl.pallas_call(functools.partial(inner_kernel, total_z=total_z), out_shap...  4.15 us
    ppermute x2, starting transfers between devices, swap_pairs(): return lax.ppermute(value, axis, [(i, i ^ 1) for i in range(count)])  4.14 us
    pallas_call x1, Pallas kernels, on_device(): pl.pallas_call(functools.partial(edges_kernel, sends=early, swapped=swapp...  1.8 us
    pallas_call x4, Pallas kernels, on_device(): pl.pallas_call(functools.partial(outer_kernel, total_z=total_z, offsets=o...  0.83 us
    pallas_call x1, Pallas kernels, on_device(): pl.pallas_call(blend_four, out_shape=out_shape, in_specs=[vmem] * 4, out_...  0.72 us
    ppermute x3, starting transfers between devices, swap_pairs(): return lax.ppermute(value, ('gx', axis), pairs)  0.58 us
  transfers between devices with their start and end apart: 9, of which 3 were waited for; matrix products, arithmetic and copies ran while one was open for 0% of the time, Pallas kernels for 21%

profile of v9, /device:TPU:0, one launch (start us, length us, event | category | flops | bytes accessed | tf_op | source)
XLA Modules:
  0.0 26.6 jit_solution(4193996957482686751)
XLA Ops:
  0.6 1.8 %edges.1 = (f32[4,2,32,256]{3,2,1,0:T(8,128)S(1)}, f32[2,2,32,256]{3,2,1,0:T(8,128)S(1)}, f32[16,2,256]{2,1,0:T(2,128)S(1)}, f32[16,2,256]{2,1,0:T(2,128)S(1)}, f32[16,128,128]{2,1,0:T(8,128)S(1)}) custom-call(f32[16,128,256]{2,1,0:T(8,128)} %x_ref.15), custom_call_target="tpu_custom_call" | custom-call | tf_op jit(solution)/shard_map/edges/pallas_call | solution.py:337
  2.4 0.5 %collective-permute-start.1 = (f32[16,128,128]{2,1,0:T(8,128)S(1)}, f32[16,128,128]{2,1,0:T(8,128)S(1)}, u32[]{:S(2)}, u32[]{:S(2)}) collective-permute-start(f32[16,128,128]{2,1,0:T(8,128)S(1)} %get-tuple-element.14), channel_id=1, source_target_pairs={{0,16},{16,0},{1,17},{17,1},{2,18},{18,2},{3,19},{19,3},{4,20},{20... | collective-permute-start | bytes 3145736 | tf_op jit(solution)/shard_map/ppermute | solution.py:352
  3.0 2.6 %collective-permute-start = (f32[4,2,32,256]{3,2,1,0:T(8,128)S(1)}, f32[4,2,32,256]{3,2,1,0:T(8,128)S(1)}, u32[]{:S(2)}, u32[]{:S(2)}) collective-permute-start(f32[4,2,32,256]{3,2,1,0:T(8,128)S(1)} %get-tuple-element.13), channel_id=1, source_target_pairs={{0,1},{1,0},{2,3},{3,2},{4,5},{5,4},{6,7},{7,6},{8,9},{9,8},{10,11... | collective-permute-start | bytes 786440 | tf_op jit(solution)/shard_map/ppermute | solution.py:305
  5.5 1.6 %collective-permute-start.2 = (f32[16,2,256]{2,1,0:T(2,128)S(1)}, f32[16,2,256]{2,1,0:T(2,128)S(1)}, u32[]{:S(2)}, u32[]{:S(2)}) collective-permute-start(f32[16,2,256]{2,1,0:T(2,128)S(1)} %get-tuple-element.16), channel_id=1, source_target_pairs={{0,4},{4,0},{8,12},{12,8},{1,5},{5,1},{9,13},{13,9},{2,6},{6,2},{1... | collective-permute-start | bytes 98312 | tf_op jit(solution)/shard_map/ppermute | solution.py:305
  7.1 0.5 %collective-permute-start.6 = (f32[2,2,32,256]{3,2,1,0:T(8,128)S(1)}, f32[2,2,32,256]{3,2,1,0:T(8,128)S(1)}, u32[]{:S(2)}, u32[]{:S(2)}) collective-permute-start(f32[2,2,32,256]{3,2,1,0:T(8,128)S(1)} %get-tuple-element.22), channel_id=1, source_target_pairs={{0,16},{1,2},{2,1},{3,19},{16,0},{17,18},{18,17},{19,3},{4,20},{5,... | collective-permute-start | bytes 393224 | tf_op jit(solution)/shard_map/ppermute | solution.py:313
  7.6 0.0 collective-permute-done.1.e_ref
  7.6 4.1 %inner.1 = (f32[5,128,256]{2,1,0:T(8,128)S(1)}, f32[4,2,128,256]{3,2,1,0:T(8,128)S(1)}, f32[16,2,16,256]{3,2,1,0:T(8,128)S(1)}) custom-call(f32[16,128,256]{2,1,0:T(8,128)S(1)} %copy-done, f32[16,128,128]{2,1,0:T(8,128)S(1)} %collective-permute-done.1.e_ref), custom_call_target="tpu_custom_call" | custom-call | flops 52428800 | bytes 4194304 | tf_op jit(solution)/shard_map/inner/pallas_call | solution.py:355
  11.8 0.0 collective-permute-done.3.refs_2_.yb_ref
  11.8 0.1 late_edges.1
  11.9 0.1 collective-permute-start.4
  12.0 0.4 %rim.1 = (f32[5,128,256]{2,1,0:T(8,128)S(1)}, f32[4,2,128,256]{3,2,1,0:T(8,128)S(1)}) custom-call(f32[16,128,256]{2,1,0:T(8,128)S(1)} %copy-done, f32[16,2,256]{2,1,0:T(2,128)S(1)} %collective-permute-done.2.refs_1_.ya_ref, f32[16,2,256]{2,1,0:T(2,128)S(1)} %collective-permute-done.3.refs_2_.yb_ref, ...), custom_call_target="tpu_custom_call", output_to_operand_aliasing={{0}: (4, {}), {1}: (5, {})} | custom-call | flops 6291456 | bytes 524288 | tf_op jit(solution)/shard_map/rim/pallas_call | solution.py:383
  12.4 0.0 collective-permute-done.6.zb_ref
  12.5 0.2 collective-permute-done.za_ref
  12.7 0.2 outer.6
  12.9 3.0 %collective-permute-start.7 = (f32[5,32,256]{2,1,0:T(8,128)S(1)}, f32[5,32,256]{2,1,0:T(8,128)S(1)}, u32[]{:S(2)}, u32[]{:S(2)}) collective-permute-start(f32[5,32,256]{2,1,0:T(8,128)S(1)} %outer.6), channel_id=1, source_target_pairs={{0,3},{1,2},{2,1},{3,0},{4,7},{5,6},{6,5},{7,4},{8,11},{9,10},{10,... | collective-permute-start | bytes 491528 | tf_op jit(solution)/shard_map/ppermute | solution.py:415
  15.9 0.2 outer.7
  16.1 3.9 %collective-permute-start.8 = (f32[5,32,256]{2,1,0:T(8,128)S(1)}, f32[5,32,256]{2,1,0:T(8,128)S(1)}, u32[]{:S(2)}, u32[]{:S(2)}) collective-permute-start(f32[5,32,256]{2,1,0:T(8,128)S(1)} %outer.7), channel_id=1, source_target_pairs={{0,2},{1,3},{2,0},{3,1},{4,6},{5,7},{6,4},{7,5},{8,10},{9,11},{10,... | collective-permute-start | bytes 491528 | tf_op jit(solution)/shard_map/ppermute | solution.py:415
  20.0 0.0 collective-permute-done.4.zb_ref
  20.0 0.2 outer.5
  20.2 1.1 %collective-permute-start.5 = (f32[5,32,256]{2,1,0:T(8,128)S(1)}, f32[5,32,256]{2,1,0:T(8,128)S(1)}, u32[]{:S(2)}, u32[]{:S(2)}) collective-permute-start(f32[5,32,256]{2,1,0:T(8,128)S(1)} %outer.5), channel_id=1, source_target_pairs={{0,1},{1,0},{2,3},{3,2},{4,5},{5,4},{6,7},{7,6},{8,9},{9,8},{10,11... | collective-permute-start | bytes 491528 | tf_op jit(solution)/shard_map/ppermute | solution.py:415
  21.3 0.2 outer.4.own_ref
  21.5 3.4 %collective-permute-done.8.two_ref = f32[5,32,256]{2,1,0:T(8,128)S(1)} collective-permute-done((f32[5,32,256]{2,1,0:T(8,128)S(1)}, f32[5,32,256]{2,1,0:T(8,128)S(1)}, u32[]{:S(2)}, u32[]{:S(2)}) %collective-permute-start.8) | collective-permute-done | bytes 163872 | tf_op jit(solution)/shard_map/ppermute | solution.py:415
  24.9 1.0 %collective-permute-done.5.one_ref = f32[5,32,256]{2,1,0:T(8,128)S(1)} collective-permute-done((f32[5,32,256]{2,1,0:T(8,128)S(1)}, f32[5,32,256]{2,1,0:T(8,128)S(1)}, u32[]{:S(2)}, u32[]{:S(2)}) %collective-permute-start.5) | collective-permute-done | bytes 163872 | tf_op jit(solution)/shard_map/ppermute | solution.py:415
  25.9 0.7 %blend.1 = (f32[3,32,256]{2,1,0:T(8,128)}, f32[32,256]{1,0:T(8,128)}, f32[32,256]{1,0:T(8,128)}) custom-call(f32[5,32,256]{2,1,0:T(8,128)S(1)} %outer.4.own_ref, f32[5,32,256]{2,1,0:T(8,128)S(1)} %collective-permute-done.5.one_ref, f32[5,32,256]{2,1,0:T(8,128)S(1)} %collective-permute-done.7.three_ref, f32[5,32,256]{2,1,0:T(8,128)S(1)} %collective-permute-done.8.two_ref), custom_call_target="tpu_custom_call" | custom-call | tf_op jit(solution)/shard_map/blend/pallas_call | solution.py:416
  (5 shorter events, 0.0 us)
Async XLA Ops:
  0.6 7.0 %copy-start = (f32[16,128,256]{2,1,0:T(8,128)S(1)}, f32[16,128,256]{2,1,0:T(8,128)}, u32[]{:S(2)}) copy-start(f32[16,128,256]{2,1,0:T(8,128)} %x_ref.15) | copy-start | bytes 6291460
  2.4 5.2 %collective-permute-start.1 = (f32[16,128,128]{2,1,0:T(8,128)S(1)}, f32[16,128,128]{2,1,0:T(8,128)S(1)}, u32[]{:S(2)}, u32[]{:S(2)}) collective-permute-start(f32[16,128,128]{2,1,0:T(8,128)S(1)} %get-tuple-element.14), channel_id=1, source_target_pairs={{0,16},{16,0},{1,17},{17,1},{2,18},{18,2},{3,19},{19,3},{4,20},{20... | collective-permute-start | bytes 3145736 | tf_op jit(solution)/shard_map/ppermute | solution.py:352
  3.0 9.7 %collective-permute-start = (f32[4,2,32,256]{3,2,1,0:T(8,128)S(1)}, f32[4,2,32,256]{3,2,1,0:T(8,128)S(1)}, u32[]{:S(2)}, u32[]{:S(2)}) collective-permute-start(f32[4,2,32,256]{3,2,1,0:T(8,128)S(1)} %get-tuple-element.13), channel_id=1, source_target_pairs={{0,1},{1,0},{2,3},{3,2},{4,5},{5,4},{6,7},{7,6},{8,9},{9,8},{10,11... | collective-permute-start | bytes 786440 | tf_op jit(solution)/shard_map/ppermute | solution.py:305
  5.5 6.3 %collective-permute-start.2 = (f32[16,2,256]{2,1,0:T(2,128)S(1)}, f32[16,2,256]{2,1,0:T(2,128)S(1)}, u32[]{:S(2)}, u32[]{:S(2)}) collective-permute-start(f32[16,2,256]{2,1,0:T(2,128)S(1)} %get-tuple-element.16), channel_id=1, source_target_pairs={{0,4},{4,0},{8,12},{12,8},{1,5},{5,1},{9,13},{13,9},{2,6},{6,2},{1... | collective-permute-start | bytes 98312 | tf_op jit(solution)/shard_map/ppermute | solution.py:305
  7.1 4.7 %collective-permute-start.3 = (f32[16,2,256]{2,1,0:T(2,128)S(1)}, f32[16,2,256]{2,1,0:T(2,128)S(1)}, u32[]{:S(2)}, u32[]{:S(2)}) collective-permute-start(f32[16,2,256]{2,1,0:T(2,128)S(1)} %get-tuple-element.17), channel_id=1, source_target_pairs={{0,16},{4,8},{8,4},{12,28},{16,0},{20,24},{24,20},{28,12},{1,17},{... | collective-permute-start | bytes 98312 | tf_op jit(solution)/shard_map/ppermute | solution.py:313
  7.1 5.3 %collective-permute-start.6 = (f32[2,2,32,256]{3,2,1,0:T(8,128)S(1)}, f32[2,2,32,256]{3,2,1,0:T(8,128)S(1)}, u32[]{:S(2)}, u32[]{:S(2)}) collective-permute-start(f32[2,2,32,256]{3,2,1,0:T(8,128)S(1)} %get-tuple-element.22), channel_id=1, source_target_pairs={{0,16},{1,2},{2,1},{3,19},{16,0},{17,18},{18,17},{19,3},{4,20},{5,... | collective-permute-start | bytes 393224 | tf_op jit(solution)/shard_map/ppermute | solution.py:313
  11.9 8.0 %collective-permute-start.4 = (f32[2,2,32,256]{3,2,1,0:T(8,128)S(1)}, f32[2,2,32,256]{3,2,1,0:T(8,128)S(1)}, u32[]{:S(2)}, u32[]{:S(2)}) collective-permute-start(f32[2,2,32,256]{3,2,1,0:T(8,128)S(1)} %late_edges.1), channel_id=1, source_target_pairs={{0,16},{1,2},{2,1},{3,19},{16,0},{17,18},{18,17},{19,3},{4,20},{5,... | collective-permute-start | bytes 393224 | tf_op jit(solution)/shard_map/ppermute | solution.py:313
  12.9 8.6 %collective-permute-start.7 = (f32[5,32,256]{2,1,0:T(8,128)S(1)}, f32[5,32,256]{2,1,0:T(8,128)S(1)}, u32[]{:S(2)}, u32[]{:S(2)}) collective-permute-start(f32[5,32,256]{2,1,0:T(8,128)S(1)} %outer.6), channel_id=1, source_target_pairs={{0,3},{1,2},{2,1},{3,0},{4,7},{5,6},{6,5},{7,4},{8,11},{9,10},{10,... | collective-permute-start | bytes 491528 | tf_op jit(solution)/shard_map/ppermute | solution.py:415
  16.1 8.8 %collective-permute-start.8 = (f32[5,32,256]{2,1,0:T(8,128)S(1)}, f32[5,32,256]{2,1,0:T(8,128)S(1)}, u32[]{:S(2)}, u32[]{:S(2)}) collective-permute-start(f32[5,32,256]{2,1,0:T(8,128)S(1)} %outer.7), channel_id=1, source_target_pairs={{0,2},{1,3},{2,0},{3,1},{4,6},{5,7},{6,4},{7,5},{8,10},{9,11},{10,... | collective-permute-start | bytes 491528 | tf_op jit(solution)/shard_map/ppermute | solution.py:415
  20.2 5.7 %collective-permute-start.5 = (f32[5,32,256]{2,1,0:T(8,128)S(1)}, f32[5,32,256]{2,1,0:T(8,128)S(1)}, u32[]{:S(2)}, u32[]{:S(2)}) collective-permute-start(f32[5,32,256]{2,1,0:T(8,128)S(1)} %outer.5), channel_id=1, source_target_pairs={{0,1},{1,0},{2,3},{3,2},{4,5},{5,4},{6,7},{7,6},{8,9},{9,8},{10,11... | collective-permute-start | bytes 491528 | tf_op jit(solution)/shard_map/ppermute | solution.py:415
